TPU v7x, 32 devices: a whole 2x2x4 slice. The times are simulated.
32 devices in a mesh: grp: 2 (over y), occ: 4 (over z), aux: 2 (over x), vir: 2 (over core).
Axes of the slice: x: 2, y: 2, z: 4, core: 2. Of those that a mesh axis runs over, the one named last changes fastest.
Arguments:
- integrals: bfloat16 [4, 1024, 8, 1280], P('occ', 'aux', 'grp', 'vir'), parts along dimension 2, may hold values from -0.59765625 to 0.59765625
- occ_energy: float32 [8], P('grp'), parts along dimension 0, may hold values from -1.5 to -0.3
- vir_energy: float32 [2560], P('grp'), parts along dimension 0, may hold values from 0.2 to 3
- round_owner: int32 [4], P('grp'), parts along dimension 0, may hold values from 0 to 3, as said below
Outputs:
- gamma_field: float32 [8, 1024, 4, 1280], P('grp', 'aux', 'occ', 'vir'), parts along dimension 0
There are 2 independent parts, one for each index of `grp`. A program takes and returns all parts, laid end to end along the dimension named above; each array names one. Nothing has to cross between parts.
Inputs may be any that keep to these rules, and one draw needn't show every extreme that they name: `round_owner`: the 2 owners are distinct.
All inputs are finite; a program needn't handle non-finite values.
Results may differ from a plain program's by a relative error of at most 0.0085.
Values may be sent and summed in bfloat16 or wider, within the bound.
No kernel may reach another device: no remote copies, remote signals or barrier semaphores. Data moves between devices by JAX's collectives and lax.ppermute only.
A program may use at most 64 MiB of HBM per device.

v0:
```python
import jax
import jax.numpy as jnp
from jax import lax
from jax.sharding import PartitionSpec as P

ROUNDS = 2


def from_root(value, axis, root):
    mine = lax.axis_index(axis) == root
    return lax.psum(jnp.where(mine, value, jnp.zeros_like(value)), axis)


def local(integrals, occ_energy, vir_energy, round_owner):
    regrouped = lax.all_to_all(integrals, "occ", split_axis=2, concat_axis=0, tiled=True)
    occ_width = regrouped.shape[2]
    vir_width = regrouped.shape[3]
    energy_i = lax.dynamic_slice_in_dim(occ_energy, lax.axis_index("occ") * occ_width, occ_width)
    energy_a = lax.dynamic_slice_in_dim(vir_energy, lax.axis_index("vir") * vir_width, vir_width)
    gamma_total = jnp.zeros(regrouped.shape, jnp.float32)
    for turn_index in range(ROUNDS):
        owner = round_owner[turn_index]
        owner_half = from_root(regrouped, "occ", owner)
        owner_whole = lax.all_gather(owner_half, "vir", axis=3, tiled=True)
        energy_j = lax.dynamic_slice_in_dim(occ_energy, owner * occ_width, occ_width)
        partial_value = jnp.einsum(
            "sria,srjb->ijab", regrouped, owner_whole, preferred_element_type=jnp.float32
        )
        base = energy_i[:, None, None] + energy_j[None, :, None] - energy_a[None, None, :]
        pair_block = lax.psum(partial_value.astype(jnp.bfloat16), "aux").astype(jnp.float32)
        amplitude = (pair_block / (base[..., None] - vir_energy)).astype(jnp.bfloat16)
        gamma_total = gamma_total + jnp.einsum(
            "ijab,srjb->sria", amplitude, owner_whole, preferred_element_type=jnp.float32
        )
    return gamma_total


def solution(mesh):
    placed = (P("occ", "aux", "grp", "vir"), P("grp"), P("grp"), P("grp"))
    return jax.shard_map(
        local, mesh=mesh, in_specs=placed, out_specs=P("grp", "aux", "occ", "vir"), check_vma=False
    )
```

profile of v0, /device:TPU:0, one launch (start us, length us, event | category | flops | bytes accessed | tf_op | source)
XLA Modules:
  0.0 432.3 jit_solution(8235440638298763735)
XLA Ops:
  6.5 3.6 copy.11
  10.1 0.0 copy-start.2
  10.1 6.4 %all-to-all-start = ((bf16[1,512,4,640]{3,1,0,2:T(8,128)(2,1)}), bf16[1,512,4,640]{3,1,0,2:T(8,128)(2,1)S(1)}, u32[]{:S(2)}, u32[]{:S(2)}) async-start(bf16[1,512,4,640]{3,1,0,2:T(8,128)(2,1)} %copy.11), calls=%async_computation | async-start | bytes 5242880 | tf_op jit(solution)/shard_map/all_to_all | solution.py:15
  16.5 0.0 all-reduce.5.cloned.1.call-start
  16.5 0.0 copy-done.2
  16.6 0.7 fusion.41
  18.5 57.4 %all-to-all-done = bf16[1,512,4,640]{3,1,0,2:T(8,128)(2,1)S(1)} async-done(((bf16[1,512,4,640]{3,1,0,2:T(8,128)(2,1)}), bf16[1,512,4,640]{3,1,0,2:T(8,128)(2,1)S(1)}, u32[]{:S(2)}, u32[]{:S(2)}) %all-to-all-start) | async-done | bytes 2621472 | tf_op jit(solution)/shard_map/all_to_all | solution.py:15
  76.0 2.8 fusion.28
  78.8 0.0 all-reduce.5.cloned.1.call-update
  78.8 0.0 all-gather.3.cloned.1.call-start
  78.8 188.5 %all-reduce.5.cloned.1.call-done = (bf16[4,512,1,640]{3,1,0,2:T(8,128)(2,1)}, bf16[4,512,1,640]{3,1,0,2:T(8,128)(2,1)}) async-done(((bf16[4,512,1,640]{3,1,0,2:T(8,128)(2,1)}, bf16[4,512,1,640]{3,1,0,2:T(8,128)(2,1)}), (bf16[4,512,1,640]{3,1,0,2:T(8,128)(2,1)}, bf16[4,512,1,640]{3,1,0,2:T(8,128)(2,1)})) %all-reduce.5.cloned.1.call-update) | async-done | bytes 5242896 | tf_op jit(solution)/shard_map/psum | solution.py:11
  267.3 0.0 all-gather.3.cloned.1.call-update
  267.4 0.0 all-gather.5.cloned.1.call-start
  267.4 0.7 all-gather.5.cloned.1.call-update
  268.1 0.0 all-reduce.7.cloned.1.call-start
  268.1 14.9 %all-gather.3.cloned.1.call-done = bf16[4,512,1,1280]{3,1,0,2:T(8,128)(2,1)} async-done(((bf16[4,512,1,640]{3,1,0,2:T(8,128)(2,1)}), bf16[4,512,1,1280]{3,1,0,2:T(8,128)(2,1)}) %all-gather.3.cloned.1.call-update) | async-done | bytes 5242896 | tf_op jit(solution)/shard_map/all_gather | solution.py:24
  283.0 8.0 %fusion.20 = bf16[1,1,640,1280]{2,3,0,1:T(8,128)(2,1)} fusion(bf16[4,512,1,1280]{3,1,0,2:T(8,128)(2,1)} %all-gather.3.cloned.1.call-done, bf16[1,512,4,640]{3,1,0,2:T(8,128)(2,1)S(1)} %all-to-all-done), kind=kOutput, calls=%fused_computation.15 | convolution fusion | flops 3356262400 | bytes 9502720 | tf_op jit(solution)/shard_map/sria,srjb->ijab/dot_general | solution.py:26
  291.0 9.9 %all-gather.5.cloned.1.call-done = bf16[4,512,1,1280]{3,1,0,2:T(8,128)(2,1)} async-done(((bf16[4,512,1,640]{3,1,0,2:T(8,128)(2,1)}), bf16[4,512,1,1280]{3,1,0,2:T(8,128)(2,1)}) %all-gather.5.cloned.1.call-update) | async-done | bytes 5242896 | tf_op jit(solution)/shard_map/all_gather | solution.py:24
  300.9 8.0 %fusion.23 = bf16[1,1,640,1280]{2,3,0,1:T(8,128)(2,1)} fusion(bf16[4,512,1,1280]{3,1,0,2:T(8,128)(2,1)} %all-gather.5.cloned.1.call-done, bf16[1,512,4,640]{3,1,0,2:T(8,128)(2,1)S(1)} %all-to-all-done), kind=kOutput, calls=%fused_computation.16 | convolution fusion | flops 3356262400 | bytes 9502720 | tf_op jit(solution)/shard_map/sria,srjb->ijab/dot_general | solution.py:26
  308.8 0.0 copy-start
  308.9 0.0 copy-start.1
  308.9 0.0 all-reduce.7.cloned.1.call-update
  312.8 0.0 copy-done
  312.9 0.7 fusion.40
  316.0 0.0 copy-done.1
  316.0 0.1 dynamic-slice_subtract_fusion.1
  316.1 82.9 %all-reduce.7.cloned.1.call-done = (bf16[1,1,640,1280]{2,3,0,1:T(8,128)(2,1)}, bf16[1,1,640,1280]{2,3,0,1:T(8,128)(2,1)}) async-done(((bf16[1,1,640,1280]{2,3,0,1:T(8,128)(2,1)}, bf16[1,1,640,1280]{2,3,0,1:T(8,128)(2,1)}), (bf16[1,1,640,1280]{2,3,0,1:T(8,128)(2,1)}, bf16[1,1,640,1280]{2,3,0,1:T(8,128)(2,1)})) %all-reduce.7.cloned.1.call-update) | async-done | bytes 3276816 | tf_op jit(solution)/shard_map/psum | solution.py:30
  399.0 0.0 copy-start.3
  399.0 7.2 %fusion = f32[4,512,640]{2,1,0:T(8,128)S(1)} fusion(bf16[4,512,1,1280]{3,1,0,2:T(8,128)(2,1)} %all-gather.5.cloned.1.call-done, bf16[1,1,640,1280]{2,3,0,1:T(8,128)(2,1)} %get-tuple-element.7, f32[640]{0:T(1024)S(1)} %get-tuple-element.12, f32[1280]{0:T(1024)S(1)} %copy-done.1), kind=kOutput, calls=%fused_computation | convolution fusion | flops 3358720000 | bytes 12131840 | tf_op jit(solution)/shard_map/ijab,srjb->sria/dot_general | solution.py:32
  406.2 0.0 copy-done.3
  406.2 9.3 %add_bitcast_fusion = f32[4,512,1,640]{3,1,0,2:T(8,128)} fusion(f32[4,512,640]{2,1,0:T(8,128)S(1)} %fusion, bf16[4,512,1,1280]{3,1,0,2:T(8,128)(2,1)} %all-gather.3.cloned.1.call-done, bf16[1,1,640,1280]{2,3,0,1:T(8,128)(2,1)S(1)} %copy-done.3, f32[1280]{0:T(1024)S(1)} %copy-done.1, f32[640]{0:T(1024)S(1)} %get-tuple-element.11), kind=kOutput, calls=%fused_computation.8 | convolution fusion | flops 3360030720 | bytes 17374720 | tf_op jit(solution)/shard_map/ijab,srjb->sria/dot_general | solution.py:32
  415.5 10.2 %copy.16 = f32[4,512,1,640]{3,2,1,0:T(1,128)} copy(f32[4,512,1,640]{3,1,0,2:T(8,128)} %add_bitcast_fusion) | data formatting | bytes 10485760 | tf_op jit(solution)/shard_map/add | solution.py:32
Async XLA Ops:
  10.1 6.5 %copy-start.2 = (s32[2]{0:T(128)S(1)}, s32[2]{0:T(128)}, u32[]{:S(2)}) copy-start(s32[2]{0:T(128)} %param.7) | copy-start | bytes 28
  10.1 65.9 %all-to-all-start = ((bf16[1,512,4,640]{3,1,0,2:T(8,128)(2,1)}), bf16[1,512,4,640]{3,1,0,2:T(8,128)(2,1)S(1)}, u32[]{:S(2)}, u32[]{:S(2)}) async-start(bf16[1,512,4,640]{3,1,0,2:T(8,128)(2,1)} %copy.11), calls=%async_computation | async-start | bytes 5242880 | tf_op jit(solution)/shard_map/all_to_all | solution.py:15
  16.5 250.8 %all-reduce.5.cloned.1.call-start = ((), (), s32[]{:S(2)}) async-start(), calls=%async_computation.3 | async-start | bytes 10485760 | tf_op jit(solution)/shard_map/psum | solution.py:11
  78.8 204.2 %all-gather.3.cloned.1.call-start = ((), (), s32[]{:S(2)}) async-start(), calls=%async_computation.1 | async-start | bytes 7864320 | tf_op jit(solution)/shard_map/all_gather | solution.py:24
  267.4 33.5 %all-gather.5.cloned.1.call-start = ((), (), s32[]{:S(2)}) async-start(), calls=%async_computation.2 | async-start | bytes 7864320 | tf_op jit(solution)/shard_map/all_gather | solution.py:24
  268.1 130.9 %all-reduce.7.cloned.1.call-start = ((), (), s32[]{:S(2)}) async-start(), calls=%async_computation.4 | async-start | bytes 6553600 | tf_op jit(solution)/shard_map/psum | solution.py:30
  308.8 4.0 copy-start
  308.9 7.1 %copy-start.1 = (f32[1280]{0:T(1024)S(1)}, f32[1280]{0:T(1024)}, u32[]{:S(2)}) copy-start(f32[1280]{0:T(1024)} %param.6) | copy-start | bytes 15364
  399.0 7.2 %copy-start.3 = (bf16[1,1,640,1280]{2,3,0,1:T(8,128)(2,1)S(1)}, bf16[1,1,640,1280]{2,3,0,1:T(8,128)(2,1)}, u32[]{:S(2)}) copy-start(bf16[1,1,640,1280]{2,3,0,1:T(8,128)(2,1)} %get-tuple-element.8) | copy-start | bytes 4915204
Sparse Core Ops, SparseCore 0:
  78.9 188.3 all-reduce.4
  268.9 14.0 all-gather.2
  284.6 16.2 all-gather.4
  309.0 89.9 all-reduce.6
where the time goes:
time: 433 us; the launch traced here: 432 us
  waiting for transfers between devices  354 us (82%)
  matrix products  32.4 us (7%)
  between operations  20.9 us (5%)
  local copies, waits for them, and re-layouts  15.1 us (3%)
  starting transfers between devices  6.57 us (2%)
    psum x1, waiting for transfers between devices, from_root(): return lax.psum(jnp.where(mine, value, jnp.zeros_like(value)), axis)  188 us
    psum x1, waiting for transfers between devices, local(): lax.psum(partial_value.astype(jnp.bfloat16), 'aux').astype(jnp.float32)  82.9 us
    all_to_all x1, waiting for transfers between devices, local(): lax.all_to_all(integrals, 'occ', split_axis=2, concat_axis=0, tiled=True)  57.4 us
    all_gather x2, waiting for transfers between devices, local(): owner_whole = lax.all_gather(owner_half, 'vir', axis=3, tiled=True)  24.8 us
    dot_general x2, matrix products, local(): jnp.einsum('ijab,srjb->sria', amplitude, owner_whole, preferred_element_t...  16.5 us
    dot_general x2, matrix products, local(): jnp.einsum('sria,srjb->ijab', regrouped, owner_whole, preferred_element_t...  15.9 us
    add x1, local copies, waits for them, and re-layouts, local(): gamma_total + jnp.einsum('ijab,srjb->sria', amplitude, owner_whole, prefe...  10.2 us
  transfers between devices with their start and end apart: 5, of which 5 were waited for; matrix products, arithmetic and copies ran while one was open for 2% of the time, Pallas kernels for 0%

commit v1 on v0

v1 whole, which is shorter than its diff:
```python
import jax
import jax.numpy as jnp
from jax import lax
from jax.sharding import PartitionSpec as P

ROUNDS = 2


def exchange_sum(part, axis, n):
    total = part.astype(jnp.float32)
    for d in range(1, n):
        perm = [(k, (k + d) % n) for k in range(n)]
        total = total + lax.ppermute(part, axis, perm).astype(jnp.float32)
    return total


def column_chunks(width):
    if width % 128 or width < 512:
        return [(t, 0, width) for t in range(ROUNDS)]
    big = (width // 256) * 128
    return [(0, 0, big), (0, big, width - big), (1, 0, width - big), (1, width - big, big)]


def regroup_four(x, me):
    slots = [lax.dynamic_index_in_dim(x, me, 1, keepdims=False)]
    for k in (1, 2, 3):
        send = lax.dynamic_index_in_dim(x, me ^ k, 1, keepdims=False)
        slots.append(lax.ppermute(send, "occ", [(z, z ^ k) for z in range(4)]))
    return jnp.concatenate(slots, axis=0)


def gather_four(own, me):
    rows = own.shape[0]
    near = lax.ppermute(own, "occ", [(0, 1), (1, 0), (2, 3), (3, 2)])
    half = jnp.concatenate([own, near], axis=0)
    mid = lax.ppermute(half, "occ", [(1, 2), (2, 1)])
    end = lax.ppermute(mid, "occ", [(1, 0), (2, 3)])
    is_mid = (me == 1) | (me == 2)
    swapped = jnp.concatenate([mid[rows:], mid[:rows]], axis=0)
    far = jnp.where(is_mid, swapped, end)
    return jnp.concatenate([half, far], axis=0)


def local(integrals, occ_energy, vir_energy, round_owner):
    n_occ = lax.axis_size("occ")
    n_aux = lax.axis_size("aux")
    me = lax.axis_index("occ")
    core = lax.axis_index("vir")
    x = integrals[0]
    rows, _, width = x.shape
    four = n_occ == 4
    if four:
        mine = regroup_four(x, me)
    else:
        mine = lax.all_to_all(x, "occ", split_axis=1, concat_axis=0, tiled=True)[:, 0]
    energy_i = lax.dynamic_slice_in_dim(occ_energy, me, 1)
    energy_a = lax.dynamic_slice_in_dim(vir_energy, core * width, width)
    gamma = None
    for turn, start, size in column_chunks(width):
        owner = round_owner[turn]
        own = lax.dynamic_slice(x, (0, owner, start), (rows, 1, size))[:, 0]
        if four:
            whole = gather_four(own, me)
        else:
            whole = lax.all_gather(own, "occ", axis=0, tiled=True)
        other = lax.ppermute(whole, "vir", [(0, 1), (1, 0)])
        partial_value = jnp.concatenate(
            [
                jnp.einsum("pb,pa->ba", block, mine, preferred_element_type=jnp.float32).astype(jnp.bfloat16)
                for block in (whole, other)
            ],
            axis=0,
        )
        pair = exchange_sum(partial_value, "aux", n_aux)
        energy_j = lax.dynamic_slice_in_dim(occ_energy, owner, 1)
        energy_b = jnp.concatenate(
            [
                lax.dynamic_slice_in_dim(vir_energy, half * width + start, size)
                for half in (core, 1 - core)
            ]
        )
        base = energy_i + energy_j - energy_a
        amplitude = (pair / (base[None, :] - energy_b[:, None])).astype(jnp.bfloat16)
        for k, block in enumerate((whole, other)):
            term = jnp.dot(block, amplitude[k * size : (k + 1) * size], preferred_element_type=jnp.float32)
            gamma = term if gamma is None else gamma + term
    gamma = gamma.reshape(n_occ, rows, width)
    if four:
        gamma = jnp.stack([lax.dynamic_index_in_dim(gamma, s ^ me, 0, keepdims=False) for s in range(4)])
    return gamma[:, :, None, :]


def solution(mesh):
    placed = (P("occ", "aux", "grp", "vir"), P("grp"), P("grp"), P("grp"))
    return jax.shard_map(
        local, mesh=mesh, in_specs=placed, out_specs=P("grp", "aux", "occ", "vir"), check_vma=False
    )
```

time: 433 us -> 299 us (0.69)
  waiting for transfers between devices: 354 us -> 154 us
  matrix products: 32.4 us -> 58.1 us
  starting transfers between devices: 6.57 us -> 32 us
  local copies, waits for them, and re-layouts: 15.1 us -> 31.9 us
  between operations: 20.9 us -> 6.89 us
  other arithmetic: 2.88 us -> 15.4 us
    psum x2 -> x0, waiting for transfers between devices: 271 us -> none  [the longest x1 188 us: from_root(): return lax.psum(jnp.where(mine, value, jnp.zeros_like(value)), axis)]
    ppermute x0 -> x23, waiting for transfers between devices: none -> 154 us  [the longest x4 102 us: gather_four(): end = lax.ppermute(mid, 'occ', [(1, 0), (2, 3)])]
    all_to_all x1 -> x0, waiting for transfers between devices: 57.4 us -> none  [local(): lax.all_to_all(integrals, 'occ', split_axis=2, concat_axis=0, tiled=True)]
    ppermute x0 -> x23, starting transfers between devices: none -> 32 us  [the longest x3 10.3 us: regroup_four(): slots.append(lax.ppermute(send, 'occ', [(z, z ^ k) for z in range(4)]))]
    dot_general x4 -> x16, matrix products: 32.4 us -> 58.1 us  [the longest x8 38.6 us: local(): jnp.dot(block, amplitude[k * size:(k + 1) * size], preferred_element_type...]
    all_gather x2 -> x0, waiting for transfers between devices: 24.8 us -> none  [local(): owner_whole = lax.all_gather(owner_half, 'vir', axis=3, tiled=True)]
    dynamic_slice x1 -> x7, local copies, waits for them, and re-layouts: 0.68 us -> 14.4 us  [the longest x1 6.52 us: regroup_four(): slots = [lax.dynamic_index_in_dim(x, me, 1, keepdims=False)]]
    concatenate x0 -> x16, other arithmetic: none -> 12.7 us  [the longest x4 7.7 us: gather_four(): half = jnp.concatenate([own, near], axis=0)]
  transfers between devices with their start and end apart: 5 -> 23, of which waited for: 5 -> 9; matrix products, arithmetic and copies ran while one was open for 2% -> 23% of each run, Pallas kernels for 0% -> 0%
where the time goes in v1:
time: 299 us; the launch traced here: 298 us
  waiting for transfers between devices  154 us (52%)
  matrix products  58.1 us (19%)
  starting transfers between devices  32 us (11%)
  local copies, waits for them, and re-layouts  31.9 us (11%)
  other arithmetic  15.4 us (5%)
  between operations  6.89 us (2%)
    ppermute x4, waiting for transfers between devices, gather_four(): end = lax.ppermute(mid, 'occ', [(1, 0), (2, 3)])  102 us
    ppermute x4, waiting for transfers between devices, exchange_sum(): total = total + lax.ppermute(part, axis, perm).astype(jnp.float32)  50.6 us
    dot_general x8, matrix products, local(): jnp.dot(block, amplitude[k * size:(k + 1) * size], preferred_element_type...  38.6 us
    dot_general x8, matrix products, local(): jnp.einsum('pb,pa->ba', block, mine, preferred_element_type=jnp.float32)  19.5 us
    ppermute x3, starting transfers between devices, regroup_four(): slots.append(lax.ppermute(send, 'occ', [(z, z ^ k) for z in range(4)]))  10.3 us
    concatenate x4, other arithmetic, gather_four(): half = jnp.concatenate([own, near], axis=0)  7.7 us
    unnamed x28, local copies, waits for them, and re-layouts  6.81 us
    dynamic_slice x1, local copies, waits for them, and re-layouts, regroup_four(): slots = [lax.dynamic_index_in_dim(x, me, 1, keepdims=False)]  6.52 us
  transfers between devices with their start and end apart: 23, of which 9 were waited for; matrix products, arithmetic and copies ran while one was open for 23% of the time, Pallas kernels for 0%

profile of v1, /device:TPU:0, one launch (start us, length us, event | category | flops | bytes accessed | tf_op | source)
XLA Modules:
  0.0 297.9 jit_solution(18357245988094159566)
XLA Ops:
  5.4 2.6 constant_dynamic-slice_fusion.11
  8.1 3.1 %collective-permute-start.18 = (bf16[512,256]{1,0:T(8,128)(2,1)S(1)}, bf16[512,256]{1,0:T(8,128)(2,1)}, u32[]{:S(2)}, u32[]{:S(2)}) collective-permute-start(bf16[512,256]{1,0:T(8,128)(2,1)S(1)} %bitcast.38), channel_id=1, source_target_pairs={{0,4},{4,0},{8,12},{12,8},{1,5},{5,1},{9,13},{13,9},{2,6},{6,2},{1... | collective-permute-start | bytes 786440 | tf_op jit(solution)/shard_map/ppermute | solution.py:34
  13.8 2.0 collective-permute-start.13
  16.7 6.5 %constant_dynamic-slice_fusion.10 = (bf16[1,512,1,640]{3,2,1,0:T(2,128)(2,1)}, bf16[1,512,1,640]{3,2,1,0:T(2,128)(2,1)}, bf16[1,512,1,640]{3,2,1,0:T(2,128)(2,1)}, bf16[1,512,1,640]{3,2,1,0:T(2,128)(2,1)S(1)}) fusion(bf16[1,512,4,640]{3,2,1,0:T(4,128)(2,1)S(1)} %copy-done, s32[]{:T(128)S(6)} %select_n.79, s32[]{:T(128)S(6)} %select_n.82, s32[]{:T(128)S(6)} %select_n.81, ...), kind=kLoop, calls=%fused_computation.68 | loop fusion | bytes 5242896 | tf_op jit(solution)/shard_map/jit(dynamic_index_in_dim)/dynamic_slice | solution.py:25
  36.2 2.1 pad_maximum_fusion.9
  40.9 2.1 pad_maximum_fusion.8
  44.5 2.3 copy.32
  48.7 7.3 %collective-permute-start.4 = (bf16[512,640]{1,0:T(8,128)(2,1)}, bf16[512,640]{1,0:T(8,128)(2,1)S(1)}, u32[]{:S(2)}, u32[]{:S(2)}) collective-permute-start(bf16[512,640]{1,0:T(8,128)(2,1)} %bitcast.30), channel_id=1, source_target_pairs={{0,8},{4,12},{8,0},{12,4},{1,9},{5,13},{9,1},{13,5},{2,10},{6,14},... | collective-permute-start | bytes 1966088 | tf_op jit(solution)/shard_map/ppermute | solution.py:28
  64.1 33.3 %collective-permute-done.2 = bf16[1024,256]{1,0:T(8,128)(2,1)S(1)} collective-permute-done((bf16[1024,256]{1,0:T(8,128)(2,1)}, bf16[1024,256]{1,0:T(8,128)(2,1)S(1)}, u32[]{:S(2)}, u32[]{:S(2)}) %collective-permute-start.2) | collective-permute-done | bytes 524320 | tf_op jit(solution)/shard_map/ppermute | solution.py:37
  100.0 45.0 %collective-permute-done.20 = bf16[1024,256]{1,0:T(8,128)(2,1)S(1)} collective-permute-done((bf16[1024,256]{1,0:T(8,128)(2,1)}, bf16[1024,256]{1,0:T(8,128)(2,1)S(1)}, u32[]{:S(2)}, u32[]{:S(2)}) %collective-permute-start.20) | collective-permute-done | bytes 524320 | tf_op jit(solution)/shard_map/ppermute | solution.py:37
  148.2 2.2 convolution_convert_fusion.5
  150.5 2.2 convolution_convert_fusion.7
  152.6 9.2 %collective-permute-done.15 = bf16[1024,384]{1,0:T(8,128)(2,1)S(1)} collective-permute-done((bf16[1024,384]{1,0:T(8,128)(2,1)}, bf16[1024,384]{1,0:T(8,128)(2,1)S(1)}, u32[]{:S(2)}, u32[]{:S(2)}) %collective-permute-start.15) | collective-permute-done | bytes 786464 | tf_op jit(solution)/shard_map/ppermute | solution.py:37
  163.4 14.3 %collective-permute-done.10 = bf16[1024,384]{1,0:T(8,128)(2,1)S(1)} collective-permute-done((bf16[1024,384]{1,0:T(8,128)(2,1)}, bf16[1024,384]{1,0:T(8,128)(2,1)S(1)}, u32[]{:S(2)}, u32[]{:S(2)}) %collective-permute-start.10) | collective-permute-done | bytes 786464 | tf_op jit(solution)/shard_map/ppermute | solution.py:37
  179.3 2.8 convolution_convert_fusion.3
  182.1 2.1 convolution_convert_fusion.6
  185.9 2.8 convolution_convert_fusion.1
  188.7 2.1 convolution_convert_fusion.4
  191.4 10.5 %collective-permute-done.7 = bf16[512,640]{1,0:T(8,128)(2,1)S(1)} collective-permute-done((bf16[512,640]{1,0:T(8,128)(2,1)S(1)}, bf16[512,640]{1,0:T(8,128)(2,1)S(1)}, u32[]{:S(2)}, u32[]{:S(2)}) %collective-permute-start.7) | collective-permute-done | bytes 655392 | tf_op jit(solution)/shard_map/ppermute | solution.py:13
  203.2 12.3 %collective-permute-done.22 = bf16[512,640]{1,0:T(8,128)(2,1)S(1)} collective-permute-done((bf16[512,640]{1,0:T(8,128)(2,1)S(1)}, bf16[512,640]{1,0:T(8,128)(2,1)S(1)}, u32[]{:S(2)}, u32[]{:S(2)}) %collective-permute-start.22) | collective-permute-done | bytes 655392 | tf_op jit(solution)/shard_map/ppermute | solution.py:13
  215.9 3.3 %fusion.8 = f32[2048,640]{1,0:T(8,128)} fusion(bf16[2048,256]{1,0:T(8,128)(2,1)S(1)} %collective-permute-done.21, bf16[512,640]{1,0:T(8,128)(2,1)S(1)} %divide_convert_fusion.2), kind=kOutput, calls=%fused_computation.45 | convolution fusion | flops 671088640 | bytes 6619136 | tf_op jit(solution)/shard_map/dot_general | solution.py:85
  219.2 2.5 convolution_convert_fusion
  225.4 2.8 convolution_convert_fusion.2
  228.9 17.7 %collective-permute-done.17 = bf16[768,640]{1,0:T(8,128)(2,1)S(1)} collective-permute-done((bf16[768,640]{1,0:T(8,128)(2,1)S(1)}, bf16[768,640]{1,0:T(8,128)(2,1)S(1)}, u32[]{:S(2)}, u32[]{:S(2)}) %collective-permute-start.17) | collective-permute-done | bytes 983072 | tf_op jit(solution)/shard_map/ppermute | solution.py:13
  247.1 5.1 %fusion.2 = f32[2048,640]{1,0:T(8,128)} fusion(bf16[768,640]{1,0:T(8,128)(2,1)S(1)} %divide_convert_fusion, bf16[1024,384]{1,0:T(8,128)(2,1)S(1)} %maximum_select_fusion.1, bf16[512,384]{1,0:T(8,128)(2,1)} %collective-permute-done.13, bf16[512,384]{1,0:T(8,128)(2,1)} %bitcast.33), kind=kOutput, calls=%fused_computation.37 | convolution fusion | flops 1011351552 | bytes 7307264 | tf_op jit(solution)/shard_map/dot_general | solution.py:85
  252.2 4.1 %fusion = f32[2048,640]{1,0:T(8,128)} fusion(bf16[2048,384]{1,0:T(8,128)(2,1)S(1)} %collective-permute-done.16, bf16[768,640]{1,0:T(8,128)(2,1)S(1)} %divide_convert_fusion), kind=kOutput, calls=%fused_computation.35 | convolution fusion | flops 1006632960 | bytes 7307264 | tf_op jit(solution)/shard_map/dot_general | solution.py:85
  256.3 10.1 %collective-permute-done.12 = bf16[768,640]{1,0:T(8,128)(2,1)S(1)} collective-permute-done((bf16[768,640]{1,0:T(8,128)(2,1)S(1)}, bf16[768,640]{1,0:T(8,128)(2,1)S(1)}, u32[]{:S(2)}, u32[]{:S(2)}) %collective-permute-start.12) | collective-permute-done | bytes 983072 | tf_op jit(solution)/shard_map/ppermute | solution.py:13
  266.9 4.0 %fusion.4 = f32[2048,640]{1,0:T(8,128)} fusion(bf16[2048,384]{1,0:T(8,128)(2,1)S(1)} %collective-permute-done.11, bf16[768,640]{1,0:T(8,128)(2,1)S(1)} %divide_convert_fusion.1), kind=kOutput, calls=%fused_computation.39 | convolution fusion | flops 1006632960 | bytes 7307264 | tf_op jit(solution)/shard_map/dot_general | solution.py:85
  270.8 5.1 %fusion.6 = f32[2048,640]{1,0:T(8,128)} fusion(bf16[768,640]{1,0:T(8,128)(2,1)S(1)} %divide_convert_fusion.1, bf16[1024,384]{1,0:T(8,128)(2,1)S(1)} %maximum_select_fusion, bf16[512,384]{1,0:T(8,128)(2,1)} %collective-permute-done.8, bf16[512,384]{1,0:T(8,128)(2,1)} %bitcast.34), kind=kOutput, calls=%fused_computation.41 | convolution fusion | flops 1011351552 | bytes 7307264 | tf_op jit(solution)/shard_map/dot_general | solution.py:85
  275.9 14.1 %add_add_fusion = f32[2048,640]{1,0:T(8,128)} fusion(f32[2048,640]{1,0:T(8,128)} %fusion.8, f32[2048,640]{1,0:T(8,128)} %fusion, f32[2048,640]{1,0:T(8,128)} %fusion.2, f32[2048,640]{1,0:T(8,128)} %fusion.4, f32[2048,640]{1,0:T(8,128)} %fusion.6, f32[2048,640]{1,0:T(8,128)S(1)} %fusion.13, f32[2048,640]{1,0:T(8,128)S(1)} %fusion.11, ...), kind=kOutput, calls=%fused_computation.1 | convolution fusion | flops 683409408 | bytes 43319296 | tf_op jit(solution)/shard_map/dot_general | solution.py:85
  290.0 2.8 constant_dynamic-slice_fusion.3
  293.2 4.7 %broadcast_in_dim.2 = f32[4,512,1,640]{3,2,1,0:T(1,128)} reshape(f32[4,512,640]{2,1,0:T(8,128)S(1)} %pad_maximum_fusion) | data formatting | bytes 10485760 | tf_op jit(solution)/shard_map/broadcast_in_dim | solution.py:90
  (97 shorter events, 47.8 us)
Async XLA Ops:
  0.0 11.3 %copy-start = (bf16[1,512,4,640]{3,2,1,0:T(4,128)(2,1)S(1)}, bf16[1,512,4,640]{3,2,1,0:T(4,128)(2,1)}, u32[]{:S(2)}) copy-start(bf16[1,512,4,640]{3,2,1,0:T(4,128)(2,1)} %param.4) | copy-start | bytes 7864324
  8.1 24.7 %collective-permute-start.18 = (bf16[512,256]{1,0:T(8,128)(2,1)S(1)}, bf16[512,256]{1,0:T(8,128)(2,1)}, u32[]{:S(2)}, u32[]{:S(2)}) collective-permute-start(bf16[512,256]{1,0:T(8,128)(2,1)S(1)} %bitcast.38), channel_id=1, source_target_pairs={{0,4},{4,0},{8,12},{12,8},{1,5},{5,1},{9,13},{13,9},{2,6},{6,2},{1... | collective-permute-start | bytes 786440 | tf_op jit(solution)/shard_map/ppermute | solution.py:34
  11.2 87.7 %copy-start.3 = (bf16[1,512,1,256]{3,1,2,0:T(8,128)(2,1)}, bf16[1,512,1,256]{3,1,2,0:T(8,128)(2,1)S(1)}, u32[]{:S(2)}) copy-start(bf16[1,512,1,256]{3,1,2,0:T(8,128)(2,1)S(1)} %copy.36) | copy-start | bytes 786436
  11.3 18.3 %collective-permute-start = (bf16[512,256]{1,0:T(8,128)(2,1)S(1)}, bf16[512,256]{1,0:T(8,128)(2,1)}, u32[]{:S(2)}, u32[]{:S(2)}) collective-permute-start(bf16[512,256]{1,0:T(8,128)(2,1)S(1)} %bitcast.43), channel_id=1, source_target_pairs={{0,4},{4,0},{8,12},{12,8},{1,5},{5,1},{9,13},{13,9},{2,6},{6,2},{1... | collective-permute-start | bytes 786440 | tf_op jit(solution)/shard_map/ppermute | solution.py:34
  13.8 22.4 %collective-permute-start.13 = (bf16[512,384]{1,0:T(8,128)(2,1)}, bf16[512,384]{1,0:T(8,128)(2,1)}, u32[]{:S(2)}, u32[]{:S(2)}) collective-permute-start(bf16[512,384]{1,0:T(8,128)(2,1)} %bitcast.33), channel_id=1, source_target_pairs={{0,4},{4,0},{8,12},{12,8},{1,5},{5,1},{9,13},{13,9},{2,6},{6,2},{1... | collective-permute-start | bytes 1179656 | tf_op jit(solution)/shard_map/ppermute | solution.py:34
  16.6 24.3 %collective-permute-start.8 = (bf16[512,384]{1,0:T(8,128)(2,1)}, bf16[512,384]{1,0:T(8,128)(2,1)}, u32[]{:S(2)}, u32[]{:S(2)}) collective-permute-start(bf16[512,384]{1,0:T(8,128)(2,1)} %bitcast.34), channel_id=1, source_target_pairs={{0,4},{4,0},{8,12},{12,8},{1,5},{5,1},{9,13},{13,9},{2,6},{6,2},{1... | collective-permute-start | bytes 1179656 | tf_op jit(solution)/shard_map/ppermute | solution.py:34
  16.6 9.4 %copy-start.8 = (f32[1280]{0:T(1024)S(1)}, f32[1280]{0:T(1024)}, u32[]{:S(2)}) copy-start(f32[1280]{0:T(1024)} %param.6) | copy-start | bytes 15364
  16.7 9.6 %copy-start.9 = (f32[4]{0:T(128)S(1)}, f32[4]{0:T(128)}, u32[]{:S(2)}) copy-start(f32[4]{0:T(128)} %param.5) | copy-start | bytes 52
  24.1 123.5 %collective-permute-start.3 = (bf16[512,640]{1,0:T(8,128)(2,1)}, bf16[512,640]{1,0:T(8,128)(2,1)}, u32[]{:S(2)}, u32[]{:S(2)}) collective-permute-start(bf16[512,640]{1,0:T(8,128)(2,1)} %bitcast.31), channel_id=1, source_target_pairs={{0,4},{4,0},{8,12},{12,8},{1,5},{5,1},{9,13},{13,9},{2,6},{6,2},{1... | collective-permute-start | bytes 1966088 | tf_op jit(solution)/shard_map/ppermute | solution.py:28
  31.3 17.4 %collective-permute-start.1 = (bf16[1024,256]{1,0:T(8,128)(2,1)}, bf16[1024,256]{1,0:T(8,128)(2,1)}, u32[]{:S(2)}, u32[]{:S(2)}) collective-permute-start(bf16[1024,256]{1,0:T(8,128)(2,1)} %pad_maximum_fusion.12), channel_id=1, source_target_pairs={{4,8},{8,4},{5,9},{9,5},{6,10},{10,6},{7,11},{11,7},{20,24},{24,20... | collective-permute-start | bytes 1572872 | tf_op jit(solution)/shard_map/ppermute | solution.py:36
  34.6 12.3 %copy-start.2 = (bf16[1,512,1,640]{3,2,1,0:T(2,128)(2,1)S(1)}, bf16[1,512,1,640]{3,2,1,0:T(2,128)(2,1)}, u32[]{:S(2)}) copy-start(bf16[1,512,1,640]{3,2,1,0:T(2,128)(2,1)} %get-tuple-element.14) | copy-start | bytes 1966084
  34.6 22.5 %collective-permute-start.19 = (bf16[1024,256]{1,0:T(8,128)(2,1)}, bf16[1024,256]{1,0:T(8,128)(2,1)}, u32[]{:S(2)}, u32[]{:S(2)}) collective-permute-start(bf16[1024,256]{1,0:T(8,128)(2,1)} %pad_maximum_fusion.13), channel_id=1, source_target_pairs={{4,8},{8,4},{5,9},{9,5},{6,10},{10,6},{7,11},{11,7},{20,24},{24,20... | collective-permute-start | bytes 1572872 | tf_op jit(solution)/shard_map/ppermute | solution.py:36
  38.3 21.1 %collective-permute-start.14 = (bf16[1024,384]{1,0:T(8,128)(2,1)}, bf16[1024,384]{1,0:T(8,128)(2,1)}, u32[]{:S(2)}, u32[]{:S(2)}) collective-permute-start(bf16[1024,384]{1,0:T(8,128)(2,1)} %pad_maximum_fusion.9), channel_id=1, source_target_pairs={{4,8},{8,4},{5,9},{9,5},{6,10},{10,6},{7,11},{11,7},{20,24},{24,20... | collective-permute-start | bytes 2359304 | tf_op jit(solution)/shard_map/ppermute | solution.py:36
  39.9 7.9 %copy-start.1 = (bf16[1,512,1,640]{3,2,1,0:T(2,128)(2,1)S(1)}, bf16[1,512,1,640]{3,2,1,0:T(2,128)(2,1)}, u32[]{:S(2)}) copy-start(bf16[1,512,1,640]{3,2,1,0:T(2,128)(2,1)} %get-tuple-element.15) | copy-start | bytes 1966084
  43.0 18.6 %collective-permute-start.9 = (bf16[1024,384]{1,0:T(8,128)(2,1)}, bf16[1024,384]{1,0:T(8,128)(2,1)}, u32[]{:S(2)}, u32[]{:S(2)}) collective-permute-start(bf16[1024,384]{1,0:T(8,128)(2,1)} %pad_maximum_fusion.8), channel_id=1, source_target_pairs={{4,8},{8,4},{5,9},{9,5},{6,10},{10,6},{7,11},{11,7},{20,24},{24,20... | collective-permute-start | bytes 2359304 | tf_op jit(solution)/shard_map/ppermute | solution.py:36
  47.7 11.7 %copy-start.7 = (bf16[1,512,1,640]{3,1,2,0:T(8,128)(2,1)S(1)}, bf16[1,512,1,640]{3,1,2,0:T(8,128)(2,1)}, u32[]{:S(2)}) copy-start(bf16[1,512,1,640]{3,1,2,0:T(8,128)(2,1)} %copy.29) | copy-start | bytes 1966084
  48.7 99.0 %collective-permute-start.4 = (bf16[512,640]{1,0:T(8,128)(2,1)}, bf16[512,640]{1,0:T(8,128)(2,1)S(1)}, u32[]{:S(2)}, u32[]{:S(2)}) collective-permute-start(bf16[512,640]{1,0:T(8,128)(2,1)} %bitcast.30), channel_id=1, source_target_pairs={{0,8},{4,12},{8,0},{12,4},{1,9},{5,13},{9,1},{13,5},{2,10},{6,14},... | collective-permute-start | bytes 1966088 | tf_op jit(solution)/shard_map/ppermute | solution.py:28
  57.0 40.4 %collective-permute-start.2 = (bf16[1024,256]{1,0:T(8,128)(2,1)}, bf16[1024,256]{1,0:T(8,128)(2,1)S(1)}, u32[]{:S(2)}, u32[]{:S(2)}) collective-permute-start(bf16[1024,256]{1,0:T(8,128)(2,1)} %collective-permute-done.1), channel_id=1, source_target_pairs={{4,0},{8,12},{5,1},{9,13},{6,2},{10,14},{7,3},{11,15},{20,16},{24,... | collective-permute-start | bytes 1572872 | tf_op jit(solution)/shard_map/ppermute | solution.py:37
  59.4 88.8 %collective-permute-start.5 = (bf16[512,640]{1,0:T(8,128)(2,1)S(1)}, bf16[512,640]{1,0:T(8,128)(2,1)S(1)}, u32[]{:S(2)}, u32[]{:S(2)}) collective-permute-start(bf16[512,640]{1,0:T(8,128)(2,1)S(1)} %bitcast.56), channel_id=1, source_target_pairs={{0,12},{4,8},{8,4},{12,0},{1,13},{5,9},{9,5},{13,1},{2,14},{6,10},... | collective-permute-start | bytes 1966088 | tf_op jit(solution)/shard_map/ppermute | solution.py:28
  61.6 83.4 %collective-permute-start.20 = (bf16[1024,256]{1,0:T(8,128)(2,1)}, bf16[1024,256]{1,0:T(8,128)(2,1)S(1)}, u32[]{:S(2)}, u32[]{:S(2)}) collective-permute-start(bf16[1024,256]{1,0:T(8,128)(2,1)} %collective-permute-done.19), channel_id=1, source_target_pairs={{4,0},{8,12},{5,1},{9,13},{6,2},{10,14},{7,3},{11,15},{20,16},{24,... | collective-permute-start | bytes 1572872 | tf_op jit(solution)/shard_map/ppermute | solution.py:37
  97.5 64.4 %collective-permute-start.15 = (bf16[1024,384]{1,0:T(8,128)(2,1)}, bf16[1024,384]{1,0:T(8,128)(2,1)S(1)}, u32[]{:S(2)}, u32[]{:S(2)}) collective-permute-start(bf16[1024,384]{1,0:T(8,128)(2,1)} %collective-permute-done.14), channel_id=1, source_target_pairs={{4,0},{8,12},{5,1},{9,13},{6,2},{10,14},{7,3},{11,15},{20,16},{24,... | collective-permute-start | bytes 2359304 | tf_op jit(solution)/shard_map/ppermute | solution.py:37
  98.9 49.3 %copy-start.6 = (bf16[1,512,1,640]{3,1,2,0:T(8,128)(2,1)S(1)}, bf16[1,512,1,640]{3,1,2,0:T(8,128)(2,1)}, u32[]{:S(2)}) copy-start(bf16[1,512,1,640]{3,1,2,0:T(8,128)(2,1)} %copy.32) | copy-start | bytes 1966084
  145.0 32.8 %collective-permute-start.10 = (bf16[1024,384]{1,0:T(8,128)(2,1)}, bf16[1024,384]{1,0:T(8,128)(2,1)S(1)}, u32[]{:S(2)}, u32[]{:S(2)}) collective-permute-start(bf16[1024,384]{1,0:T(8,128)(2,1)} %collective-permute-done.9), channel_id=1, source_target_pairs={{4,0},{8,12},{5,1},{9,13},{6,2},{10,14},{7,3},{11,15},{20,16},{24,... | collective-permute-start | bytes 2359304 | tf_op jit(solution)/shard_map/ppermute | solution.py:37
  147.6 41.0 %collective-permute-start.21 = (bf16[2048,256]{1,0:T(8,128)(2,1)S(1)}, bf16[2048,256]{1,0:T(8,128)(2,1)S(1)}, u32[]{:S(2)}, u32[]{:S(2)}) collective-permute-start(bf16[2048,256]{1,0:T(8,128)(2,1)S(1)} %pad_maximum_fusion.5), channel_id=1, source_target_pairs={{0,1},{1,0},{2,3},{3,2},{4,5},{5,4},{6,7},{7,6},{8,9},{9,8},{10,11... | collective-permute-start | bytes 3145736 | tf_op jit(solution)/shard_map/ppermute | solution.py:66
  147.7 34.4 %collective-permute-start.6 = (bf16[2048,256]{1,0:T(8,128)(2,1)S(1)}, bf16[2048,256]{1,0:T(8,128)(2,1)S(1)}, u32[]{:S(2)}, u32[]{:S(2)}) collective-permute-start(bf16[2048,256]{1,0:T(8,128)(2,1)S(1)} %pad_maximum_fusion.4), channel_id=1, source_target_pairs={{0,1},{1,0},{2,3},{3,2},{4,5},{5,4},{6,7},{7,6},{8,9},{9,8},{10,11... | collective-permute-start | bytes 3145736 | tf_op jit(solution)/shard_map/ppermute | solution.py:66
  163.3 55.9 %collective-permute-start.16 = (bf16[2048,384]{1,0:T(8,128)(2,1)S(1)}, bf16[2048,384]{1,0:T(8,128)(2,1)S(1)}, u32[]{:S(2)}, u32[]{:S(2)}) collective-permute-start(bf16[2048,384]{1,0:T(8,128)(2,1)S(1)} %pad_maximum_fusion.3), channel_id=1, source_target_pairs={{0,1},{1,0},{2,3},{3,2},{4,5},{5,4},{6,7},{7,6},{8,9},{9,8},{10,11... | collective-permute-start | bytes 4718600 | tf_op jit(solution)/shard_map/ppermute | solution.py:66
  179.3 46.1 %collective-permute-start.11 = (bf16[2048,384]{1,0:T(8,128)(2,1)S(1)}, bf16[2048,384]{1,0:T(8,128)(2,1)S(1)}, u32[]{:S(2)}, u32[]{:S(2)}) collective-permute-start(bf16[2048,384]{1,0:T(8,128)(2,1)S(1)} %pad_maximum_fusion.2), channel_id=1, source_target_pairs={{0,1},{1,0},{2,3},{3,2},{4,5},{5,4},{6,7},{7,6},{8,9},{9,8},{10,11... | collective-permute-start | bytes 4718600 | tf_op jit(solution)/shard_map/ppermute | solution.py:66
  184.3 17.6 %collective-permute-start.7 = (bf16[512,640]{1,0:T(8,128)(2,1)S(1)}, bf16[512,640]{1,0:T(8,128)(2,1)S(1)}, u32[]{:S(2)}, u32[]{:S(2)}) collective-permute-start(bf16[512,640]{1,0:T(8,128)(2,1)S(1)} %pad_maximum_fusion.10), channel_id=1, source_target_pairs={{0,2},{2,0},{1,3},{3,1},{4,6},{6,4},{5,7},{7,5},{8,10},{10,8},{9,1... | collective-permute-start | bytes 1966088 | tf_op jit(solution)/shard_map/ppermute | solution.py:13
  190.8 24.7 %collective-permute-start.22 = (bf16[512,640]{1,0:T(8,128)(2,1)S(1)}, bf16[512,640]{1,0:T(8,128)(2,1)S(1)}, u32[]{:S(2)}, u32[]{:S(2)}) collective-permute-start(bf16[512,640]{1,0:T(8,128)(2,1)S(1)} %pad_maximum_fusion.11), channel_id=1, source_target_pairs={{0,2},{2,0},{1,3},{3,1},{4,6},{6,4},{5,7},{7,5},{8,10},{10,8},{9,1... | collective-permute-start | bytes 1966088 | tf_op jit(solution)/shard_map/ppermute | solution.py:13
  215.9 3.4 %copy-start.5 = (bf16[512,640]{1,0:T(8,128)(2,1)}, bf16[512,640]{1,0:T(8,128)(2,1)S(1)}, u32[]{:S(2)}) copy-start(bf16[512,640]{1,0:T(8,128)(2,1)S(1)} %divide_convert_fusion.2) | copy-start | bytes 1966084
  221.9 24.7 %collective-permute-start.17 = (bf16[768,640]{1,0:T(8,128)(2,1)S(1)}, bf16[768,640]{1,0:T(8,128)(2,1)S(1)}, u32[]{:S(2)}, u32[]{:S(2)}) collective-permute-start(bf16[768,640]{1,0:T(8,128)(2,1)S(1)} %pad_maximum_fusion.7), channel_id=1, source_target_pairs={{0,2},{2,0},{1,3},{3,1},{4,6},{6,4},{5,7},{7,5},{8,10},{10,8},{9,1... | collective-permute-start | bytes 2949128 | tf_op jit(solution)/shard_map/ppermute | solution.py:13
  228.3 38.1 %collective-permute-start.12 = (bf16[768,640]{1,0:T(8,128)(2,1)S(1)}, bf16[768,640]{1,0:T(8,128)(2,1)S(1)}, u32[]{:S(2)}, u32[]{:S(2)}) collective-permute-start(bf16[768,640]{1,0:T(8,128)(2,1)S(1)} %pad_maximum_fusion.6), channel_id=1, source_target_pairs={{0,2},{2,0},{1,3},{3,1},{4,6},{6,4},{5,7},{7,5},{8,10},{10,8},{9,1... | collective-permute-start | bytes 2949128 | tf_op jit(solution)/shard_map/ppermute | solution.py:13
  (1 other events, 2.2 us)

commit v2 on v0

v2 whole, which is shorter than its diff:
```python
import functools

import jax
import jax.numpy as jnp
from jax import lax
from jax.experimental import pallas as pl
from jax.experimental.pallas import tpu as pltpu
from jax.sharding import PartitionSpec as P

ROUNDS = 2
LANES = 128
SWAP = [(0, 1), (1, 0)]
PAIRS = [(0, 1), (1, 0), (2, 3), (3, 2)]
SKIPS = [(0, 2), (2, 0), (1, 3), (3, 1)]
MIDDLE = [(1, 2), (2, 1)]
ENDS = [(0, 3), (3, 0)]
OUTWARD = [(1, 0), (2, 3)]
F32 = jnp.float32
BF16 = jnp.bfloat16


def column_chunks(width):
    cut = (width // (2 * LANES)) * LANES
    if width % LANES or not cut:
        return [(t, 0, width) for t in range(ROUNDS)]
    return [(0, 0, cut), (0, cut, width - cut), (1, 0, width - cut), (1, width - cut, cut)]


def pair_kernel(near_ref, far_ref, mine_ref, out_ref, acc_ref):
    k = pl.program_id(0)

    @pl.when(k == 0)
    def _():
        acc_ref[...] = jnp.zeros_like(acc_ref)

    def add(ref):
        acc_ref[...] += lax.dot_general(
            ref[...], mine_ref[...], (((0,), (0,)), ((), ())), preferred_element_type=F32
        )

    pl.when(k < 2)(lambda: add(near_ref))
    pl.when(k >= 2)(lambda: add(far_ref))

    @pl.when(k == 3)
    def _():
        out_ref[...] = acc_ref[...].astype(BF16)


def pair_sum(near, far, mine):
    rows, size = near.shape[0] // 2, near.shape[1]
    width = mine.shape[1]
    return pl.pallas_call(
        pair_kernel,
        grid=(4,),
        in_specs=[
            pl.BlockSpec((rows, size), lambda k: (jnp.minimum(k, 1), 0)),
            pl.BlockSpec((rows, size), lambda k: (jnp.maximum(k - 2, 0), 0)),
            pl.BlockSpec((rows, width), lambda k: (k, 0)),
        ],
        out_specs=pl.BlockSpec((size, width), lambda k: (0, 0)),
        out_shape=jax.ShapeDtypeStruct((size, width), BF16),
        scratch_shapes=[pltpu.VMEM((size, width), F32)],
        compiler_params=pltpu.CompilerParams(vmem_limit_bytes=24 << 20),
        cost_estimate=pl.CostEstimate(
            flops=8 * rows * size * width,
            bytes_accessed=8 * rows * (size + width) + 2 * size * width,
            transcendentals=0,
        ),
    )(near, far, mine)


def gamma_kernel(n_aux, last, order_ref, *refs):
    del order_ref
    n_in = 2 * (n_aux + 3) + 1 + (0 if last == "first" else 1)
    ins, out_ref, amp_ref = refs[:n_in], refs[n_in], refs[n_in + 1]
    base_ref = ins[0]
    halves = [ins[1 + h * (n_aux + 3) : 1 + (h + 1) * (n_aux + 3)] for h in range(2)]
    r = pl.program_id(0)
    blocks = pl.num_programs(0)

    @pl.when(r == 0)
    def _():
        for h, half in enumerate(halves):
            total = half[0][...].astype(F32)
            for other in half[1:n_aux]:
                total = total + other[...].astype(F32)
            amp_ref[h] = (total / (base_ref[...] - half[n_aux][...])).astype(BF16)

    def run(which):
        value = jnp.dot(halves[0][n_aux + 1 + which][...], amp_ref[0], preferred_element_type=F32)
        value += jnp.dot(halves[1][n_aux + 1 + which][...], amp_ref[1], preferred_element_type=F32)
        if last != "first":
            value += ins[-1][...]
        if last == "last":
            height, width = value.shape
            step = width // LANES
            for c in range(step):
                out_ref[pl.ds(c, height, stride=step), :] = value[:, c * LANES : (c + 1) * LANES]
        else:
            out_ref[...] = value

    pl.when(r < blocks // 2)(lambda: run(0))
    pl.when(r >= blocks // 2)(lambda: run(1))


def gamma_step(order, base, halves, acc, last):
    n_aux = len(halves[0]) - 3
    near = halves[0][-2]
    rows, size = near.shape[0] // 2, near.shape[1]
    width = base.shape[1]
    block = rows // 2
    full = lambda shape: pl.BlockSpec(shape, lambda r, order: (0, 0))
    specs, args = [full((1, width))], [base]
    for half in halves:
        specs += [full((size, width))] * n_aux + [full((size, 1))]
        specs += [
            pl.BlockSpec((block, size), lambda r, order: (jnp.minimum(r, 3), 0)),
            pl.BlockSpec((block, size), lambda r, order: (jnp.maximum(r - 4, 0), 0)),
        ]
        args += list(half)
    if acc is not None:
        specs.append(pl.BlockSpec((block, width), lambda r, order: (r, 0)))
        args.append(acc)
    if last:
        step = width // LANES
        out_shape = jax.ShapeDtypeStruct((4 * rows * step, LANES), F32)
        out_spec = pl.BlockSpec((block * step, LANES), lambda r, order: (order[r // 2] * 2 + r % 2, 0))
    else:
        out_shape = jax.ShapeDtypeStruct((4 * rows, width), F32)
        out_spec = pl.BlockSpec((block, width), lambda r, order: (r, 0))
    mode = "last" if last else ("first" if acc is None else "more")
    return pl.pallas_call(
        functools.partial(gamma_kernel, n_aux, mode),
        grid_spec=pltpu.PrefetchScalarGridSpec(
            num_scalar_prefetch=1,
            grid=(8,),
            in_specs=specs,
            out_specs=out_spec,
            scratch_shapes=[pltpu.VMEM((2, size, width), BF16)],
        ),
        out_shape=out_shape,
        compiler_params=pltpu.CompilerParams(vmem_limit_bytes=32 << 20),
        cost_estimate=pl.CostEstimate(
            flops=16 * rows * size * width,
            bytes_accessed=16 * rows * size + 4 * n_aux * size * width + 32 * rows * width,
            transcendentals=0,
        ),
    )(order, *args)


def shifted(part, axis, n):
    return [part] + [lax.ppermute(part, axis, [(k, (k + d) % n) for k in range(n)]) for d in range(1, n)]


def local_four(integrals, occ_energy, vir_energy, round_owner):
    n_aux = lax.axis_size("aux")
    me = lax.axis_index("occ")
    core = lax.axis_index("vir")
    by_orbital = lax.optimization_barrier(jnp.transpose(integrals[0], (1, 0, 2)))
    rows, width = by_orbital.shape[1:]
    is_mid = (me == 1) | (me == 2)
    orbital = lambda k: lax.dynamic_index_in_dim(by_orbital, k, 0, keepdims=False)

    b1 = lax.ppermute(orbital(me ^ 1), "occ", PAIRS)
    across = orbital(me ^ 3)
    b3_mid = lax.ppermute(across, "occ", MIDDLE)
    b2 = lax.ppermute(orbital(me ^ 2), "occ", SKIPS)
    own = [orbital(round_owner[t]) for t in range(ROUNDS)]
    near = [lax.ppermute(own[0], "occ", PAIRS)]
    b3_end = lax.ppermute(across, "occ", ENDS)
    near.append(lax.ppermute(own[1], "occ", PAIRS))
    mine = jnp.concatenate([orbital(me), b1, b2, jnp.where(is_mid, b3_mid, b3_end)], axis=0)

    energy_i = lax.dynamic_slice_in_dim(occ_energy, me, 1)
    energy_a = lax.dynamic_slice_in_dim(vir_energy, core * width, width)
    order = (jnp.arange(4, dtype=jnp.int32)) ^ me.astype(jnp.int32)
    chunks = column_chunks(width)
    acc = None
    for index, (turn, start, size) in enumerate(chunks):
        columns = slice(start, start + size)
        half = jnp.concatenate([own[turn][:, columns], near[turn][:, columns]], axis=0)
        half_swap = lax.ppermute(half, "vir", SWAP)
        mid = lax.ppermute(half, "occ", MIDDLE)
        end = lax.ppermute(mid, "occ", OUTWARD)
        turned = jnp.concatenate([mid[rows:], mid[:rows]], axis=0)
        far = jnp.where(is_mid, turned, end)
        far_swap = lax.ppermute(far, "vir", SWAP)
        energy_j = lax.dynamic_slice_in_dim(occ_energy, round_owner[turn], 1)
        base = (energy_i + energy_j - energy_a)[None, :]
        halves = []
        for which, blocks in ((core, (half, far)), (1 - core, (half_swap, far_swap))):
            energy_b = lax.dynamic_slice_in_dim(vir_energy, which * width + start, size)[:, None]
            part = pair_sum(*blocks, mine)
            halves.append((*shifted(part, "aux", n_aux), energy_b, *blocks))
        acc = gamma_step(order, base, halves, acc, index == len(chunks) - 1)
    return acc.reshape(4, rows, 1, width)


def local_any(integrals, occ_energy, vir_energy, round_owner):
    n_aux = lax.axis_size("aux")
    me = lax.axis_index("occ")
    core = lax.axis_index("vir")
    x = integrals[0]
    rows, n_occ, width = x.shape
    mine = lax.all_to_all(x, "occ", split_axis=1, concat_axis=0, tiled=True)[:, 0]
    energy_i = lax.dynamic_slice_in_dim(occ_energy, me, 1)
    energy_a = lax.dynamic_slice_in_dim(vir_energy, core * width, width)
    gamma = jnp.zeros(mine.shape, F32)
    for turn in range(ROUNDS):
        owner = round_owner[turn]
        own = lax.dynamic_index_in_dim(x, owner, 1, keepdims=False)
        whole = lax.all_gather(own, "occ", axis=0, tiled=True)
        other = lax.ppermute(whole, "vir", SWAP)
        energy_j = lax.dynamic_slice_in_dim(occ_energy, owner, 1)
        base = (energy_i + energy_j - energy_a)[None, :]
        for which, block in ((core, whole), (1 - core, other)):
            energy_b = lax.dynamic_slice_in_dim(vir_energy, which * width, width)[:, None]
            part = jnp.einsum("pb,pa->ba", block, mine, preferred_element_type=F32).astype(BF16)
            pair = sum(p.astype(F32) for p in shifted(part, "aux", n_aux))
            amplitude = (pair / (base - energy_b)).astype(BF16)
            gamma = gamma + jnp.dot(block, amplitude, preferred_element_type=F32)
    return gamma.reshape(-1, rows, 1, width)


def solution(mesh):
    placed = (P("occ", "aux", "grp", "vir"), P("grp"), P("grp"), P("grp"))
    local = local_four if mesh.shape["occ"] == 4 else local_any
    return jax.shard_map(
        local, mesh=mesh, in_specs=placed, out_specs=P("grp", "aux", "occ", "vir"), check_vma=False
    )
```

time: 433 us -> 279 us (0.64)
  waiting for transfers between devices: 354 us -> 146 us
  Pallas kernels: 0 us -> 47 us
  matrix products: 32.4 us -> 0 us
  starting transfers between devices: 6.57 us -> 38.9 us
  local copies, waits for them, and re-layouts: 15.1 us -> 29.8 us
  between operations: 20.9 us -> 7.2 us
  other arithmetic: 2.88 us -> 9.32 us
    psum x2 -> x0, waiting for transfers between devices: 271 us -> none  [the longest x1 188 us: from_root(): return lax.psum(jnp.where(mine, value, jnp.zeros_like(value)), axis)]
    ppermute x0 -> x30, waiting for transfers between devices: none -> 146 us  [the longest x4 108 us: local_four(): end = lax.ppermute(mid, 'occ', OUTWARD)]
    all_to_all x1 -> x0, waiting for transfers between devices: 57.4 us -> none  [local(): lax.all_to_all(integrals, 'occ', split_axis=2, concat_axis=0, tiled=True)]
    pallas_call x0 -> x12, Pallas kernels: none -> 47 us  [the longest x4 26.1 us: gamma_step(): pl.pallas_call(functools.partial(gamma_kernel, n_aux, mode), grid_spec=pl...]
    ppermute x0 -> x30, starting transfers between devices: none -> 38.9 us  [the longest x8 8.22 us: shifted(): lax.ppermute(part, axis, [(k, (k + d) % n) for k in range(n)])]
    dot_general x4 -> x0, matrix products: 32.4 us -> none  [the longest x2 16.5 us: local(): jnp.einsum('ijab,srjb->sria', amplitude, owner_whole, preferred_element_t...]
    all_gather x2 -> x0, waiting for transfers between devices: 24.8 us -> none  [local(): owner_whole = lax.all_gather(owner_half, 'vir', axis=3, tiled=True)]
    broadcast_in_dim x0 -> x10, local copies, waits for them, and re-layouts: none -> 10.4 us  [the longest x8 10.4 us: local_four(): lax.dynamic_slice_in_dim(vir_energy, which * width + start, size)[:, None]]
  transfers between devices with their start and end apart: 5 -> 30, of which waited for: 5 -> 10; matrix products, arithmetic and copies ran while one was open for 2% -> 11% of each run, Pallas kernels for 0% -> 15%
where the time goes in v2:
time: 279 us; the launch traced here: 278 us
  waiting for transfers between devices  146 us (52%)
  Pallas kernels  47 us (17%)
  starting transfers between devices  38.9 us (14%)
  local copies, waits for them, and re-layouts  29.8 us (11%)
  other arithmetic  9.32 us (3%)
  between operations  7.2 us (3%)
    ppermute x4, waiting for transfers between devices, local_four(): end = lax.ppermute(mid, 'occ', OUTWARD)  108 us
    pallas_call x4, Pallas kernels, gamma_step(): pl.pallas_call(functools.partial(gamma_kernel, n_aux, mode), grid_spec=pl...  26.1 us
    pallas_call x8, Pallas kernels, pair_sum(): pl.pallas_call(pair_kernel, grid=(4,), in_specs=[pl.BlockSpec((rows, size...  20.9 us
    ppermute x8, waiting for transfers between devices, shifted(): lax.ppermute(part, axis, [(k, (k + d) % n) for k in range(n)])  15.9 us
    broadcast_in_dim x8, local copies, waits for them, and re-layouts, local_four(): lax.dynamic_slice_in_dim(vir_energy, which * width + start, size)[:, None]  10.4 us
    ppermute x1, waiting for transfers between devices, local_four(): near.append(lax.ppermute(own[1], 'occ', PAIRS))  10.4 us
    ppermute x1, waiting for transfers between devices, local_four(): b3_end = lax.ppermute(across, 'occ', ENDS)  10.1 us
    ppermute x8, starting transfers between devices, shifted(): lax.ppermute(part, axis, [(k, (k + d) % n) for k in range(n)])  8.22 us
  transfers between devices with their start and end apart: 30, of which 10 were waited for; matrix products, arithmetic and copies ran while one was open for 11% of the time, Pallas kernels for 15%

profile of v2, /device:TPU:0, one launch (start us, length us, event | category | flops | bytes accessed | tf_op | source)
XLA Modules:
  0.0 278.4 jit_solution(1698886742713006314)
XLA Ops:
  3.9 2.1 copy.17
  7.3 1.8 dynamic-slice_bitcast_fusion
  9.1 3.0 %collective-permute-start.17 = (bf16[512,640]{1,0:T(8,128)(2,1)}, bf16[512,640]{1,0:T(8,128)(2,1)S(1)}, u32[]{:S(2)}, u32[]{:S(2)}) collective-permute-start(bf16[512,640]{1,0:T(8,128)(2,1)} %get-tuple-element.5), channel_id=1, source_target_pairs={{0,4},{4,0},{8,12},{12,8},{1,5},{5,1},{9,13},{13,9},{2,6},{6,2},{1... | collective-permute-start | bytes 1966088 | tf_op jit(solution)/shard_map/ppermute | solution.py:169
  12.1 1.5 collective-permute-start.5
  13.6 5.9 %collective-permute-start.6 = (bf16[512,640]{1,0:T(8,128)(2,1)}, bf16[512,640]{1,0:T(8,128)(2,1)}, u32[]{:S(2)}, u32[]{:S(2)}) collective-permute-start(bf16[512,640]{1,0:T(8,128)(2,1)} %get-tuple-element.6), channel_id=1, source_target_pairs={{0,12},{12,0},{1,13},{13,1},{2,14},{14,2},{3,15},{15,3},{16,28},{2... | collective-permute-start | bytes 1966088 | tf_op jit(solution)/shard_map/ppermute | solution.py:170
  25.6 2.2 collective-permute-done.17
  27.9 1.5 collective-permute-start.24
  29.6 1.5 collective-permute-start.18
  31.1 10.4 %collective-permute-done = bf16[512,640]{1,0:T(8,128)(2,1)} collective-permute-done((bf16[512,640]{1,0:T(8,128)(2,1)S(1)}, bf16[512,640]{1,0:T(8,128)(2,1)}, u32[]{:S(2)}, u32[]{:S(2)}) %collective-permute-start) | collective-permute-done | bytes 655392 | tf_op jit(solution)/shard_map/ppermute | solution.py:171
  47.4 10.1 %collective-permute-done.6 = bf16[512,640]{1,0:T(8,128)(2,1)} collective-permute-done((bf16[512,640]{1,0:T(8,128)(2,1)}, bf16[512,640]{1,0:T(8,128)(2,1)}, u32[]{:S(2)}, u32[]{:S(2)}) %collective-permute-start.6) | collective-permute-done | bytes 655392 | tf_op jit(solution)/shard_map/ppermute | solution.py:170
  58.7 8.0 %collective-permute-start.4 = (bf16[512,640]{1,0:T(8,128)(2,1)S(1)}, bf16[512,640]{1,0:T(8,128)(2,1)S(1)}, u32[]{:S(2)}, u32[]{:S(2)}) collective-permute-start(bf16[512,640]{1,0:T(8,128)(2,1)S(1)} %copy-done.44), channel_id=1, source_target_pairs={{0,8},{8,0},{4,12},{12,4},{1,9},{9,1},{5,13},{13,5},{2,10},{10,2},... | collective-permute-start | bytes 1966088 | tf_op jit(solution)/shard_map/ppermute | solution.py:167
  74.1 67.5 %collective-permute-done.25 = bf16[1024,256]{1,0:T(8,128)(2,1)S(1)} collective-permute-done((bf16[1024,256]{1,0:T(8,128)(2,1)}, bf16[1024,256]{1,0:T(8,128)(2,1)S(1)}, u32[]{:S(2)}, u32[]{:S(2)}) %collective-permute-start.25) | collective-permute-done | bytes 524320 | tf_op jit(solution)/shard_map/ppermute | solution.py:184
  142.4 16.0 %collective-permute-done.19 = bf16[1024,384]{1,0:T(8,128)(2,1)S(1)} collective-permute-done((bf16[1024,384]{1,0:T(8,128)(2,1)}, bf16[1024,384]{1,0:T(8,128)(2,1)S(1)}, u32[]{:S(2)}, u32[]{:S(2)}) %collective-permute-start.19) | collective-permute-done | bytes 786464 | tf_op jit(solution)/shard_map/ppermute | solution.py:184
  159.9 15.3 %collective-permute-done.12 = bf16[1024,384]{1,0:T(8,128)(2,1)S(1)} collective-permute-done((bf16[1024,384]{1,0:T(8,128)(2,1)S(1)}, bf16[1024,384]{1,0:T(8,128)(2,1)S(1)}, u32[]{:S(2)}, u32[]{:S(2)}) %collective-permute-start.12) | collective-permute-done | bytes 786464 | tf_op jit(solution)/shard_map/ppermute | solution.py:184
  176.1 8.7 %collective-permute-done.2 = bf16[1024,256]{1,0:T(8,128)(2,1)S(1)} collective-permute-done((bf16[1024,256]{1,0:T(8,128)(2,1)}, bf16[1024,256]{1,0:T(8,128)(2,1)S(1)}, u32[]{:S(2)}, u32[]{:S(2)}) %collective-permute-start.2) | collective-permute-done | bytes 524320 | tf_op jit(solution)/shard_map/ppermute | solution.py:184
  186.4 6.3 %pad_maximum_fusion.mine_ref = bf16[2048,640]{1,0:T(8,128)(2,1)S(1)} fusion(bf16[512,640]{1,0:T(8,128)(2,1)S(1)} %broadcast_select_fusion, bf16[512,640]{1,0:T(8,128)(2,1)S(1)} %collective-permute-done.4, bf16[512,640]{1,0:T(8,128)(2,1)S(1)} %collective-permute-done.3, bf16[512,640]{1,0:T(8,128)(2,1)S(1)} %copy-done.43), kind=kLoop, calls=%fused_computation | loop fusion | flops 10485760 | bytes 5242880 | tf_op jit(solution)/shard_map/concatenate | solution.py:172
  192.7 1.8 shard_map.52.refs_1_
  194.6 3.0 %shard_map.50.refs_1_ = bf16[384,640]{1,0:T(8,128)(2,1)} custom-call(bf16[1024,384]{1,0:T(8,128)(2,1)S(1)} %copy-done.3, bf16[1024,384]{1,0:T(8,128)(2,1)S(1)} %maximum_select_fusion.1.far_ref.refs_5_, bf16[2048,640]{1,0:T(8,128)(2,1)S(1)} %pad_maximum_fusion.mine_ref), custom_call_target="tpu_custom_call" | custom-call | flops 1006632960 | bytes 4685824 | tf_op jit(solution)/shard_map/pallas_call | solution.py:52
  199.1 4.0 %shard_map.48.refs_1_ = bf16[384,640]{1,0:T(8,128)(2,1)} custom-call(bf16[1024,384]{1,0:T(8,128)(2,1)} %pad_maximum_fusion.1.near_ref.refs_4_, bf16[1024,384]{1,0:T(8,128)(2,1)S(1)} %maximum_select_fusion.far_ref.refs_5_, bf16[2048,640]{1,0:T(8,128)(2,1)S(1)} %pad_maximum_fusion.mine_ref), custom_call_target="tpu_custom_call" | custom-call | flops 1006632960 | bytes 4685824 | tf_op jit(solution)/shard_map/pallas_call | solution.py:52
  203.1 3.0 %shard_map.51.refs_6_ = bf16[384,640]{1,0:T(8,128)(2,1)} custom-call(bf16[1024,384]{1,0:T(8,128)(2,1)S(1)} %collective-permute-done.21.near_ref.refs_9_, bf16[1024,384]{1,0:T(8,128)(2,1)S(1)} %collective-permute-done.22.far_ref.refs_10_, bf16[2048,640]{1,0:T(8,128)(2,1)S(1)} %pad_maximum_fusion.mine_ref), custom_call_target="tpu_custom_call" | custom-call | flops 1006632960 | bytes 4685824 | tf_op jit(solution)/shard_map/pallas_call | solution.py:52
  208.2 2.5 shard_map.53.refs_6_
  211.2 3.0 %shard_map.49.refs_6_ = bf16[384,640]{1,0:T(8,128)(2,1)} custom-call(bf16[1024,384]{1,0:T(8,128)(2,1)S(1)} %collective-permute-done.14.near_ref.refs_9_, bf16[1024,384]{1,0:T(8,128)(2,1)S(1)} %collective-permute-done.15.far_ref.refs_10_, bf16[2048,640]{1,0:T(8,128)(2,1)S(1)} %pad_maximum_fusion.mine_ref), custom_call_target="tpu_custom_call" | custom-call | flops 1006632960 | bytes 4685824 | tf_op jit(solution)/shard_map/pallas_call | solution.py:52
  230.4 1.7 shard_map.46.refs_1_
  232.2 1.8 shard_map.47.refs_6_
  234.0 4.1 %collective-permute-done.29.refs_7_ = bf16[256,640]{1,0:T(8,128)(2,1)} collective-permute-done((bf16[256,640]{1,0:T(8,128)(2,1)}, bf16[256,640]{1,0:T(8,128)(2,1)}, u32[]{:S(2)}, u32[]{:S(2)}) %collective-permute-start.29) | collective-permute-done | bytes 327712 | tf_op jit(solution)/shard_map/ppermute | solution.py:152
  238.7 5.1 %shard_map.54.refs_11_ = f32[2048,640]{1,0:T(8,128)S(1)} custom-call(s32[4]{0:T(128)S(1)} %iota_xor_fusion.order_ref, f32[1,640]{1,0:T(1,128)S(1)} %broadcast_in_dim.37.refs_0_, bf16[256,640]{1,0:T(8,128)(2,1)S(1)} %copy-done.33, bf16[256,640]{1,0:T(8,128)(2,1)S(1)} %copy-done.42, f32[256,1]{1,0:T(8,128)S(1)} %copy.7.refs_3_, ...), custom_call_target="tpu_custom_call" | custom-call | flops 1342177280 | bytes 13893632 | tf_op jit(solution)/shard_map/pallas_call | solution.py:132
  243.9 1.6 collective-permute-start.10
  245.5 7.3 %shard_map.55.refs_11_ = f32[2048,640]{1,0:T(8,128)S(1)} custom-call(s32[4]{0:T(128)S(1)} %iota_xor_fusion.order_ref, f32[1,640]{1,0:T(1,128)S(1)} %broadcast_in_dim.37.refs_0_, bf16[384,640]{1,0:T(8,128)(2,1)} %shard_map.50.refs_1_, bf16[384,640]{1,0:T(8,128)(2,1)} %collective-permute-done.20.refs_2_, f32[384,1]{1,0:T(8,128)S(1)} %copy-done.36, ...), custom_call_target="tpu_custom_call" | custom-call | flops 2013265920 | bytes 15597568 | tf_op jit(solution)/shard_map/pallas_call | solution.py:132
  252.8 6.4 %collective-permute-done.16.refs_7_ = bf16[384,640]{1,0:T(8,128)(2,1)} collective-permute-done((bf16[384,640]{1,0:T(8,128)(2,1)}, bf16[384,640]{1,0:T(8,128)(2,1)}, u32[]{:S(2)}, u32[]{:S(2)}) %collective-permute-start.16) | collective-permute-done | bytes 491552 | tf_op jit(solution)/shard_map/ppermute | solution.py:152
  259.2 7.6 %shard_map.56.refs_11_ = f32[2048,640]{1,0:T(8,128)S(1)} custom-call(s32[4]{0:T(128)S(1)} %iota_xor_fusion.order_ref, f32[1,640]{1,0:T(1,128)S(1)} %broadcast_in_dim.32.refs_0_, bf16[384,640]{1,0:T(8,128)(2,1)} %shard_map.48.refs_1_, bf16[384,640]{1,0:T(8,128)(2,1)} %collective-permute-done.13.refs_2_, f32[384,1]{1,0:T(8,128)S(1)} %copy-done.34, ...), custom_call_target="tpu_custom_call" | custom-call | flops 2013265920 | bytes 15597568 | tf_op jit(solution)/shard_map/pallas_call | solution.py:132
  266.8 5.4 %collective-permute-done.10.refs_7_ = bf16[256,640]{1,0:T(8,128)(2,1)S(1)} collective-permute-done((bf16[256,640]{1,0:T(8,128)(2,1)S(1)}, bf16[256,640]{1,0:T(8,128)(2,1)S(1)}, u32[]{:S(2)}, u32[]{:S(2)}) %collective-permute-start.10) | collective-permute-done | bytes 327712 | tf_op jit(solution)/shard_map/ppermute | solution.py:152
  272.2 6.2 %shard_map.57 = f32[10240,128]{1,0:T(8,128)} custom-call(s32[4]{0:T(128)S(1)} %iota_xor_fusion.order_ref, f32[1,640]{1,0:T(1,128)S(1)} %broadcast_in_dim.32.refs_0_, bf16[256,640]{1,0:T(8,128)(2,1)S(1)} %shard_map.46.refs_1_, bf16[256,640]{1,0:T(8,128)(2,1)S(1)} %collective-permute-done.7.refs_2_, f32[256,1]{1,0:T(8,128)S(1)} %copy-done.39, ...), custom_call_target="tpu_custom_call" | custom-call | flops 1342177280 | bytes 13893632 | tf_op jit(solution)/shard_map/pallas_call | solution.py:132
  (176 shorter events, 44.9 us)
Async XLA Ops:
  9.1 18.8 %collective-permute-start.17 = (bf16[512,640]{1,0:T(8,128)(2,1)}, bf16[512,640]{1,0:T(8,128)(2,1)S(1)}, u32[]{:S(2)}, u32[]{:S(2)}) collective-permute-start(bf16[512,640]{1,0:T(8,128)(2,1)} %get-tuple-element.5), channel_id=1, source_target_pairs={{0,4},{4,0},{8,12},{12,8},{1,5},{5,1},{9,13},{13,9},{2,6},{6,2},{1... | collective-permute-start | bytes 1966088 | tf_op jit(solution)/shard_map/ppermute | solution.py:169
  12.1 29.4 %collective-permute-start = (bf16[512,640]{1,0:T(8,128)(2,1)S(1)}, bf16[512,640]{1,0:T(8,128)(2,1)}, u32[]{:S(2)}, u32[]{:S(2)}) collective-permute-start(bf16[512,640]{1,0:T(8,128)(2,1)S(1)} %get-tuple-element.10), channel_id=1, source_target_pairs={{0,4},{4,0},{8,12},{12,8},{1,5},{5,1},{9,13},{13,9},{2,6},{6,2},{1... | collective-permute-start | bytes 1966088 | tf_op jit(solution)/shard_map/ppermute | solution.py:171
  12.1 33.1 %collective-permute-start.5 = (bf16[512,640]{1,0:T(8,128)(2,1)}, bf16[512,640]{1,0:T(8,128)(2,1)}, u32[]{:S(2)}, u32[]{:S(2)}) collective-permute-start(bf16[512,640]{1,0:T(8,128)(2,1)} %get-tuple-element.6), channel_id=1, source_target_pairs={{4,8},{8,4},{5,9},{9,5},{6,10},{10,6},{7,11},{11,7},{20,24},{24,20... | collective-permute-start | bytes 1966088 | tf_op jit(solution)/shard_map/ppermute | solution.py:166
  13.6 43.9 %collective-permute-start.6 = (bf16[512,640]{1,0:T(8,128)(2,1)}, bf16[512,640]{1,0:T(8,128)(2,1)}, u32[]{:S(2)}, u32[]{:S(2)}) collective-permute-start(bf16[512,640]{1,0:T(8,128)(2,1)} %get-tuple-element.6), channel_id=1, source_target_pairs={{0,12},{12,0},{1,13},{13,1},{2,14},{14,2},{3,15},{15,3},{16,28},{2... | collective-permute-start | bytes 1966088 | tf_op jit(solution)/shard_map/ppermute | solution.py:170
  27.9 113.8 %copy-start.8 = (bf16[1024,256]{1,0:T(8,128)(2,1)}, bf16[1024,256]{1,0:T(8,128)(2,1)S(1)}, u32[]{:S(2)}) copy-start(bf16[1024,256]{1,0:T(8,128)(2,1)S(1)} %pad_maximum_fusion.4.near_ref.refs_4_) | copy-start | bytes 1572868
  27.9 30.8 %collective-permute-start.24 = (bf16[1024,256]{1,0:T(8,128)(2,1)S(1)}, bf16[1024,256]{1,0:T(8,128)(2,1)}, u32[]{:S(2)}, u32[]{:S(2)}) collective-permute-start(bf16[1024,256]{1,0:T(8,128)(2,1)S(1)} %pad_maximum_fusion.4.near_ref.refs_4_), channel_id=1, source_target_pairs={{4,8},{8,4},{5,9},{9,5},{6,10},{10,6},{7,11},{11,7},{20,24},{24,20... | collective-permute-start | bytes 1572872 | tf_op jit(solution)/shard_map/ppermute | solution.py:183
  29.6 112.0 %copy-start.2 = (bf16[1024,384]{1,0:T(8,128)(2,1)}, bf16[1024,384]{1,0:T(8,128)(2,1)S(1)}, u32[]{:S(2)}) copy-start(bf16[1024,384]{1,0:T(8,128)(2,1)S(1)} %pad_maximum_fusion.2.near_ref.refs_4_) | copy-start | bytes 2359300
  29.6 39.5 %collective-permute-start.18 = (bf16[1024,384]{1,0:T(8,128)(2,1)S(1)}, bf16[1024,384]{1,0:T(8,128)(2,1)}, u32[]{:S(2)}, u32[]{:S(2)}) collective-permute-start(bf16[1024,384]{1,0:T(8,128)(2,1)S(1)} %pad_maximum_fusion.2.near_ref.refs_4_), channel_id=1, source_target_pairs={{4,8},{8,4},{5,9},{9,5},{6,10},{10,6},{7,11},{11,7},{20,24},{24,20... | collective-permute-start | bytes 2359304 | tf_op jit(solution)/shard_map/ppermute | solution.py:183
  43.5 28.0 %collective-permute-start.11 = (bf16[1024,384]{1,0:T(8,128)(2,1)}, bf16[1024,384]{1,0:T(8,128)(2,1)S(1)}, u32[]{:S(2)}, u32[]{:S(2)}) collective-permute-start(bf16[1024,384]{1,0:T(8,128)(2,1)} %pad_maximum_fusion.1.near_ref.refs_4_), channel_id=1, source_target_pairs={{4,8},{8,4},{5,9},{9,5},{6,10},{10,6},{7,11},{11,7},{20,24},{24,20... | collective-permute-start | bytes 2359304 | tf_op jit(solution)/shard_map/ppermute | solution.py:183
  45.2 22.6 %collective-permute-start.1 = (bf16[1024,256]{1,0:T(8,128)(2,1)S(1)}, bf16[1024,256]{1,0:T(8,128)(2,1)}, u32[]{:S(2)}, u32[]{:S(2)}) collective-permute-start(bf16[1024,256]{1,0:T(8,128)(2,1)S(1)} %pad_maximum_fusion.3.near_ref.refs_4_), channel_id=1, source_target_pairs={{4,8},{8,4},{5,9},{9,5},{6,10},{10,6},{7,11},{11,7},{20,24},{24,20... | collective-permute-start | bytes 1572872 | tf_op jit(solution)/shard_map/ppermute | solution.py:183
  57.5 84.2 %collective-permute-start.3 = (bf16[512,640]{1,0:T(8,128)(2,1)}, bf16[512,640]{1,0:T(8,128)(2,1)S(1)}, u32[]{:S(2)}, u32[]{:S(2)}) collective-permute-start(bf16[512,640]{1,0:T(8,128)(2,1)} %get-tuple-element.8), channel_id=1, source_target_pairs={{0,4},{4,0},{8,12},{12,8},{1,5},{5,1},{9,13},{13,9},{2,6},{6,2},{1... | collective-permute-start | bytes 1966088 | tf_op jit(solution)/shard_map/ppermute | solution.py:164
  58.7 83.6 %collective-permute-start.4 = (bf16[512,640]{1,0:T(8,128)(2,1)S(1)}, bf16[512,640]{1,0:T(8,128)(2,1)S(1)}, u32[]{:S(2)}, u32[]{:S(2)}) collective-permute-start(bf16[512,640]{1,0:T(8,128)(2,1)S(1)} %copy-done.44), channel_id=1, source_target_pairs={{0,8},{8,0},{4,12},{12,4},{1,9},{9,1},{5,13},{13,5},{2,10},{10,2},... | collective-permute-start | bytes 1966088 | tf_op jit(solution)/shard_map/ppermute | solution.py:167
  67.8 73.7 %collective-permute-start.25 = (bf16[1024,256]{1,0:T(8,128)(2,1)}, bf16[1024,256]{1,0:T(8,128)(2,1)S(1)}, u32[]{:S(2)}, u32[]{:S(2)}) collective-permute-start(bf16[1024,256]{1,0:T(8,128)(2,1)} %collective-permute-done.24), channel_id=1, source_target_pairs={{4,0},{8,12},{5,1},{9,13},{6,2},{10,14},{7,3},{11,15},{20,16},{24,... | collective-permute-start | bytes 1572872 | tf_op jit(solution)/shard_map/ppermute | solution.py:184
  69.1 89.3 %collective-permute-start.19 = (bf16[1024,384]{1,0:T(8,128)(2,1)}, bf16[1024,384]{1,0:T(8,128)(2,1)S(1)}, u32[]{:S(2)}, u32[]{:S(2)}) collective-permute-start(bf16[1024,384]{1,0:T(8,128)(2,1)} %collective-permute-done.18), channel_id=1, source_target_pairs={{4,0},{8,12},{5,1},{9,13},{6,2},{10,14},{7,3},{11,15},{20,16},{24,... | collective-permute-start | bytes 2359304 | tf_op jit(solution)/shard_map/ppermute | solution.py:184
  71.5 103.8 %collective-permute-start.12 = (bf16[1024,384]{1,0:T(8,128)(2,1)S(1)}, bf16[1024,384]{1,0:T(8,128)(2,1)S(1)}, u32[]{:S(2)}, u32[]{:S(2)}) collective-permute-start(bf16[1024,384]{1,0:T(8,128)(2,1)S(1)} %collective-permute-done.11), channel_id=1, source_target_pairs={{4,0},{8,12},{5,1},{9,13},{6,2},{10,14},{7,3},{11,15},{20,16},{24,... | collective-permute-start | bytes 2359304 | tf_op jit(solution)/shard_map/ppermute | solution.py:184
  141.6 44.8 %collective-permute-start.21 = (bf16[1024,384]{1,0:T(8,128)(2,1)S(1)}, bf16[1024,384]{1,0:T(8,128)(2,1)S(1)}, u32[]{:S(2)}, u32[]{:S(2)}) collective-permute-start(bf16[1024,384]{1,0:T(8,128)(2,1)S(1)} %pad_maximum_fusion.2.near_ref.refs_4_), channel_id=1, source_target_pairs={{0,1},{1,0},{2,3},{3,2},{4,5},{5,4},{6,7},{7,6},{8,9},{9,8},{10,11... | collective-permute-start | bytes 2359304 | tf_op jit(solution)/shard_map/ppermute | solution.py:182
  141.7 33.8 %collective-permute-start.27 = (bf16[1024,256]{1,0:T(8,128)(2,1)S(1)}, bf16[1024,256]{1,0:T(8,128)(2,1)S(1)}, u32[]{:S(2)}, u32[]{:S(2)}) collective-permute-start(bf16[1024,256]{1,0:T(8,128)(2,1)S(1)} %pad_maximum_fusion.4.near_ref.refs_4_), channel_id=1, source_target_pairs={{0,1},{1,0},{2,3},{3,2},{4,5},{5,4},{6,7},{7,6},{8,9},{9,8},{10,11... | collective-permute-start | bytes 1572872 | tf_op jit(solution)/shard_map/ppermute | solution.py:182
  142.3 42.6 %collective-permute-start.8 = (bf16[1024,256]{1,0:T(8,128)(2,1)S(1)}, bf16[1024,256]{1,0:T(8,128)(2,1)S(1)}, u32[]{:S(2)}, u32[]{:S(2)}) collective-permute-start(bf16[1024,256]{1,0:T(8,128)(2,1)S(1)} %pad_maximum_fusion.3.near_ref.refs_4_), channel_id=1, source_target_pairs={{0,1},{1,0},{2,3},{3,2},{4,5},{5,4},{6,7},{7,6},{8,9},{9,8},{10,11... | collective-permute-start | bytes 1572872 | tf_op jit(solution)/shard_map/ppermute | solution.py:182
  158.4 26.4 %collective-permute-start.2 = (bf16[1024,256]{1,0:T(8,128)(2,1)}, bf16[1024,256]{1,0:T(8,128)(2,1)S(1)}, u32[]{:S(2)}, u32[]{:S(2)}) collective-permute-start(bf16[1024,256]{1,0:T(8,128)(2,1)} %collective-permute-done.1), channel_id=1, source_target_pairs={{4,0},{8,12},{5,1},{9,13},{6,2},{10,14},{7,3},{11,15},{20,16},{24,... | collective-permute-start | bytes 1572872 | tf_op jit(solution)/shard_map/ppermute | solution.py:184
  175.3 22.3 %collective-permute-start.22 = (bf16[1024,384]{1,0:T(8,128)(2,1)S(1)}, bf16[1024,384]{1,0:T(8,128)(2,1)S(1)}, u32[]{:S(2)}, u32[]{:S(2)}) collective-permute-start(bf16[1024,384]{1,0:T(8,128)(2,1)S(1)} %maximum_select_fusion.1.far_ref.refs_5_), channel_id=1, source_target_pairs={{0,1},{1,0},{2,3},{3,2},{4,5},{5,4},{6,7},{7,6},{8,9},{9,8},{10,11... | collective-permute-start | bytes 2359304 | tf_op jit(solution)/shard_map/ppermute | solution.py:187
  175.5 30.6 %collective-permute-start.14 = (bf16[1024,384]{1,0:T(8,128)(2,1)}, bf16[1024,384]{1,0:T(8,128)(2,1)S(1)}, u32[]{:S(2)}, u32[]{:S(2)}) collective-permute-start(bf16[1024,384]{1,0:T(8,128)(2,1)} %pad_maximum_fusion.1.near_ref.refs_4_), channel_id=1, source_target_pairs={{0,1},{1,0},{2,3},{3,2},{4,5},{5,4},{6,7},{7,6},{8,9},{9,8},{10,11... | collective-permute-start | bytes 2359304 | tf_op jit(solution)/shard_map/ppermute | solution.py:182
  184.8 25.9 %collective-permute-start.15 = (bf16[1024,384]{1,0:T(8,128)(2,1)S(1)}, bf16[1024,384]{1,0:T(8,128)(2,1)S(1)}, u32[]{:S(2)}, u32[]{:S(2)}) collective-permute-start(bf16[1024,384]{1,0:T(8,128)(2,1)S(1)} %maximum_select_fusion.far_ref.refs_5_), channel_id=1, source_target_pairs={{0,1},{1,0},{2,3},{3,2},{4,5},{5,4},{6,7},{7,6},{8,9},{9,8},{10,11... | collective-permute-start | bytes 2359304 | tf_op jit(solution)/shard_map/ppermute | solution.py:187
  185.8 20.9 %collective-permute-start.28 = (bf16[1024,256]{1,0:T(8,128)(2,1)S(1)}, bf16[1024,256]{1,0:T(8,128)(2,1)S(1)}, u32[]{:S(2)}, u32[]{:S(2)}) collective-permute-start(bf16[1024,256]{1,0:T(8,128)(2,1)S(1)} %maximum_select_fusion.3.far_ref.refs_5_), channel_id=1, source_target_pairs={{0,1},{1,0},{2,3},{3,2},{4,5},{5,4},{6,7},{7,6},{8,9},{9,8},{10,11... | collective-permute-start | bytes 1572872 | tf_op jit(solution)/shard_map/ppermute | solution.py:187
  186.3 30.2 %collective-permute-start.9 = (bf16[1024,256]{1,0:T(8,128)(2,1)S(1)}, bf16[1024,256]{1,0:T(8,128)(2,1)S(1)}, u32[]{:S(2)}, u32[]{:S(2)}) collective-permute-start(bf16[1024,256]{1,0:T(8,128)(2,1)S(1)} %maximum_select_fusion.2.far_ref.refs_5_), channel_id=1, source_target_pairs={{0,1},{1,0},{2,3},{3,2},{4,5},{5,4},{6,7},{7,6},{8,9},{9,8},{10,11... | collective-permute-start | bytes 1572872 | tf_op jit(solution)/shard_map/ppermute | solution.py:187
  197.6 16.7 %collective-permute-start.26 = (bf16[256,640]{1,0:T(8,128)(2,1)S(1)}, bf16[256,640]{1,0:T(8,128)(2,1)S(1)}, u32[]{:S(2)}, u32[]{:S(2)}) collective-permute-start(bf16[256,640]{1,0:T(8,128)(2,1)S(1)} %shard_map.52.refs_1_), channel_id=1, source_target_pairs={{0,2},{2,0},{1,3},{3,1},{4,6},{6,4},{5,7},{7,5},{8,10},{10,8},{9,1... | collective-permute-start | bytes 983048 | tf_op jit(solution)/shard_map/ppermute | solution.py:152
  206.1 37.7 %collective-permute-start.20 = (bf16[384,640]{1,0:T(8,128)(2,1)}, bf16[384,640]{1,0:T(8,128)(2,1)}, u32[]{:S(2)}, u32[]{:S(2)}) collective-permute-start(bf16[384,640]{1,0:T(8,128)(2,1)} %shard_map.50.refs_1_), channel_id=1, source_target_pairs={{0,2},{2,0},{1,3},{3,1},{4,6},{6,4},{5,7},{7,5},{8,10},{10,8},{9,1... | collective-permute-start | bytes 1474568 | tf_op jit(solution)/shard_map/ppermute | solution.py:152
  206.7 38.7 %collective-permute-start.23 = (bf16[384,640]{1,0:T(8,128)(2,1)}, bf16[384,640]{1,0:T(8,128)(2,1)}, u32[]{:S(2)}, u32[]{:S(2)}) collective-permute-start(bf16[384,640]{1,0:T(8,128)(2,1)} %shard_map.51.refs_6_), channel_id=1, source_target_pairs={{0,2},{2,0},{1,3},{3,1},{4,6},{6,4},{5,7},{7,5},{8,10},{10,8},{9,1... | collective-permute-start | bytes 1474568 | tf_op jit(solution)/shard_map/ppermute | solution.py:152
  210.7 27.4 %collective-permute-start.29 = (bf16[256,640]{1,0:T(8,128)(2,1)}, bf16[256,640]{1,0:T(8,128)(2,1)}, u32[]{:S(2)}, u32[]{:S(2)}) collective-permute-start(bf16[256,640]{1,0:T(8,128)(2,1)} %shard_map.53.refs_6_), channel_id=1, source_target_pairs={{0,2},{2,0},{1,3},{3,1},{4,6},{6,4},{5,7},{7,5},{8,10},{10,8},{9,1... | collective-permute-start | bytes 983048 | tf_op jit(solution)/shard_map/ppermute | solution.py:152
  215.0 37.8 %collective-permute-start.13 = (bf16[384,640]{1,0:T(8,128)(2,1)}, bf16[384,640]{1,0:T(8,128)(2,1)}, u32[]{:S(2)}, u32[]{:S(2)}) collective-permute-start(bf16[384,640]{1,0:T(8,128)(2,1)} %shard_map.48.refs_1_), channel_id=1, source_target_pairs={{0,2},{2,0},{1,3},{3,1},{4,6},{6,4},{5,7},{7,5},{8,10},{10,8},{9,1... | collective-permute-start | bytes 1474568 | tf_op jit(solution)/shard_map/ppermute | solution.py:152
  217.3 41.9 %collective-permute-start.16 = (bf16[384,640]{1,0:T(8,128)(2,1)}, bf16[384,640]{1,0:T(8,128)(2,1)}, u32[]{:S(2)}, u32[]{:S(2)}) collective-permute-start(bf16[384,640]{1,0:T(8,128)(2,1)} %shard_map.49.refs_6_), channel_id=1, source_target_pairs={{0,2},{2,0},{1,3},{3,1},{4,6},{6,4},{5,7},{7,5},{8,10},{10,8},{9,1... | collective-permute-start | bytes 1474568 | tf_op jit(solution)/shard_map/ppermute | solution.py:152
  238.1 28.7 %collective-permute-start.7 = (bf16[256,640]{1,0:T(8,128)(2,1)S(1)}, bf16[256,640]{1,0:T(8,128)(2,1)S(1)}, u32[]{:S(2)}, u32[]{:S(2)}) collective-permute-start(bf16[256,640]{1,0:T(8,128)(2,1)S(1)} %shard_map.46.refs_1_), channel_id=1, source_target_pairs={{0,2},{2,0},{1,3},{3,1},{4,6},{6,4},{5,7},{7,5},{8,10},{10,8},{9,1... | collective-permute-start | bytes 983048 | tf_op jit(solution)/shard_map/ppermute | solution.py:152
  243.9 28.3 %collective-permute-start.10 = (bf16[256,640]{1,0:T(8,128)(2,1)S(1)}, bf16[256,640]{1,0:T(8,128)(2,1)S(1)}, u32[]{:S(2)}, u32[]{:S(2)}) collective-permute-start(bf16[256,640]{1,0:T(8,128)(2,1)S(1)} %shard_map.47.refs_6_), channel_id=1, source_target_pairs={{0,2},{2,0},{1,3},{3,1},{4,6},{6,4},{5,7},{7,5},{8,10},{10,8},{9,1... | collective-permute-start | bytes 983048 | tf_op jit(solution)/shard_map/ppermute | solution.py:152
  (46 other events, 630.0 us)

commit v3 on v2

v3 whole, which is shorter than its diff:
```python
import functools

import jax
import jax.numpy as jnp
from jax import lax
from jax.experimental import pallas as pl
from jax.experimental.pallas import tpu as pltpu
from jax.sharding import PartitionSpec as P

ROUNDS = 2
LANES = 128
SWAP = [(0, 1), (1, 0)]
PAIRS = [(0, 1), (1, 0), (2, 3), (3, 2)]
SKIPS = [(0, 2), (2, 0), (1, 3), (3, 1)]
MIDDLE = [(1, 2), (2, 1)]
ENDS = [(0, 3), (3, 0)]
OUTWARD = [(1, 0), (2, 3)]
F32 = jnp.float32
BF16 = jnp.bfloat16


def column_chunks(width):
    cut = (width // (2 * LANES)) * LANES
    if width % LANES or not cut:
        return [(t, 0, width) for t in range(ROUNDS)]
    return [(0, 0, cut), (0, cut, width - cut), (1, 0, width - cut), (1, width - cut, cut)]


def after(value, *done):
    return lax.optimization_barrier((value, *done))[0]


def pair_kernel(half_index, par_ref, near_ref, far_ref, *refs):
    del par_ref
    slots, out_ref, acc_ref = refs[:4], refs[-2], refs[-1]
    k = pl.program_id(0)

    for step in range(4):

        @pl.when(k == step)
        def _(step=step):
            value = lax.dot_general(
                (near_ref if step < 2 else far_ref)[...],
                slots[step][...],
                (((0,), (0,)), ((), ())),
                preferred_element_type=F32,
            )
            if step:
                value += acc_ref[...]
            if step < 3:
                acc_ref[...] = value
            else:
                out_ref[...] = value.astype(BF16)


def pair_sum(par, near, far, mine, into):
    rows, size = near.shape[0] // 2, near.shape[1]
    width = mine[0][0].shape[1]
    half_index = 0 if into is None else 1
    specs = [
        pl.BlockSpec((rows, size), lambda k, par: (jnp.minimum(k, 1) ^ par[0], 0)),
        pl.BlockSpec((rows, size), lambda k, par: (jnp.maximum(k - 2, 0) ^ par[0], 0)),
        *[pl.BlockSpec((rows, width), lambda k, par, at=at: (at, 0)) for _, at in mine],
    ]
    args = [near, far, *[array for array, _ in mine]]
    if half_index:
        specs.append(pl.BlockSpec(memory_space=pl.ANY))
        args.append(into)
    return pl.pallas_call(
        functools.partial(pair_kernel, half_index),
        grid_spec=pltpu.PrefetchScalarGridSpec(
            num_scalar_prefetch=1,
            grid=(4,),
            in_specs=specs,
            out_specs=pl.BlockSpec((size, width), lambda k, par: (half_index, 0)),
            scratch_shapes=[pltpu.VMEM((size, width), F32)],
        ),
        out_shape=jax.ShapeDtypeStruct((2 * size, width), BF16),
        input_output_aliases={len(args): 0} if half_index else {},
        compiler_params=pltpu.CompilerParams(vmem_limit_bytes=24 << 20),
        cost_estimate=pl.CostEstimate(
            flops=8 * rows * size * width,
            bytes_accessed=8 * rows * (size + width) + 2 * size * width,
            transcendentals=0,
        ),
    )(par, *args)


def gamma_kernel(n_aux, turn, start, mode, order_ref, core_ref, base_ref, column_ref, *refs):
    del order_ref
    parts, blocks = refs[:n_aux], refs[n_aux : n_aux + 4]
    refs = refs[n_aux + 4 :]
    if mode != "first":
        acc_ref, refs = refs[0], refs[1:]
    out_ref, amp_ref = refs
    size, width = amp_ref.shape[1:]
    r = pl.program_id(0)
    count = pl.num_programs(0)

    @pl.when(r == 0)
    def _():
        for h in range(2):
            lines = slice(h * size, (h + 1) * size)
            total = parts[0][lines, :].astype(F32)
            for other in parts[1:]:
                total = total + other[lines, :].astype(F32)
            which = core_ref[0] if h == 0 else 1 - core_ref[0]
            first = pl.multiple_of(which * width + start, LANES)
            below = base_ref[turn : turn + 1, :] - column_ref[pl.ds(first, size), :]
            amp_ref[h] = (total / below).astype(BF16)

    def run(which):
        value = jnp.dot(blocks[which][...], amp_ref[0], preferred_element_type=F32)
        value += jnp.dot(blocks[2 + which][...], amp_ref[1], preferred_element_type=F32)
        if mode != "first":
            value += acc_ref[...]
        if mode == "last":
            height = value.shape[0]
            step = width // LANES
            for c in range(step):
                out_ref[pl.ds(c, height, stride=step), :] = value[:, c * LANES : (c + 1) * LANES]
        else:
            out_ref[...] = value

    pl.when(r < count // 2)(lambda: run(0))
    pl.when(r >= count // 2)(lambda: run(1))


def gamma_step(table, turn, start, parts, blocks, acc, last):
    order, core, base, column = table
    near = blocks[0]
    rows, size = near.shape[0] // 2, near.shape[1]
    width = base.shape[1]
    block = rows // 2
    full = lambda array: pl.BlockSpec(array.shape, lambda r, order, core: (0, 0))
    args = [base, column, *parts]
    specs = [full(array) for array in args]
    for _ in range(2):
        specs += [
            pl.BlockSpec((block, size), lambda r, order, core: (jnp.minimum(r, 3), 0)),
            pl.BlockSpec((block, size), lambda r, order, core: (jnp.maximum(r - 4, 0), 0)),
        ]
    args += blocks
    if acc is not None:
        specs.append(pl.BlockSpec((block, width), lambda r, order, core: (r, 0)))
        args.append(acc)
    if last:
        step = width // LANES
        out_shape = jax.ShapeDtypeStruct((4 * rows * step, LANES), F32)
        out_spec = pl.BlockSpec(
            (block * step, LANES), lambda r, order, core: (order[r // 2] * 2 + r % 2, 0)
        )
    else:
        out_shape = jax.ShapeDtypeStruct((4 * rows, width), F32)
        out_spec = pl.BlockSpec((block, width), lambda r, order, core: (r, 0))
    mode = "last" if last else ("first" if acc is None else "more")
    return pl.pallas_call(
        functools.partial(gamma_kernel, len(parts), turn, start, mode),
        grid_spec=pltpu.PrefetchScalarGridSpec(
            num_scalar_prefetch=2,
            grid=(8,),
            in_specs=specs,
            out_specs=out_spec,
            scratch_shapes=[pltpu.VMEM((2, size, width), BF16)],
        ),
        out_shape=out_shape,
        compiler_params=pltpu.CompilerParams(vmem_limit_bytes=32 << 20),
        cost_estimate=pl.CostEstimate(
            flops=16 * rows * size * width,
            bytes_accessed=16 * rows * size + 4 * len(parts) * size * width + 32 * rows * width,
            transcendentals=0,
        ),
    )(order, core, *args)


def shifted(part, axis, n):
    return [part] + [lax.ppermute(part, axis, [(k, (k + d) % n) for k in range(n)]) for d in range(1, n)]


def local_four(integrals, occ_energy, vir_energy, round_owner):
    n_aux = lax.axis_size("aux")
    me = lax.axis_index("occ").astype(jnp.int32)
    core = lax.axis_index("vir").astype(jnp.int32)
    by_orbital = lax.optimization_barrier(jnp.transpose(integrals[0], (1, 0, 2)))
    rows, width = by_orbital.shape[1:]
    is_mid = (me == 1) | (me == 2)
    odd = me % 2
    orbital = lambda k: lax.dynamic_index_in_dim(by_orbital, k, 0, keepdims=False)

    own = [orbital(round_owner[t]) for t in range(ROUNDS)]
    across = orbital(me ^ 3)
    beside = lax.ppermute(jnp.concatenate([own[0], orbital(me ^ 1)], axis=0), "occ", PAIRS)
    b3_mid = lax.ppermute(across, "occ", MIDDLE)
    b2 = lax.ppermute(orbital(me ^ 2), "occ", SKIPS)
    b3_end = lax.ppermute(across, "occ", ENDS)
    near = [beside[:rows], lax.ppermute(own[1], "occ", PAIRS)]
    mine = [(orbital(me), 0), (beside, 1), (b2, 0), (jnp.where(is_mid, b3_mid, b3_end), 0)]

    energy_i = lax.dynamic_slice_in_dim(occ_energy, me, 1)
    energy_a = lax.dynamic_slice_in_dim(vir_energy, core * width, width)
    energy_j = jnp.take(occ_energy, round_owner)
    base = energy_i + energy_j[:, None] - energy_a[None, :]
    order = jnp.arange(4, dtype=jnp.int32) ^ (me & 2)
    table = (order, core[None], base, vir_energy[:, None])

    chunks = column_chunks(width)
    count = len(chunks)
    half, mid, part = [None] * count, [None] * count, [None] * count

    def hop(c, *done):
        turn, start, size = chunks[c]
        columns = slice(start, start + size)
        pieces = own[turn][:, columns], near[turn][:, columns]
        half[c] = jnp.where(odd == 1, jnp.concatenate(pieces[::-1], axis=0), jnp.concatenate(pieces, axis=0))
        if done:
            half[c] = after(half[c], *done)
        mid[c] = lax.ppermute(half[c], "occ", MIDDLE)

    hop(0, b3_mid)
    hop(1, b2, b3_end)
    acc, total = None, []
    for c, (turn, start, size) in enumerate(chunks):
        if c + 2 < count:
            hop(c + 2, mid[c], *([part[c - 1]] if c else []))
        half_swap = lax.ppermute(half[c], "vir", SWAP)
        end = lax.ppermute(mid[c], "occ", OUTWARD)
        if c + 1 < count:
            end = after(end, mid[c + 1])
        far = jnp.where(is_mid, mid[c], end)
        far_swap = lax.ppermute(far, "vir", SWAP)
        if c == 0:
            far = after(far, near[1])
        if c > 1:
            far = after(far, total[c - 2])
        for blocks in ((half[c], far), (half_swap, far_swap)):
            part[c] = pair_sum(odd[None], *blocks, mine, part[c])
        parts = shifted(part[c], "aux", n_aux)
        acc = gamma_step(table, turn, start, parts, [half[c], far, half_swap, far_swap], acc, c == count - 1)
        total.append(acc)
    return acc.reshape(4, rows, 1, width)


def local_any(integrals, occ_energy, vir_energy, round_owner):
    n_aux = lax.axis_size("aux")
    me = lax.axis_index("occ")
    core = lax.axis_index("vir")
    x = integrals[0]
    rows, n_occ, width = x.shape
    mine = lax.all_to_all(x, "occ", split_axis=1, concat_axis=0, tiled=True)[:, 0]
    energy_i = lax.dynamic_slice_in_dim(occ_energy, me, 1)
    energy_a = lax.dynamic_slice_in_dim(vir_energy, core * width, width)
    gamma = jnp.zeros(mine.shape, F32)
    for turn in range(ROUNDS):
        owner = round_owner[turn]
        own = lax.dynamic_index_in_dim(x, owner, 1, keepdims=False)
        whole = lax.all_gather(own, "occ", axis=0, tiled=True)
        other = lax.ppermute(whole, "vir", SWAP)
        energy_j = lax.dynamic_slice_in_dim(occ_energy, owner, 1)
        base = (energy_i + energy_j - energy_a)[None, :]
        for which, block in ((core, whole), (1 - core, other)):
            energy_b = lax.dynamic_slice_in_dim(vir_energy, which * width, width)[:, None]
            part = jnp.einsum("pb,pa->ba", block, mine, preferred_element_type=F32).astype(BF16)
            pair = sum(p.astype(F32) for p in shifted(part, "aux", n_aux))
            amplitude = (pair / (base - energy_b)).astype(BF16)
            gamma = gamma + jnp.dot(block, amplitude, preferred_element_type=F32)
    return gamma.reshape(-1, rows, 1, width)


def solution(mesh):
    placed = (P("occ", "aux", "grp", "vir"), P("grp"), P("grp"), P("grp"))
    local = local_four if mesh.shape["occ"] == 4 else local_any
    return jax.shard_map(
        local, mesh=mesh, in_specs=placed, out_specs=P("grp", "aux", "occ", "vir"), check_vma=False
    )
```

time: 279 us -> 219 us (0.78); the launches traced: 278 us -> 215 us
  waiting for transfers between devices: 146 us -> 102 us
  local copies, waits for them, and re-layouts: 29.8 us -> 16.7 us
  starting transfers between devices: 38.9 us -> 31.2 us
  between operations: 7.2 us -> 4.21 us
  Pallas kernels: 47 us -> 49.8 us
    ppermute x15 -> x14, waiting for transfers between devices: 120 us -> 65.2 us  [the longest x1 31.6 us: local_four(): lax.ppermute(jnp.concatenate([own[0], orbital(me ^ 1)], axis=0), 'occ', P...]
    ppermute x1, waiting for transfers between devices: 0.01 us -> 16.8 us  [local_four(): b2 = lax.ppermute(orbital(me ^ 2), 'occ', SKIPS)]
    ppermute x1, waiting for transfers between devices: 10.1 us -> 0.01 us  [local_four(): b3_end = lax.ppermute(across, 'occ', ENDS)]
    broadcast_in_dim x10 -> x1, local copies, waits for them, and re-layouts: 10.4 us -> 1.09 us  [local_four(): table = (order, core[None], base, vir_energy[:, None])]
    select_n x4 -> x9, other arithmetic: 0.68 us -> 7.91 us  [the longest x4 4.45 us: hop(): jnp.where(odd == 1, jnp.concatenate(pieces[::-1], axis=0), jnp.concatenat...]
    concatenate x5 -> x1, other arithmetic: 7.39 us -> 1.17 us  [local_four(): jnp.concatenate([own[0], orbital(me ^ 1)], axis=0)]
    ppermute x1, starting transfers between devices: 8.02 us -> 3.04 us  [local_four(): b2 = lax.ppermute(orbital(me ^ 2), 'occ', SKIPS)]
    ppermute x8 -> x4, waiting for transfers between devices: 15.9 us -> 20.1 us  [shifted(): lax.ppermute(part, axis, [(k, (k + d) % n) for k in range(n)])]
  transfers between devices with their start and end apart: 30 -> 25, of which waited for: 10 -> 10; matrix products, arithmetic and copies ran while one was open for 11% -> 8% of each run, Pallas kernels for 15% -> 20%
where the time goes in v3:
time: 219 us; the launch traced here: 215 us
  waiting for transfers between devices  102 us (47%)
  Pallas kernels  49.8 us (23%)
  starting transfers between devices  31.2 us (14%)
  local copies, waits for them, and re-layouts  16.7 us (8%)
  other arithmetic  11.1 us (5%)
  between operations  4.21 us (2%)
    ppermute x1, waiting for transfers between devices, local_four(): lax.ppermute(jnp.concatenate([own[0], orbital(me ^ 1)], axis=0), 'occ', P...  31.6 us
    ppermute x4, waiting for transfers between devices, local_four(): end = lax.ppermute(mid[c], 'occ', OUTWARD)  28.7 us
    pallas_call x4, Pallas kernels, gamma_step(): pl.pallas_call(functools.partial(gamma_kernel, len(parts), turn, start, m...  28.2 us
    pallas_call x8, Pallas kernels, pair_sum(): pl.pallas_call(functools.partial(pair_kernel, half_index), grid_spec=pltp...  21.5 us
    ppermute x4, waiting for transfers between devices, shifted(): lax.ppermute(part, axis, [(k, (k + d) % n) for k in range(n)])  20.1 us
    ppermute x1, waiting for transfers between devices, local_four(): b2 = lax.ppermute(orbital(me ^ 2), 'occ', SKIPS)  16.8 us
    ppermute x4, starting transfers between devices, shifted(): lax.ppermute(part, axis, [(k, (k + d) % n) for k in range(n)])  6.24 us
    ppermute x4, starting transfers between devices, hop(): mid[c] = lax.ppermute(half[c], 'occ', MIDDLE)  6.06 us
  transfers between devices with their start and end apart: 25, of which 10 were waited for; matrix products, arithmetic and copies ran while one was open for 8% of the time, Pallas kernels for 20%

profile of v3, /device:TPU:0, one launch (start us, length us, event | category | flops | bytes accessed | tf_op | source)
XLA Modules:
  0.0 215.1 jit_solution(13884113547013334073)
XLA Ops:
  3.9 3.6 %copy.17 = bf16[1,512,4,640]{3,1,2,0:T(8,128)(2,1)} copy(bf16[1,512,4,640]{3,2,1,0:T(4,128)(2,1)} %param.4) | data formatting | bytes 5242880 | tf_op args[0]
  8.7 3.5 %dynamic-slice_bitcast_fusion = (bf16[512,640]{1,0:T(8,128)(2,1)S(1)}, bf16[512,640]{1,0:T(8,128)(2,1)}, bf16[512,640]{1,0:T(8,128)(2,1)}, bf16[512,640]{1,0:T(8...) fusion(bf16[4,512,640]{2,1,0:T(8,128)(2,1)} %bitcast.23, s32[]{:T(128)S(6)} %select_n.93, ...), kind=kLoop, calls=%fused_computation.7 | loop fusion | bytes 7864344 | tf_op jit(solution)/shard_map/jit(dynamic_index_in_dim)/squeeze | solution.py:188
  13.3 3.1 %collective-permute-start.1 = (bf16[1024,640]{1,0:T(8,128)(2,1)}, bf16[1024,640]{1,0:T(8,128)(2,1)S(1)}, u32[]{:S(2)}, u32[]{:S(2)}) collective-permute-start(bf16[1024,640]{1,0:T(8,128)(2,1)} %pad_maximum_fusion), channel_id=1, source_target_pairs={{0,4},{4,0},{8,12},{12,8},{1,5},{5,1},{9,13},{13,9},{2,6},{6,2},{1... | collective-permute-start | bytes 3932168 | tf_op jit(solution)/shard_map/ppermute | solution.py:192
  17.9 3.0 %collective-permute-start.2 = (bf16[512,640]{1,0:T(8,128)(2,1)}, bf16[512,640]{1,0:T(8,128)(2,1)S(1)}, u32[]{:S(2)}, u32[]{:S(2)}) collective-permute-start(bf16[512,640]{1,0:T(8,128)(2,1)} %get-tuple-element.27), channel_id=1, source_target_pairs={{0,8},{8,0},{4,12},{12,4},{1,9},{9,1},{5,13},{13,5},{2,10},{10,2},... | collective-permute-start | bytes 1966088 | tf_op jit(solution)/shard_map/ppermute | solution.py:194
  20.9 4.8 %collective-permute-start.3 = (bf16[512,640]{1,0:T(8,128)(2,1)}, bf16[512,640]{1,0:T(8,128)(2,1)}, u32[]{:S(2)}, u32[]{:S(2)}) collective-permute-start(bf16[512,640]{1,0:T(8,128)(2,1)} %get-tuple-element.26), channel_id=1, source_target_pairs={{0,12},{12,0},{1,13},{13,1},{2,14},{14,2},{3,15},{15,3},{16,28},{2... | collective-permute-start | bytes 1966088 | tf_op jit(solution)/shard_map/ppermute | solution.py:195
  26.7 31.6 %collective-permute-done.1.refs_1_ = bf16[1024,640]{1,0:T(8,128)(2,1)S(1)} collective-permute-done((bf16[1024,640]{1,0:T(8,128)(2,1)}, bf16[1024,640]{1,0:T(8,128)(2,1)S(1)}, u32[]{:S(2)}, u32[]{:S(2)}) %collective-permute-start.1) | collective-permute-done | bytes 1310752 | tf_op jit(solution)/shard_map/ppermute | solution.py:192
  62.0 16.8 %collective-permute-done.2.refs_2_ = bf16[512,640]{1,0:T(8,128)(2,1)S(1)} collective-permute-done((bf16[512,640]{1,0:T(8,128)(2,1)}, bf16[512,640]{1,0:T(8,128)(2,1)S(1)}, u32[]{:S(2)}, u32[]{:S(2)}) %collective-permute-start.2) | collective-permute-done | bytes 655392 | tf_op jit(solution)/shard_map/ppermute | solution.py:194
  82.8 4.8 %collective-permute-done = bf16[512,640]{1,0:T(8,128)(2,1)} collective-permute-done((bf16[512,640]{1,0:T(8,128)(2,1)}, bf16[512,640]{1,0:T(8,128)(2,1)}, u32[]{:S(2)}, u32[]{:S(2)}) %collective-permute-start) | collective-permute-done | bytes 655392 | tf_op jit(solution)/shard_map/ppermute | solution.py:196
  89.8 1.6 collective-permute-start.16
  95.6 6.6 %collective-permute-done.8 = bf16[1024,256]{1,0:T(8,128)(2,1)S(1)} collective-permute-done((bf16[1024,256]{1,0:T(8,128)(2,1)}, bf16[1024,256]{1,0:T(8,128)(2,1)S(1)}, u32[]{:S(2)}, u32[]{:S(2)}) %collective-permute-start.8) | collective-permute-done | bytes 524320 | tf_op jit(solution)/shard_map/ppermute | solution.py:226
  105.9 2.6 %shard_map.46.refs_4_ = bf16[512,640]{1,0:T(8,128)(2,1)S(1)} custom-call(s32[1]{0:T(128)} %bitcast.2.par_ref, bf16[1024,256]{1,0:T(8,128)(2,1)} %maximum_select_fusion.3.near_ref.refs_2_, bf16[1024,256]{1,0:T(8,128)(2,1)S(1)} %broadcast_select_fusion.4.far_ref.refs_3_, bf16[512,640]{1,0:T(8,128)(2,1)S(1)} %get-tuple-element.25.refs_0_, ...), custom_call_target="tpu_custom_call" | custom-call | flops 671088640 | bytes 3997696 | tf_op jit(solution)/shard_map/pallas_call | solution.py:69
  109.9 14.8 %collective-permute-done.15 = bf16[1024,384]{1,0:T(8,128)(2,1)} collective-permute-done((bf16[1024,384]{1,0:T(8,128)(2,1)}, bf16[1024,384]{1,0:T(8,128)(2,1)}, u32[]{:S(2)}, u32[]{:S(2)}) %collective-permute-start.15) | collective-permute-done | bytes 786464 | tf_op jit(solution)/shard_map/ppermute | solution.py:226
  124.7 2.1 broadcast_select_fusion.1.far_ref.refs_3_
  126.9 1.7 shard_map.47.refs_0_
  132.3 1.6 collective-permute-start.19
  133.8 3.7 %shard_map.48.refs_4_ = bf16[768,640]{1,0:T(8,128)(2,1)S(1)} custom-call(s32[1]{0:T(128)} %bitcast.2.par_ref, bf16[1024,384]{1,0:T(8,128)(2,1)} %maximum_select_fusion.near_ref.refs_2_, bf16[1024,384]{1,0:T(8,128)(2,1)} %broadcast_select_fusion.1.far_ref.refs_3_, bf16[512,640]{1,0:T(8,128)(2,1)S(1)} %get-tuple-element.25.refs_0_, ...), custom_call_target="tpu_custom_call" | custom-call | flops 1006632960 | bytes 4685824 | tf_op jit(solution)/shard_map/pallas_call | solution.py:69
  137.9 3.7 %collective-permute-done.22 = bf16[1024,384]{1,0:T(8,128)(2,1)} collective-permute-done((bf16[1024,384]{1,0:T(8,128)(2,1)}, bf16[1024,384]{1,0:T(8,128)(2,1)}, u32[]{:S(2)}, u32[]{:S(2)}) %collective-permute-start.22) | collective-permute-done | bytes 786464 | tf_op jit(solution)/shard_map/ppermute | solution.py:226
  142.9 1.6 collective-permute-start.12
  144.6 3.7 %shard_map.49.refs_0_ = bf16[768,640]{1,0:T(8,128)(2,1)S(1)} custom-call(s32[1]{0:T(128)} %bitcast.2.par_ref, bf16[1024,384]{1,0:T(8,128)(2,1)} %collective-permute-done.14.near_ref.refs_4_, bf16[1024,384]{1,0:T(8,128)(2,1)} %collective-permute-done.17.far_ref.refs_5_, ...), custom_call_target="tpu_custom_call", output_to_operand_aliasing={{}: (7, {})} | custom-call | flops 1006632960 | bytes 4685824 | tf_op jit(solution)/shard_map/pallas_call | solution.py:69
  150.0 5.5 %shard_map.50.refs_6_ = f32[2048,640]{1,0:T(8,128)S(1)} custom-call(s32[4]{0:T(128)S(1)} %iota_xor_fusion.order_ref, s32[1]{0:T(128)} %bitcast.core_ref, f32[2,640]{1,0:T(2,128)S(1)} %broadcast_subtract_fusion.base_ref, f32[1280,1]{1,0:T(8,128)S(1)} %copy-done, bf16[512,640]{1,0:T(8,128)(2,1)S(1)} %copy-done.2, ...), custom_call_target="tpu_custom_call" | custom-call | flops 1342177280 | bytes 13893632 | tf_op jit(solution)/shard_map/pallas_call | solution.py:157
  155.5 3.2 %shard_map.54.refs_4_ = bf16[768,640]{1,0:T(8,128)(2,1)S(1)} custom-call(s32[1]{0:T(128)} %bitcast.2.par_ref, bf16[1024,384]{1,0:T(8,128)(2,1)} %maximum_select_fusion.1.near_ref.refs_2_, bf16[1024,384]{1,0:T(8,128)(2,1)S(1)} %broadcast_select_fusion.far_ref.refs_3_, bf16[512,640]{1,0:T(8,128)(2,1)S(1)} %get-tuple-element.25.refs_0_, ...), custom_call_target="tpu_custom_call" | custom-call | flops 1006632960 | bytes 4685824 | tf_op jit(solution)/shard_map/pallas_call | solution.py:69
  158.7 3.6 %collective-permute-done.12 = bf16[1024,256]{1,0:T(8,128)(2,1)S(1)} collective-permute-done((bf16[1024,256]{1,0:T(8,128)(2,1)}, bf16[1024,256]{1,0:T(8,128)(2,1)S(1)}, u32[]{:S(2)}, u32[]{:S(2)}) %collective-permute-start.12) | collective-permute-done | bytes 524320 | tf_op jit(solution)/shard_map/ppermute | solution.py:226
  162.5 2.2 %shard_map.55.refs_0_ = bf16[768,640]{1,0:T(8,128)(2,1)S(1)} custom-call(s32[1]{0:T(128)} %bitcast.2.par_ref, bf16[1024,384]{1,0:T(8,128)(2,1)S(1)} %collective-permute-done.21.near_ref.refs_4_, bf16[1024,384]{1,0:T(8,128)(2,1)S(1)} %collective-permute-done.23.far_ref.refs_5_, ...), custom_call_target="tpu_custom_call", output_to_operand_aliasing={{}: (7, {})} | custom-call | flops 1006632960 | bytes 4685824 | tf_op jit(solution)/shard_map/pallas_call | solution.py:69
  166.3 6.7 %collective-permute-done.18.refs_1_ = bf16[768,640]{1,0:T(8,128)(2,1)S(1)} collective-permute-done((bf16[768,640]{1,0:T(8,128)(2,1)S(1)}, bf16[768,640]{1,0:T(8,128)(2,1)S(1)}, u32[]{:S(2)}, u32[]{:S(2)}) %collective-permute-start.18) | collective-permute-done | bytes 983072 | tf_op jit(solution)/shard_map/ppermute | solution.py:177
  173.0 8.2 %shard_map.51.refs_6_ = f32[2048,640]{1,0:T(8,128)S(1)} custom-call(s32[4]{0:T(128)S(1)} %iota_xor_fusion.order_ref, s32[1]{0:T(128)} %bitcast.core_ref, f32[2,640]{1,0:T(2,128)S(1)} %broadcast_subtract_fusion.base_ref, f32[1280,1]{1,0:T(8,128)S(1)} %copy-done, bf16[768,640]{1,0:T(8,128)(2,1)S(1)} %shard_map.49.refs_0_, ...), custom_call_target="tpu_custom_call" | custom-call | flops 2013265920 | bytes 15597568 | tf_op jit(solution)/shard_map/pallas_call | solution.py:157
  181.2 2.7 %shard_map.52.refs_4_ = bf16[512,640]{1,0:T(8,128)(2,1)S(1)} custom-call(s32[1]{0:T(128)} %bitcast.2.par_ref, bf16[1024,256]{1,0:T(8,128)(2,1)} %maximum_select_fusion.2.near_ref.refs_2_, bf16[1024,256]{1,0:T(8,128)(2,1)S(1)} %broadcast_select_fusion.3.far_ref.refs_3_, bf16[512,640]{1,0:T(8,128)(2,1)S(1)} %get-tuple-element.25.refs_0_, ...), custom_call_target="tpu_custom_call" | custom-call | flops 671088640 | bytes 3997696 | tf_op jit(solution)/shard_map/pallas_call | solution.py:69
  183.9 1.7 shard_map.53.refs_0_
  185.6 1.6 collective-permute-start.20
  187.2 6.9 %collective-permute-done.24.refs_1_ = bf16[768,640]{1,0:T(8,128)(2,1)S(1)} collective-permute-done((bf16[768,640]{1,0:T(8,128)(2,1)S(1)}, bf16[768,640]{1,0:T(8,128)(2,1)S(1)}, u32[]{:S(2)}, u32[]{:S(2)}) %collective-permute-start.24) | collective-permute-done | bytes 983072 | tf_op jit(solution)/shard_map/ppermute | solution.py:177
  194.0 6.9 %shard_map.56.refs_6_ = f32[2048,640]{1,0:T(8,128)S(1)} custom-call(s32[4]{0:T(128)S(1)} %iota_xor_fusion.order_ref, s32[1]{0:T(128)} %bitcast.core_ref, f32[2,640]{1,0:T(2,128)S(1)} %broadcast_subtract_fusion.base_ref, f32[1280,1]{1,0:T(8,128)S(1)} %copy-done, bf16[768,640]{1,0:T(8,128)(2,1)S(1)} %shard_map.55.refs_0_, ...), custom_call_target="tpu_custom_call" | custom-call | flops 2013265920 | bytes 15597568 | tf_op jit(solution)/shard_map/pallas_call | solution.py:157
  200.9 6.6 %collective-permute-done.20.refs_1_ = bf16[512,640]{1,0:T(8,128)(2,1)S(1)} collective-permute-done((bf16[512,640]{1,0:T(8,128)(2,1)S(1)}, bf16[512,640]{1,0:T(8,128)(2,1)S(1)}, u32[]{:S(2)}, u32[]{:S(2)}) %collective-permute-start.20) | collective-permute-done | bytes 655392 | tf_op jit(solution)/shard_map/ppermute | solution.py:177
  207.5 7.6 %shard_map.57 = f32[10240,128]{1,0:T(8,128)} custom-call(s32[4]{0:T(128)S(1)} %iota_xor_fusion.order_ref, s32[1]{0:T(128)} %bitcast.core_ref, f32[2,640]{1,0:T(2,128)S(1)} %broadcast_subtract_fusion.base_ref, f32[1280,1]{1,0:T(8,128)S(1)} %copy-done, bf16[512,640]{1,0:T(8,128)(2,1)S(1)} %shard_map.53.refs_0_, ...), custom_call_target="tpu_custom_call" | custom-call | flops 1342177280 | bytes 13893632 | tf_op jit(solution)/shard_map/pallas_call | solution.py:157
  (86 shorter events, 32.7 us)
Async XLA Ops:
  13.3 45.0 %collective-permute-start.1 = (bf16[1024,640]{1,0:T(8,128)(2,1)}, bf16[1024,640]{1,0:T(8,128)(2,1)S(1)}, u32[]{:S(2)}, u32[]{:S(2)}) collective-permute-start(bf16[1024,640]{1,0:T(8,128)(2,1)} %pad_maximum_fusion), channel_id=1, source_target_pairs={{0,4},{4,0},{8,12},{12,8},{1,5},{5,1},{9,13},{13,9},{2,6},{6,2},{1... | collective-permute-start | bytes 3932168 | tf_op jit(solution)/shard_map/ppermute | solution.py:192
  16.4 43.0 %collective-permute-start.5 = (bf16[512,640]{1,0:T(8,128)(2,1)}, bf16[512,640]{1,0:T(8,128)(2,1)}, u32[]{:S(2)}, u32[]{:S(2)}) collective-permute-start(bf16[512,640]{1,0:T(8,128)(2,1)} %get-tuple-element.26), channel_id=1, source_target_pairs={{4,8},{8,4},{5,9},{9,5},{6,10},{10,6},{7,11},{11,7},{20,24},{24,20... | collective-permute-start | bytes 1966088 | tf_op jit(solution)/shard_map/ppermute | solution.py:193
  17.9 61.0 %collective-permute-start.2 = (bf16[512,640]{1,0:T(8,128)(2,1)}, bf16[512,640]{1,0:T(8,128)(2,1)S(1)}, u32[]{:S(2)}, u32[]{:S(2)}) collective-permute-start(bf16[512,640]{1,0:T(8,128)(2,1)} %get-tuple-element.27), channel_id=1, source_target_pairs={{0,8},{8,0},{4,12},{12,4},{1,9},{9,1},{5,13},{13,5},{2,10},{10,2},... | collective-permute-start | bytes 1966088 | tf_op jit(solution)/shard_map/ppermute | solution.py:194
  20.9 57.9 %collective-permute-start.3 = (bf16[512,640]{1,0:T(8,128)(2,1)}, bf16[512,640]{1,0:T(8,128)(2,1)}, u32[]{:S(2)}, u32[]{:S(2)}) collective-permute-start(bf16[512,640]{1,0:T(8,128)(2,1)} %get-tuple-element.26), channel_id=1, source_target_pairs={{0,12},{12,0},{1,13},{13,1},{2,14},{14,2},{3,15},{15,3},{16,28},{2... | collective-permute-start | bytes 1966088 | tf_op jit(solution)/shard_map/ppermute | solution.py:195
  25.7 61.9 %collective-permute-start = (bf16[512,640]{1,0:T(8,128)(2,1)}, bf16[512,640]{1,0:T(8,128)(2,1)}, u32[]{:S(2)}, u32[]{:S(2)}) collective-permute-start(bf16[512,640]{1,0:T(8,128)(2,1)} %get-tuple-element.30), channel_id=1, source_target_pairs={{0,4},{4,0},{8,12},{12,8},{1,5},{5,1},{9,13},{13,9},{2,6},{6,2},{1... | collective-permute-start | bytes 1966088 | tf_op jit(solution)/shard_map/ppermute | solution.py:196
  26.6 34.2 %copy-start.10 = (bf16[512,384]{1,0:T(8,128)(2,1)S(1)}, bf16[512,384]{1,0:T(8,128)(2,1)}, u32[]{:S(2)}) copy-start(bf16[512,384]{1,0:T(8,128)(2,1)} %slice.48) | copy-start | bytes 1179652
  59.3 21.1 %collective-permute-start.7 = (bf16[1024,256]{1,0:T(8,128)(2,1)}, bf16[1024,256]{1,0:T(8,128)(2,1)}, u32[]{:S(2)}, u32[]{:S(2)}) collective-permute-start(bf16[1024,256]{1,0:T(8,128)(2,1)} %maximum_select_fusion.3.near_ref.refs_2_), channel_id=1, source_target_pairs={{4,8},{8,4},{5,9},{9,5},{6,10},{10,6},{7,11},{11,7},{20,24},{24,20... | collective-permute-start | bytes 1572872 | tf_op jit(solution)/shard_map/ppermute | solution.py:217
  62.0 30.7 %copy-start.12 = (s32[2]{0:T(128)S(1)}, s32[2]{0:T(128)}, u32[]{:S(2)}) copy-start(s32[2]{0:T(128)} %param.7) | copy-start | bytes 28
  78.9 12.5 %collective-permute-start.4 = (bf16[1024,384]{1,0:T(8,128)(2,1)}, bf16[1024,384]{1,0:T(8,128)(2,1)}, u32[]{:S(2)}, u32[]{:S(2)}) collective-permute-start(bf16[1024,384]{1,0:T(8,128)(2,1)} %maximum_select_fusion.near_ref.refs_2_), channel_id=1, source_target_pairs={{4,8},{8,4},{5,9},{9,5},{6,10},{10,6},{7,11},{11,7},{20,24},{24,20... | collective-permute-start | bytes 2359304 | tf_op jit(solution)/shard_map/ppermute | solution.py:217
  80.4 21.7 %collective-permute-start.8 = (bf16[1024,256]{1,0:T(8,128)(2,1)}, bf16[1024,256]{1,0:T(8,128)(2,1)S(1)}, u32[]{:S(2)}, u32[]{:S(2)}) collective-permute-start(bf16[1024,256]{1,0:T(8,128)(2,1)} %collective-permute-done.7), channel_id=1, source_target_pairs={{4,0},{8,12},{5,1},{9,13},{6,2},{10,14},{7,3},{11,15},{20,16},{24,... | collective-permute-start | bytes 1572872 | tf_op jit(solution)/shard_map/ppermute | solution.py:226
  82.7 11.0 %copy-start.11 = (f32[1280]{0:T(1024)S(1)}, f32[1280]{0:T(1024)}, u32[]{:S(2)}) copy-start(f32[1280]{0:T(1024)} %param.6) | copy-start | bytes 15364
  89.8 18.8 %collective-permute-start.16 = (bf16[1024,384]{1,0:T(8,128)(2,1)}, bf16[1024,384]{1,0:T(8,128)(2,1)}, u32[]{:S(2)}, u32[]{:S(2)}) collective-permute-start(bf16[1024,384]{1,0:T(8,128)(2,1)} %maximum_select_fusion.1.near_ref.refs_2_), channel_id=1, source_target_pairs={{4,8},{8,4},{5,9},{9,5},{6,10},{10,6},{7,11},{11,7},{20,24},{24,20... | collective-permute-start | bytes 2359304 | tf_op jit(solution)/shard_map/ppermute | solution.py:217
  91.4 33.3 %collective-permute-start.15 = (bf16[1024,384]{1,0:T(8,128)(2,1)}, bf16[1024,384]{1,0:T(8,128)(2,1)}, u32[]{:S(2)}, u32[]{:S(2)}) collective-permute-start(bf16[1024,384]{1,0:T(8,128)(2,1)} %collective-permute-done.4), channel_id=1, source_target_pairs={{4,0},{8,12},{5,1},{9,13},{6,2},{10,14},{7,3},{11,15},{20,16},{24,... | collective-permute-start | bytes 2359304 | tf_op jit(solution)/shard_map/ppermute | solution.py:226
  95.5 31.3 %collective-permute-start.6 = (bf16[1024,256]{1,0:T(8,128)(2,1)}, bf16[1024,256]{1,0:T(8,128)(2,1)S(1)}, u32[]{:S(2)}, u32[]{:S(2)}) collective-permute-start(bf16[1024,256]{1,0:T(8,128)(2,1)} %maximum_select_fusion.3.near_ref.refs_2_), channel_id=1, source_target_pairs={{0,1},{1,0},{2,3},{3,2},{4,5},{5,4},{6,7},{7,6},{8,9},{9,8},{10,11... | collective-permute-start | bytes 1572872 | tf_op jit(solution)/shard_map/ppermute | solution.py:225
  102.2 24.6 %collective-permute-start.9 = (bf16[1024,256]{1,0:T(8,128)(2,1)S(1)}, bf16[1024,256]{1,0:T(8,128)(2,1)S(1)}, u32[]{:S(2)}, u32[]{:S(2)}) collective-permute-start(bf16[1024,256]{1,0:T(8,128)(2,1)S(1)} %broadcast_select_fusion.4.far_ref.refs_3_), channel_id=1, source_target_pairs={{0,1},{1,0},{2,3},{3,2},{4,5},{5,4},{6,7},{7,6},{8,9},{9,8},{10,11... | collective-permute-start | bytes 1572872 | tf_op jit(solution)/shard_map/ppermute | solution.py:230
  105.6 37.4 %collective-permute-start.14 = (bf16[1024,384]{1,0:T(8,128)(2,1)}, bf16[1024,384]{1,0:T(8,128)(2,1)}, u32[]{:S(2)}, u32[]{:S(2)}) collective-permute-start(bf16[1024,384]{1,0:T(8,128)(2,1)} %maximum_select_fusion.near_ref.refs_2_), channel_id=1, source_target_pairs={{0,1},{1,0},{2,3},{3,2},{4,5},{5,4},{6,7},{7,6},{8,9},{9,8},{10,11... | collective-permute-start | bytes 2359304 | tf_op jit(solution)/shard_map/ppermute | solution.py:225
  108.6 33.0 %collective-permute-start.22 = (bf16[1024,384]{1,0:T(8,128)(2,1)}, bf16[1024,384]{1,0:T(8,128)(2,1)}, u32[]{:S(2)}, u32[]{:S(2)}) collective-permute-start(bf16[1024,384]{1,0:T(8,128)(2,1)} %collective-permute-done.16), channel_id=1, source_target_pairs={{4,0},{8,12},{5,1},{9,13},{6,2},{10,14},{7,3},{11,15},{20,16},{24,... | collective-permute-start | bytes 2359304 | tf_op jit(solution)/shard_map/ppermute | solution.py:226
  126.8 17.7 %collective-permute-start.17 = (bf16[1024,384]{1,0:T(8,128)(2,1)}, bf16[1024,384]{1,0:T(8,128)(2,1)}, u32[]{:S(2)}, u32[]{:S(2)}) collective-permute-start(bf16[1024,384]{1,0:T(8,128)(2,1)} %broadcast_select_fusion.1.far_ref.refs_3_), channel_id=1, source_target_pairs={{0,1},{1,0},{2,3},{3,2},{4,5},{5,4},{6,7},{7,6},{8,9},{9,8},{10,11... | collective-permute-start | bytes 2359304 | tf_op jit(solution)/shard_map/ppermute | solution.py:230
  129.4 8.1 %collective-permute-start.11 = (bf16[1024,256]{1,0:T(8,128)(2,1)}, bf16[1024,256]{1,0:T(8,128)(2,1)}, u32[]{:S(2)}, u32[]{:S(2)}) collective-permute-start(bf16[1024,256]{1,0:T(8,128)(2,1)} %maximum_select_fusion.2.near_ref.refs_2_), channel_id=1, source_target_pairs={{4,8},{8,4},{5,9},{9,5},{6,10},{10,6},{7,11},{11,7},{20,24},{24,20... | collective-permute-start | bytes 1572872 | tf_op jit(solution)/shard_map/ppermute | solution.py:217
  132.3 17.7 %collective-permute-start.19 = (bf16[512,640]{1,0:T(8,128)(2,1)}, bf16[512,640]{1,0:T(8,128)(2,1)S(1)}, u32[]{:S(2)}, u32[]{:S(2)}) collective-permute-start(bf16[512,640]{1,0:T(8,128)(2,1)} %copy-done.1), channel_id=1, source_target_pairs={{0,2},{2,0},{1,3},{3,1},{4,6},{6,4},{5,7},{7,5},{8,10},{10,8},{9,1... | collective-permute-start | bytes 1966088 | tf_op jit(solution)/shard_map/ppermute | solution.py:177
  137.6 24.9 %collective-permute-start.21 = (bf16[1024,384]{1,0:T(8,128)(2,1)}, bf16[1024,384]{1,0:T(8,128)(2,1)S(1)}, u32[]{:S(2)}, u32[]{:S(2)}) collective-permute-start(bf16[1024,384]{1,0:T(8,128)(2,1)} %maximum_select_fusion.1.near_ref.refs_2_), channel_id=1, source_target_pairs={{0,1},{1,0},{2,3},{3,2},{4,5},{5,4},{6,7},{7,6},{8,9},{9,8},{10,11... | collective-permute-start | bytes 2359304 | tf_op jit(solution)/shard_map/ppermute | solution.py:225
  142.8 7.2 %copy-start = (f32[1280,1]{1,0:T(8,128)S(1)}, f32[1280,1]{1,0:T(8,128)}, u32[]{:S(2)}) copy-start(f32[1280,1]{1,0:T(8,128)} %broadcast_in_dim.14.column_ref) | copy-start | bytes 15364
  142.8 7.2 %copy-start.2 = (bf16[512,640]{1,0:T(8,128)(2,1)S(1)}, bf16[512,640]{1,0:T(8,128)(2,1)}, u32[]{:S(2)}) copy-start(bf16[512,640]{1,0:T(8,128)(2,1)} %copy-done.1) | copy-start | bytes 1966084
  142.8 7.2 %copy-start.4 = (bf16[1024,256]{1,0:T(8,128)(2,1)S(1)}, bf16[1024,256]{1,0:T(8,128)(2,1)}, u32[]{:S(2)}) copy-start(bf16[1024,256]{1,0:T(8,128)(2,1)} %copy-done.3) | copy-start | bytes 1572868
  142.8 7.2 %copy-start.6 = (bf16[1024,256]{1,0:T(8,128)(2,1)S(1)}, bf16[1024,256]{1,0:T(8,128)(2,1)}, u32[]{:S(2)}) copy-start(bf16[1024,256]{1,0:T(8,128)(2,1)} %copy-done.5) | copy-start | bytes 1572868
  142.9 19.7 %collective-permute-start.23 = (bf16[1024,384]{1,0:T(8,128)(2,1)S(1)}, bf16[1024,384]{1,0:T(8,128)(2,1)S(1)}, u32[]{:S(2)}, u32[]{:S(2)}) collective-permute-start(bf16[1024,384]{1,0:T(8,128)(2,1)S(1)} %broadcast_select_fusion.far_ref.refs_3_), channel_id=1, source_target_pairs={{0,1},{1,0},{2,3},{3,2},{4,5},{5,4},{6,7},{7,6},{8,9},{9,8},{10,11... | collective-permute-start | bytes 2359304 | tf_op jit(solution)/shard_map/ppermute | solution.py:230
  142.9 19.4 %collective-permute-start.12 = (bf16[1024,256]{1,0:T(8,128)(2,1)}, bf16[1024,256]{1,0:T(8,128)(2,1)S(1)}, u32[]{:S(2)}, u32[]{:S(2)}) collective-permute-start(bf16[1024,256]{1,0:T(8,128)(2,1)} %collective-permute-done.11), channel_id=1, source_target_pairs={{4,0},{8,12},{5,1},{9,13},{6,2},{10,14},{7,3},{11,15},{20,16},{24,... | collective-permute-start | bytes 1572872 | tf_op jit(solution)/shard_map/ppermute | solution.py:226
  148.3 24.6 %collective-permute-start.18 = (bf16[768,640]{1,0:T(8,128)(2,1)S(1)}, bf16[768,640]{1,0:T(8,128)(2,1)S(1)}, u32[]{:S(2)}, u32[]{:S(2)}) collective-permute-start(bf16[768,640]{1,0:T(8,128)(2,1)S(1)} %shard_map.49.refs_0_), channel_id=1, source_target_pairs={{0,2},{2,0},{1,3},{3,1},{4,6},{6,4},{5,7},{7,5},{8,10},{10,8},{9,1... | collective-permute-start | bytes 2949128 | tf_op jit(solution)/shard_map/ppermute | solution.py:177
  149.9 33.9 %collective-permute-start.10 = (bf16[1024,256]{1,0:T(8,128)(2,1)}, bf16[1024,256]{1,0:T(8,128)(2,1)S(1)}, u32[]{:S(2)}, u32[]{:S(2)}) collective-permute-start(bf16[1024,256]{1,0:T(8,128)(2,1)} %maximum_select_fusion.2.near_ref.refs_2_), channel_id=1, source_target_pairs={{0,1},{1,0},{2,3},{3,2},{4,5},{5,4},{6,7},{7,6},{8,9},{9,8},{10,11... | collective-permute-start | bytes 1572872 | tf_op jit(solution)/shard_map/ppermute | solution.py:225
  162.4 21.4 %collective-permute-start.13 = (bf16[1024,256]{1,0:T(8,128)(2,1)S(1)}, bf16[1024,256]{1,0:T(8,128)(2,1)S(1)}, u32[]{:S(2)}, u32[]{:S(2)}) collective-permute-start(bf16[1024,256]{1,0:T(8,128)(2,1)S(1)} %broadcast_select_fusion.3.far_ref.refs_3_), channel_id=1, source_target_pairs={{0,1},{1,0},{2,3},{3,2},{4,5},{5,4},{6,7},{7,6},{8,9},{9,8},{10,11... | collective-permute-start | bytes 1572872 | tf_op jit(solution)/shard_map/ppermute | solution.py:230
  164.7 29.3 %collective-permute-start.24 = (bf16[768,640]{1,0:T(8,128)(2,1)S(1)}, bf16[768,640]{1,0:T(8,128)(2,1)S(1)}, u32[]{:S(2)}, u32[]{:S(2)}) collective-permute-start(bf16[768,640]{1,0:T(8,128)(2,1)S(1)} %shard_map.55.refs_0_), channel_id=1, source_target_pairs={{0,2},{2,0},{1,3},{3,1},{4,6},{6,4},{5,7},{7,5},{8,10},{10,8},{9,1... | collective-permute-start | bytes 2949128 | tf_op jit(solution)/shard_map/ppermute | solution.py:177
  185.6 21.9 %collective-permute-start.20 = (bf16[512,640]{1,0:T(8,128)(2,1)S(1)}, bf16[512,640]{1,0:T(8,128)(2,1)S(1)}, u32[]{:S(2)}, u32[]{:S(2)}) collective-permute-start(bf16[512,640]{1,0:T(8,128)(2,1)S(1)} %shard_map.53.refs_0_), channel_id=1, source_target_pairs={{0,2},{2,0},{1,3},{3,1},{4,6},{6,4},{5,7},{7,5},{8,10},{10,8},{9,1... | collective-permute-start | bytes 1966088 | tf_op jit(solution)/shard_map/ppermute | solution.py:177
  (6 other events, 21.5 us)

commit v4 on v3

v4 whole, which is shorter than its diff:
```python
import functools

import jax
import jax.numpy as jnp
from jax import lax
from jax.experimental import pallas as pl
from jax.experimental.pallas import tpu as pltpu
from jax.sharding import PartitionSpec as P

ROUNDS = 2
F32 = jnp.float32
BF16 = jnp.bfloat16
LANES = 128
NARROW = 1
SEND = BF16
SWAP = [(0, 1), (1, 0)]
PAIRS = [(0, 1), (1, 0), (2, 3), (3, 2)]
SKIPS = [(0, 2), (2, 0), (1, 3), (3, 1)]
MIDDLE = [(1, 2), (2, 1)]
ENDS = [(0, 3), (3, 0)]
OUTWARD = [(1, 0), (2, 3)]


def column_chunks(width):
    cut = (width // (2 * LANES)) * LANES
    if width % LANES or not cut:
        return [(t, 0, width) for t in range(ROUNDS)]
    return [(0, 0, cut), (0, cut, width - cut), (1, 0, width - cut), (1, width - cut, cut)]


def after(value, *done):
    return lax.optimization_barrier((value, *done))[0]


def pack_kernel(chunk_starts, index_ref, first_ref, second_ref, *outs):
    k = pl.program_id(0)

    def put(ref):
        for start, out_ref in zip(chunk_starts, outs):
            out_ref[...] = ref[:, start : start + out_ref.shape[1]]

    pl.when(k == 0)(lambda: put(first_ref))
    pl.when(k == 1)(lambda: put(second_ref))


def pack(index, first, second, pieces):
    second, at = second
    rows, width = first.shape
    return pl.pallas_call(
        functools.partial(pack_kernel, [start for start, _ in pieces]),
        grid_spec=pltpu.PrefetchScalarGridSpec(
            num_scalar_prefetch=1,
            grid=(2,),
            in_specs=[
                pl.BlockSpec((rows, width), lambda k, index: (0, 0)),
                pl.BlockSpec((rows, width), lambda k, index: (at, 0)),
            ],
            out_specs=[pl.BlockSpec((rows, size), lambda k, index: (k ^ index[0], 0)) for _, size in pieces],
        ),
        out_shape=[jax.ShapeDtypeStruct((2 * rows, size), first.dtype) for _, size in pieces],
        compiler_params=pltpu.CompilerParams(vmem_limit_bytes=16 << 20),
        cost_estimate=pl.CostEstimate(flops=0, bytes_accessed=8 * rows * width, transcendentals=0),
    )(index, first, second)


def pair_kernel(par_ref, near_ref, far_ref, *refs):
    del par_ref
    slots, out_ref, acc_ref = refs[:-2], refs[-2], refs[-1]
    size = near_ref.shape[1]
    k = pl.program_id(0)

    def add(block_ref, which, first, final):
        block = block_ref[...]
        for h in range(len(slots) // 2):
            lines = slice(h * size, (h + 1) * size)
            value = lax.dot_general(
                block, slots[2 * h + which][...], (((0,), (0,)), ((), ())), preferred_element_type=F32
            )
            if not first:
                value += acc_ref[lines, :]
            if final:
                out_ref[lines, :] = value.astype(BF16)
            else:
                acc_ref[lines, :] = value

    pl.when(k == 0)(lambda: add(near_ref, 0, True, False))
    pl.when(k == 1)(lambda: add(near_ref, 0, False, False))
    pl.when(k == 2)(lambda: add(far_ref, 1, False, False))
    pl.when(k == 3)(lambda: add(far_ref, 1, False, True))


def pair_sum(par, near, far, slots):
    rows, size = near.shape[0] // 2, near.shape[1]
    width = slots[0].shape[1]
    lines = len(slots) // 2 * size
    first = lambda k, par: (jnp.minimum(k, 1), 0)
    second = lambda k, par: (jnp.maximum(k - 2, 0), 0)
    return pl.pallas_call(
        pair_kernel,
        grid_spec=pltpu.PrefetchScalarGridSpec(
            num_scalar_prefetch=1,
            grid=(4,),
            in_specs=[
                pl.BlockSpec((rows, size), lambda k, par: (jnp.minimum(k, 1) ^ par[0], 0)),
                pl.BlockSpec((rows, size), lambda k, par: (jnp.maximum(k - 2, 0) ^ par[0], 0)),
                *[pl.BlockSpec((rows, width), first), pl.BlockSpec((rows, width), second)] * (len(slots) // 2),
            ],
            out_specs=pl.BlockSpec((lines, width), lambda k, par: (0, 0)),
            scratch_shapes=[pltpu.VMEM((lines, width), F32)],
        ),
        out_shape=jax.ShapeDtypeStruct((lines, width), BF16),
        compiler_params=pltpu.CompilerParams(vmem_limit_bytes=24 << 20),
        cost_estimate=pl.CostEstimate(
            flops=8 * rows * lines * width,
            bytes_accessed=8 * rows * size + 4 * rows * len(slots) * width + 2 * lines * width,
            transcendentals=0,
        ),
    )(par, near, far, *slots)


def gamma_kernel(n_aux, turn, start, wide, n_add, final, order_ref, core_ref, base_ref, column_ref, *refs):
    del order_ref
    n_blocks = 2 if wide else 4
    parts, refs = refs[:n_aux], refs[n_aux:]
    blocks, refs = refs[:n_blocks], refs[n_blocks:]
    adds, outs, amp_ref = refs[:n_add], refs[n_add:-1], refs[-1]
    size, width = amp_ref.shape[1:]
    r = pl.program_id(0)
    count = pl.num_programs(0)

    @pl.when(r == 0)
    def _():
        for h in range(2):
            lines = slice(h * size, (h + 1) * size)
            total = parts[0][lines, :].astype(F32)
            for other in parts[1:]:
                total = total + other[lines, :].astype(F32)
            which = 1 - core_ref[0] if h and not wide else core_ref[0]
            row = turn + (ROUNDS if h and wide else 0)
            first = pl.multiple_of(which * width + start, LANES)
            below = base_ref[row : row + 1, :] - column_ref[pl.ds(first, size), :]
            amp_ref[h] = (total / below).astype(BF16)

    def run(which):
        if wide:
            for h in range(2):
                value = jnp.dot(blocks[which][...], amp_ref[h], preferred_element_type=F32)
                if n_add:
                    value += adds[h][...]
                outs[h][...] = value.astype(outs[h].dtype)
            return
        value = jnp.dot(blocks[which][...], amp_ref[0], preferred_element_type=F32)
        value += jnp.dot(blocks[2 + which][...], amp_ref[1], preferred_element_type=F32)
        for extra in adds:
            value += extra[...].astype(F32)
        if final:
            height = value.shape[0]
            step = width // LANES
            for c in range(step):
                outs[0][pl.ds(c, height, stride=step), :] = value[:, c * LANES : (c + 1) * LANES]
        else:
            outs[0][...] = value

    pl.when(r < count // 2)(lambda: run(0))
    pl.when(r >= count // 2)(lambda: run(1))


def gamma_step(table, turn, start, parts, blocks, adds, kinds, final=False):
    order, core, base, column = table
    wide = len(blocks) == 2
    rows, size = blocks[0].shape[0] // 2, blocks[0].shape[1]
    width = base.shape[1]
    block = rows // 2
    full = lambda array: pl.BlockSpec(array.shape, lambda r, order, core: (0, 0))
    row_block = pl.BlockSpec((block, width), lambda r, order, core: (r, 0))
    args = [base, column, *parts]
    specs = [full(array) for array in args]
    for _ in range(len(blocks) // 2):
        specs += [
            pl.BlockSpec((block, size), lambda r, order, core: (jnp.minimum(r, 3), 0)),
            pl.BlockSpec((block, size), lambda r, order, core: (jnp.maximum(r - 4, 0), 0)),
        ]
    args += [*blocks, *adds]
    specs += [row_block] * len(adds)
    if final:
        step = width // LANES
        out_shape = [jax.ShapeDtypeStruct((4 * rows * step, LANES), F32)]
        out_specs = [
            pl.BlockSpec((block * step, LANES), lambda r, order, core: (order[r // 2] * 2 + r % 2, 0))
        ]
    else:
        out_shape = [jax.ShapeDtypeStruct((4 * rows, width), kind) for kind in kinds]
        out_specs = [row_block] * len(kinds)
    return pl.pallas_call(
        functools.partial(gamma_kernel, len(parts), turn, start, wide, len(adds), final),
        grid_spec=pltpu.PrefetchScalarGridSpec(
            num_scalar_prefetch=2,
            grid=(8,),
            in_specs=specs,
            out_specs=out_specs,
            scratch_shapes=[pltpu.VMEM((2, size, width), BF16)],
        ),
        out_shape=out_shape,
        compiler_params=pltpu.CompilerParams(vmem_limit_bytes=32 << 20),
        cost_estimate=pl.CostEstimate(
            flops=16 * rows * size * width,
            bytes_accessed=16 * rows * size + 4 * len(parts) * size * width + 32 * rows * width,
            transcendentals=0,
        ),
    )(order, core, *args)


def shifted(part, axis, n):
    return [part] + [lax.ppermute(part, axis, [(k, (k + d) % n) for k in range(n)]) for d in range(1, n)]


def local_four(integrals, occ_energy, vir_energy, round_owner):
    n_aux = lax.axis_size("aux")
    me = lax.axis_index("occ").astype(jnp.int32)
    core = lax.axis_index("vir").astype(jnp.int32)
    by_orbital = lax.optimization_barrier(jnp.transpose(integrals[0], (1, 0, 2)))
    rows, width = by_orbital.shape[1:]
    is_mid = (me == 1) | (me == 2)
    odd = me % 2
    orbital = lambda k: lax.dynamic_index_in_dim(by_orbital, k, 0, keepdims=False)

    own = [orbital(round_owner[t]) for t in range(ROUNDS)]
    across = orbital(me ^ 3)
    beside = lax.ppermute(jnp.concatenate([own[0], orbital(me ^ 1)], axis=0), "occ", PAIRS)
    b3_mid = lax.ppermute(across, "occ", MIDDLE)
    b2 = lax.ppermute(orbital(me ^ 2), "occ", SKIPS)
    b3_end = lax.ppermute(across, "occ", ENDS)
    near = [(beside, 0), (lax.ppermute(own[1], "occ", PAIRS), 0)]

    energy_i = lax.dynamic_slice_in_dim(occ_energy, me, 1)
    energy_j = jnp.take(occ_energy, round_owner)
    bases = [
        energy_i + energy_j[:, None] - lax.dynamic_slice_in_dim(vir_energy, k * width, width)[None, :]
        for k in (core, 1 - core)
    ]
    order = jnp.arange(4, dtype=jnp.int32) ^ (me & 2)
    table = (order, core[None], jnp.concatenate(bases, axis=0), vir_energy[:, None])

    chunks = column_chunks(width)
    count = len(chunks)
    wide = count - NARROW
    half, mid, part, got, total = [None] * count, [None] * count, [None] * count, [None] * count, []

    for t in range(ROUNDS):
        members = [c for c in range(count) if chunks[c][0] == t]
        packed = pack(odd[None], own[t], near[t], [chunks[c][1:] for c in members])
        for c, array in zip(members, packed):
            half[c] = array

    def hop(c, *done):
        mid[c] = lax.ppermute(after(half[c], *done), "occ", MIDDLE)

    hop(0, b3_mid)
    hop(1, b2, b3_end)
    none = jnp.zeros((1,), jnp.int32)
    (mine_near,) = pack(none, orbital(me), (beside, 1), [(0, width)])
    (mine_far,) = pack(none, b2, (jnp.where(is_mid, b3_mid, b3_end), 0), [(0, width)])
    mine_far = after(mine_far, mid[0], near[1][0])
    mine_near_swap = lax.ppermute(mine_near, "vir", SWAP)
    mine_far_swap = lax.ppermute(mine_far, "vir", SWAP)
    pending = []

    def settle(acc, there, *done):
        c, turn, start, parts, blocks = pending.pop(0)
        parts = [after(parts[0], *done), *parts[1:]] if done else parts
        if c >= wide:
            last = c == count - 1
            adds = [*acc, there] if last else acc
            return gamma_step(table, turn, start, parts, blocks, adds, (F32,), final=last), there
        kinds = (F32, F32 if c < wide - 1 else SEND)
        acc = gamma_step(table, turn, start, parts, blocks, acc, kinds)
        if c == wide - 1:
            there = lax.ppermute(acc[1], "vir", SWAP)
            acc = acc[:1]
        return acc, there

    acc, there = (), None
    for c, (turn, start, size) in enumerate(chunks):
        if c + 2 < count:
            hop(c + 2, mid[c], mine_near_swap, *([mine_far_swap] if c else []))
        end = lax.ppermute(mid[c], "occ", OUTWARD)
        if c + 1 < count:
            end = after(end, mid[c + 1])
        here = mid[c]
        if c == 0:
            here = after(here, near[1][0], mine_near_swap, mine_far_swap)
        if c > 1:
            here = after(here, *total[c - 2])
        if c:
            here = after(here, part[c - 1])
        far = jnp.where(is_mid, here, end)
        blocks = [half[c], far]
        if c < wide:
            part[c] = pair_sum(odd[None], *blocks, [mine_near, mine_far, mine_near_swap, mine_far_swap])
        else:
            blocks += [lax.ppermute(half[c], "vir", SWAP), lax.ppermute(far, "vir", SWAP)]
            part[c] = jnp.concatenate(
                [pair_sum(odd[None], *blocks[2 * h : 2 * h + 2], [mine_near, mine_far]) for h in range(2)], axis=0
            )
        got[c] = shifted(part[c], "aux", n_aux)
        pending.append((c, turn, start, got[c], blocks))
        if c:
            acc, there = settle(acc, there, part[c])
            total.append(acc)
    acc, there = settle(acc, there)
    return acc[0].reshape(4, rows, 1, width)


def local_any(integrals, occ_energy, vir_energy, round_owner):
    n_aux = lax.axis_size("aux")
    me = lax.axis_index("occ")
    core = lax.axis_index("vir")
    x = integrals[0]
    rows, n_occ, width = x.shape
    mine = lax.all_to_all(x, "occ", split_axis=1, concat_axis=0, tiled=True)[:, 0]
    energy_i = lax.dynamic_slice_in_dim(occ_energy, me, 1)
    energy_a = lax.dynamic_slice_in_dim(vir_energy, core * width, width)
    gamma = jnp.zeros(mine.shape, F32)
    for turn in range(ROUNDS):
        owner = round_owner[turn]
        own = lax.dynamic_index_in_dim(x, owner, 1, keepdims=False)
        whole = lax.all_gather(own, "occ", axis=0, tiled=True)
        other = lax.ppermute(whole, "vir", SWAP)
        energy_j = lax.dynamic_slice_in_dim(occ_energy, owner, 1)
        base = (energy_i + energy_j - energy_a)[None, :]
        for which, block in ((core, whole), (1 - core, other)):
            energy_b = lax.dynamic_slice_in_dim(vir_energy, which * width, width)[:, None]
            part = jnp.einsum("pb,pa->ba", block, mine, preferred_element_type=F32).astype(BF16)
            pair = sum(p.astype(F32) for p in shifted(part, "aux", n_aux))
            amplitude = (pair / (base - energy_b)).astype(BF16)
            gamma = gamma + jnp.dot(block, amplitude, preferred_element_type=F32)
    return gamma.reshape(-1, rows, 1, width)


def solution(mesh):
    placed = (P("occ", "aux", "grp", "vir"), P("grp"), P("grp"), P("grp"))
    local = local_four if mesh.shape["occ"] == 4 else local_any
    return jax.shard_map(
        local, mesh=mesh, in_specs=placed, out_specs=P("grp", "aux", "occ", "vir"), check_vma=False
    )
```

time: 219 us -> 211 us (0.963)
  waiting for transfers between devices: 102 us -> 111 us
  other arithmetic: 11.1 us -> 4.58 us
  local copies, waits for them, and re-layouts: 16.7 us -> 11.3 us
  starting transfers between devices: 31.2 us -> 28 us
    ppermute x1, waiting for transfers between devices: 31.6 us -> 47.7 us  [local_four(): lax.ppermute(jnp.concatenate([own[0], orbital(me ^ 1)], axis=0), 'occ', P...]
    ppermute x1, waiting for transfers between devices: 16.8 us -> 2.16 us  [local_four(): b2 = lax.ppermute(orbital(me ^ 2), 'occ', SKIPS)]
    select_n x8 -> x4, other arithmetic: 7.91 us -> 2.51 us  [local_four(): far = jnp.where(is_mid, here, end)]
    slice x8 -> x0, local copies, waits for them, and re-layouts: 4.88 us -> none  [hop(): pieces = (own[turn][:, columns], near[turn][:, columns])]
    ppermute x4, waiting for transfers between devices: 28.7 us -> 31.6 us  [local_four(): end = lax.ppermute(mid[c], 'occ', OUTWARD)]
    ppermute x1, starting transfers between devices: 3.04 us -> 0.16 us  [local_four(): b2 = lax.ppermute(orbital(me ^ 2), 'occ', SKIPS)]
    unnamed x27 -> x19, local copies, waits for them, and re-layouts: 4.46 us -> 6.83 us
    ppermute x13 -> x10, waiting for transfers between devices: 4.88 us -> 7.23 us  [the longest x1 7.2 us: local_four(): near = [(beside, 0), (lax.ppermute(own[1], 'occ', PAIRS), 0)]]
  transfers between devices with their start and end apart: 25 -> 22, of which waited for: 10 -> 8; matrix products, arithmetic and copies ran while one was open for 8% -> 3% of each run, Pallas kernels for 20% -> 17%
where the time goes in v4:
time: 211 us; the launch traced here: 208 us
  waiting for transfers between devices  111 us (53%)
  Pallas kernels  49 us (23%)
  starting transfers between devices  28 us (13%)
  local copies, waits for them, and re-layouts  11.3 us (5%)
  other arithmetic  4.58 us (2%)
  between operations  4.2 us (2%)
    ppermute x1, waiting for transfers between devices, local_four(): lax.ppermute(jnp.concatenate([own[0], orbital(me ^ 1)], axis=0), 'occ', P...  47.7 us
    ppermute x4, waiting for transfers between devices, local_four(): end = lax.ppermute(mid[c], 'occ', OUTWARD)  31.6 us
    pallas_call x4, Pallas kernels, gamma_step(): pl.pallas_call(functools.partial(gamma_kernel, len(parts), turn, start, w...  26.7 us
    ppermute x4, waiting for transfers between devices, shifted(): lax.ppermute(part, axis, [(k, (k + d) % n) for k in range(n)])  22.2 us
    pallas_call x5, Pallas kernels, pair_sum(): pl.pallas_call(pair_kernel, grid_spec=pltpu.PrefetchScalarGridSpec(num_sc...  17.8 us
    ppermute x1, waiting for transfers between devices, local_four(): near = [(beside, 0), (lax.ppermute(own[1], 'occ', PAIRS), 0)]  7.2 us
    unnamed x19, local copies, waits for them, and re-layouts  6.83 us
    ppermute x4, starting transfers between devices, shifted(): lax.ppermute(part, axis, [(k, (k + d) % n) for k in range(n)])  6.25 us
  transfers between devices with their start and end apart: 22, of which 8 were waited for; matrix products, arithmetic and copies ran while one was open for 3% of the time, Pallas kernels for 17%

profile of v4, /device:TPU:0, one launch (start us, length us, event | category | flops | bytes accessed | tf_op | source)
XLA Modules:
  0.0 208.0 jit_solution(1443628218024768891)
XLA Ops:
  3.9 2.1 copy.13
  7.2 1.6 dynamic-slice_bitcast_fusion
  9.0 3.1 %collective-permute-start.1 = (bf16[1024,640]{1,0:T(8,128)(2,1)S(1)}, bf16[1024,640]{1,0:T(8,128)(2,1)S(1)}, u32[]{:S(2)}, u32[]{:S(2)}) collective-permute-start(bf16[1024,640]{1,0:T(8,128)(2,1)S(1)} %pad_maximum_fusion), channel_id=1, source_target_pairs={{0,4},{4,0},{8,12},{12,8},{1,5},{5,1},{9,13},{13,9},{2,6},{6,2},{1... | collective-permute-start | bytes 3932168 | tf_op jit(solution)/shard_map/ppermute | solution.py:229
  12.1 1.5 collective-permute-start.6
  13.6 4.4 %collective-permute-start.3 = (bf16[512,640]{1,0:T(8,128)(2,1)}, bf16[512,640]{1,0:T(8,128)(2,1)}, u32[]{:S(2)}, u32[]{:S(2)}) collective-permute-start(bf16[512,640]{1,0:T(8,128)(2,1)} %get-tuple-element.60), channel_id=1, source_target_pairs={{0,12},{12,0},{1,13},{13,1},{2,14},{14,2},{3,15},{15,3},{16,28},{2... | collective-permute-start | bytes 1966088 | tf_op jit(solution)/shard_map/ppermute | solution.py:232
  18.1 1.8 collective-permute-start
  19.9 47.7 %collective-permute-done.1.second_ref = bf16[1024,640]{1,0:T(8,128)(2,1)S(1)} collective-permute-done((bf16[1024,640]{1,0:T(8,128)(2,1)S(1)}, bf16[1024,640]{1,0:T(8,128)(2,1)S(1)}, u32[]{:S(2)}, u32[]{:S(2)}) %collective-permute-start.1) | collective-permute-done | bytes 1310752 | tf_op jit(solution)/shard_map/ppermute | solution.py:229
  72.5 2.2 %collective-permute-done.2.first_ref = bf16[512,640]{1,0:T(8,128)(2,1)} collective-permute-done((bf16[512,640]{1,0:T(8,128)(2,1)}, bf16[512,640]{1,0:T(8,128)(2,1)}, u32[]{:S(2)}, u32[]{:S(2)}) %collective-permute-start.2) | collective-permute-done | bytes 655392 | tf_op jit(solution)/shard_map/ppermute | solution.py:231
  75.9 7.2 %collective-permute-done.second_ref = bf16[512,640]{1,0:T(8,128)(2,1)} collective-permute-done((bf16[512,640]{1,0:T(8,128)(2,1)}, bf16[512,640]{1,0:T(8,128)(2,1)}, u32[]{:S(2)}, u32[]{:S(2)}) %collective-permute-start) | collective-permute-done | bytes 655392 | tf_op jit(solution)/shard_map/ppermute | solution.py:233
  83.1 1.6 collective-permute-start.4
  86.6 2.2 %shard_map.46 = (bf16[1024,384]{1,0:T(8,128)(2,1)}, bf16[1024,256]{1,0:T(8,128)(2,1)S(1)}) custom-call(s32[1]{0:T(128)} %bitcast.2.index_ref.par_ref, bf16[512,640]{1,0:T(8,128)(2,1)} %get-tuple-element.64.first_ref, bf16[512,640]{1,0:T(8,128)(2,1)} %collective-permute-done.second_ref), custom_call_target="tpu_custom_call" | custom-call | bytes 2621440 | tf_op jit(solution)/shard_map/pallas_call | solution.py:49
  90.9 1.6 collective-permute-start.12
  93.8 9.0 %collective-permute-done.10 = bf16[1024,256]{1,0:T(8,128)(2,1)} collective-permute-done((bf16[1024,256]{1,0:T(8,128)(2,1)}, bf16[1024,256]{1,0:T(8,128)(2,1)}, u32[]{:S(2)}, u32[]{:S(2)}) %collective-permute-start.10) | collective-permute-done | bytes 524320 | tf_op jit(solution)/shard_map/ppermute | solution.py:286
  104.7 4.4 %shard_map.50.refs_0_ = bf16[512,640]{1,0:T(8,128)(2,1)S(1)} custom-call(s32[1]{0:T(128)} %bitcast.2.index_ref.par_ref, bf16[1024,256]{1,0:T(8,128)(2,1)} %get-tuple-element.36.near_ref.refs_2_, bf16[1024,256]{1,0:T(8,128)(2,1)S(1)} %broadcast_select_fusion.4.far_ref.refs_3_, bf16[1024,640]{1,0:T(8,128)(2,1)S(1)} %shard_map.48.refs_0_, ...), custom_call_target="tpu_custom_call" | custom-call | flops 1342177280 | bytes 6946816 | tf_op jit(solution)/shard_map/pallas_call | solution.py:98
  109.0 1.6 collective-permute-start.13
  110.6 15.6 %collective-permute-done.11 = bf16[1024,384]{1,0:T(8,128)(2,1)} collective-permute-done((bf16[1024,384]{1,0:T(8,128)(2,1)}, bf16[1024,384]{1,0:T(8,128)(2,1)}, u32[]{:S(2)}, u32[]{:S(2)}) %collective-permute-start.11) | collective-permute-done | bytes 786464 | tf_op jit(solution)/shard_map/ppermute | solution.py:286
  128.8 5.0 %shard_map.51.refs_0_ = bf16[768,640]{1,0:T(8,128)(2,1)S(1)} custom-call(s32[1]{0:T(128)} %bitcast.2.index_ref.par_ref, bf16[1024,384]{1,0:T(8,128)(2,1)S(1)} %get-tuple-element.34.near_ref.refs_2_, bf16[1024,384]{1,0:T(8,128)(2,1)S(1)} %broadcast_select_fusion.1.far_ref.refs_3_, bf16[1024,640]{1,0:T(8,128)(2,1)S(1)} %shard_map.48.refs_0_, ...), custom_call_target="tpu_custom_call" | custom-call | flops 2013265920 | bytes 7798784 | tf_op jit(solution)/shard_map/pallas_call | solution.py:98
  133.8 1.6 collective-permute-start.15
  135.8 1.5 collective-permute-start.16
  137.2 5.4 %shard_map.52 = (f32[2048,640]{1,0:T(8,128)S(1)}, f32[2048,640]{1,0:T(8,128)S(1)}) custom-call(s32[4]{0:T(128)S(1)} %iota_xor_fusion.order_ref, s32[1]{0:T(128)} %bitcast.core_ref, f32[4,640]{1,0:T(4,128)S(1)} %pad_maximum_fusion.2.base_ref, f32[1280,1]{1,0:T(8,128)S(1)} %broadcast_in_dim.14.column_ref, bf16[512,640]{1,0:T(8,128)(2,1)S(1)} %shard_map.50.refs_0_, ...), custom_call_target="tpu_custom_call" | custom-call | flops 1342177280 | bytes 13893632 | tf_op jit(solution)/shard_map/pallas_call | solution.py:194
  142.7 2.3 %copy-done.2 = f32[2048,640]{1,0:T(8,128)} copy-done((f32[2048,640]{1,0:T(8,128)}, f32[2048,640]{1,0:T(8,128)S(1)}, u32[]{:S(2)}) %copy-start.2) | copy-done | bytes 5242904
  145.1 6.9 %collective-permute-done.14 = bf16[1024,384]{1,0:T(8,128)(2,1)S(1)} collective-permute-done((bf16[1024,384]{1,0:T(8,128)(2,1)}, bf16[1024,384]{1,0:T(8,128)(2,1)S(1)}, u32[]{:S(2)}, u32[]{:S(2)}) %collective-permute-start.14) | collective-permute-done | bytes 786464 | tf_op jit(solution)/shard_map/ppermute | solution.py:286
  152.1 5.1 %shard_map.53.refs_0_ = bf16[768,640]{1,0:T(8,128)(2,1)S(1)} custom-call(s32[1]{0:T(128)} %bitcast.2.index_ref.par_ref, bf16[1024,384]{1,0:T(8,128)(2,1)} %get-tuple-element.43.near_ref.refs_2_, bf16[1024,384]{1,0:T(8,128)(2,1)S(1)} %broadcast_select_fusion.far_ref.refs_3_, bf16[1024,640]{1,0:T(8,128)(2,1)S(1)} %shard_map.48.refs_0_, ...), custom_call_target="tpu_custom_call" | custom-call | flops 2013265920 | bytes 7798784 | tf_op jit(solution)/shard_map/pallas_call | solution.py:98
  157.2 1.6 collective-permute-start.20
  158.7 8.3 %shard_map.54 = (f32[2048,640]{1,0:T(8,128)S(1)}, f32[2048,640]{1,0:T(8,128)S(1)}) custom-call(s32[4]{0:T(128)S(1)} %iota_xor_fusion.order_ref, s32[1]{0:T(128)} %bitcast.core_ref, f32[4,640]{1,0:T(4,128)S(1)} %pad_maximum_fusion.2.base_ref, f32[1280,1]{1,0:T(8,128)S(1)} %broadcast_in_dim.14.column_ref, bf16[768,640]{1,0:T(8,128)(2,1)S(1)} %shard_map.51.refs_0_, ...), custom_call_target="tpu_custom_call" | custom-call | flops 2013265920 | bytes 15597568 | tf_op jit(solution)/shard_map/pallas_call | solution.py:194
  167.2 1.7 shard_map.55
  169.4 1.7 shard_map.56
  171.1 6.6 %collective-permute-done.20.refs_1_ = bf16[768,640]{1,0:T(8,128)(2,1)S(1)} collective-permute-done((bf16[768,640]{1,0:T(8,128)(2,1)S(1)}, bf16[768,640]{1,0:T(8,128)(2,1)S(1)}, u32[]{:S(2)}, u32[]{:S(2)}) %collective-permute-start.20) | collective-permute-done | bytes 983072 | tf_op jit(solution)/shard_map/ppermute | solution.py:214
  177.7 6.8 %shard_map.57 = (f32[2048,640]{1,0:T(8,128)S(1)}, bf16[2048,640]{1,0:T(8,128)(2,1)S(1)}) custom-call(s32[4]{0:T(128)S(1)} %iota_xor_fusion.order_ref, s32[1]{0:T(128)} %bitcast.core_ref, f32[4,640]{1,0:T(4,128)S(1)} %pad_maximum_fusion.2.base_ref, f32[1280,1]{1,0:T(8,128)S(1)} %broadcast_in_dim.14.column_ref, bf16[768,640]{1,0:T(8,128)(2,1)S(1)} %shard_map.53.refs_0_, ...), custom_call_target="tpu_custom_call" | custom-call | flops 2013265920 | bytes 15597568 | tf_op jit(solution)/shard_map/pallas_call | solution.py:194
  184.6 1.6 collective-permute-start.19
  186.2 15.6 %collective-permute-done.19.refs_1_ = bf16[512,640]{1,0:T(8,128)(2,1)S(1)} collective-permute-done((bf16[512,640]{1,0:T(8,128)(2,1)S(1)}, bf16[512,640]{1,0:T(8,128)(2,1)S(1)}, u32[]{:S(2)}, u32[]{:S(2)}) %collective-permute-start.19) | collective-permute-done | bytes 655392 | tf_op jit(solution)/shard_map/ppermute | solution.py:214
  201.8 6.2 %shard_map.58 = f32[10240,128]{1,0:T(8,128)} custom-call(s32[4]{0:T(128)S(1)} %iota_xor_fusion.order_ref, s32[1]{0:T(128)} %bitcast.core_ref, f32[4,640]{1,0:T(4,128)S(1)} %pad_maximum_fusion.2.base_ref, f32[1280,1]{1,0:T(8,128)S(1)} %broadcast_in_dim.14.column_ref, bf16[512,640]{1,0:T(8,128)(2,1)S(1)} %pad_maximum_fusion.1.refs_0_, ...), custom_call_target="tpu_custom_call" | custom-call | flops 1342177280 | bytes 13893632 | tf_op jit(solution)/shard_map/pallas_call | solution.py:194
  (63 shorter events, 18.5 us)
Async XLA Ops:
  9.0 58.6 %collective-permute-start.1 = (bf16[1024,640]{1,0:T(8,128)(2,1)S(1)}, bf16[1024,640]{1,0:T(8,128)(2,1)S(1)}, u32[]{:S(2)}, u32[]{:S(2)}) collective-permute-start(bf16[1024,640]{1,0:T(8,128)(2,1)S(1)} %pad_maximum_fusion), channel_id=1, source_target_pairs={{0,4},{4,0},{8,12},{12,8},{1,5},{5,1},{9,13},{13,9},{2,6},{6,2},{1... | collective-permute-start | bytes 3932168 | tf_op jit(solution)/shard_map/ppermute | solution.py:229
  12.1 56.4 %collective-permute-start.6 = (bf16[512,640]{1,0:T(8,128)(2,1)}, bf16[512,640]{1,0:T(8,128)(2,1)}, u32[]{:S(2)}, u32[]{:S(2)}) collective-permute-start(bf16[512,640]{1,0:T(8,128)(2,1)} %get-tuple-element.60), channel_id=1, source_target_pairs={{4,8},{8,4},{5,9},{9,5},{6,10},{10,6},{7,11},{11,7},{20,24},{24,20... | collective-permute-start | bytes 1966088 | tf_op jit(solution)/shard_map/ppermute | solution.py:230
  13.6 57.7 %collective-permute-start.3 = (bf16[512,640]{1,0:T(8,128)(2,1)}, bf16[512,640]{1,0:T(8,128)(2,1)}, u32[]{:S(2)}, u32[]{:S(2)}) collective-permute-start(bf16[512,640]{1,0:T(8,128)(2,1)} %get-tuple-element.60), channel_id=1, source_target_pairs={{0,12},{12,0},{1,13},{13,1},{2,14},{14,2},{3,15},{15,3},{16,28},{2... | collective-permute-start | bytes 1966088 | tf_op jit(solution)/shard_map/ppermute | solution.py:232
  17.9 56.7 %collective-permute-start.2 = (bf16[512,640]{1,0:T(8,128)(2,1)}, bf16[512,640]{1,0:T(8,128)(2,1)}, u32[]{:S(2)}, u32[]{:S(2)}) collective-permute-start(bf16[512,640]{1,0:T(8,128)(2,1)} %get-tuple-element.61), channel_id=1, source_target_pairs={{0,8},{8,0},{4,12},{12,4},{1,9},{9,1},{5,13},{13,5},{2,10},{10,2},... | collective-permute-start | bytes 1966088 | tf_op jit(solution)/shard_map/ppermute | solution.py:231
  18.1 65.0 %collective-permute-start = (bf16[512,640]{1,0:T(8,128)(2,1)}, bf16[512,640]{1,0:T(8,128)(2,1)}, u32[]{:S(2)}, u32[]{:S(2)}) collective-permute-start(bf16[512,640]{1,0:T(8,128)(2,1)} %get-tuple-element.64.first_ref), channel_id=1, source_target_pairs={{0,4},{4,0},{8,12},{12,8},{1,5},{5,1},{9,13},{13,9},{2,6},{6,2},{1... | collective-permute-start | bytes 1966088 | tf_op jit(solution)/shard_map/ppermute | solution.py:233
  68.5 14.6 %collective-permute-start.7 = (bf16[1024,256]{1,0:T(8,128)(2,1)}, bf16[1024,256]{1,0:T(8,128)(2,1)}, u32[]{:S(2)}, u32[]{:S(2)}) collective-permute-start(bf16[1024,256]{1,0:T(8,128)(2,1)} %get-tuple-element.36.near_ref.refs_2_), channel_id=1, source_target_pairs={{4,8},{8,4},{5,9},{9,5},{6,10},{10,6},{7,11},{11,7},{20,24},{24,20... | collective-permute-start | bytes 1572872 | tf_op jit(solution)/shard_map/ppermute | solution.py:256
  69.9 1.1 copy-start.3
  71.2 14.8 %copy-start.8 = (s32[2]{0:T(128)S(1)}, s32[2]{0:T(128)}, u32[]{:S(2)}) copy-start(s32[2]{0:T(128)} %param.7) | copy-start | bytes 28
  71.2 14.8 %copy-start.6 = (f32[4]{0:T(128)S(1)}, f32[4]{0:T(128)}, u32[]{:S(2)}) copy-start(f32[4]{0:T(128)} %param.5) | copy-start | bytes 52
  71.2 19.7 %collective-permute-start.5 = (bf16[1024,640]{1,0:T(8,128)(2,1)S(1)}, bf16[1024,640]{1,0:T(8,128)(2,1)}, u32[]{:S(2)}, u32[]{:S(2)}) collective-permute-start(bf16[1024,640]{1,0:T(8,128)(2,1)S(1)} %shard_map.48.refs_0_), channel_id=1, source_target_pairs={{0,1},{1,0},{2,3},{3,2},{4,5},{5,4},{6,7},{7,6},{8,9},{9,8},{10,11... | collective-permute-start | bytes 3932168 | tf_op jit(solution)/shard_map/ppermute | solution.py:264
  72.5 20.6 %copy-start.7 = (f32[1280]{0:T(1024)S(1)}, f32[1280]{0:T(1024)}, u32[]{:S(2)}) copy-start(f32[1280]{0:T(1024)} %param.6) | copy-start | bytes 15364
  83.1 19.8 %collective-permute-start.8 = (bf16[1024,640]{1,0:T(8,128)(2,1)S(1)}, bf16[1024,640]{1,0:T(8,128)(2,1)}, u32[]{:S(2)}, u32[]{:S(2)}) collective-permute-start(bf16[1024,640]{1,0:T(8,128)(2,1)S(1)} %shard_map.49.refs_1_), channel_id=1, source_target_pairs={{0,1},{1,0},{2,3},{3,2},{4,5},{5,4},{6,7},{7,6},{8,9},{9,8},{10,11... | collective-permute-start | bytes 3932168 | tf_op jit(solution)/shard_map/ppermute | solution.py:265
  83.1 6.5 %collective-permute-start.4 = (bf16[1024,384]{1,0:T(8,128)(2,1)S(1)}, bf16[1024,384]{1,0:T(8,128)(2,1)}, u32[]{:S(2)}, u32[]{:S(2)}) collective-permute-start(bf16[1024,384]{1,0:T(8,128)(2,1)S(1)} %get-tuple-element.34.near_ref.refs_2_), channel_id=1, source_target_pairs={{4,8},{8,4},{5,9},{9,5},{6,10},{10,6},{7,11},{11,7},{20,24},{24,20... | collective-permute-start | bytes 2359304 | tf_op jit(solution)/shard_map/ppermute | solution.py:256
  84.6 18.2 %collective-permute-start.10 = (bf16[1024,256]{1,0:T(8,128)(2,1)}, bf16[1024,256]{1,0:T(8,128)(2,1)}, u32[]{:S(2)}, u32[]{:S(2)}) collective-permute-start(bf16[1024,256]{1,0:T(8,128)(2,1)} %collective-permute-done.7), channel_id=1, source_target_pairs={{4,0},{8,12},{5,1},{9,13},{6,2},{10,14},{7,3},{11,15},{20,16},{24,... | collective-permute-start | bytes 1572872 | tf_op jit(solution)/shard_map/ppermute | solution.py:286
  88.8 0.8 copy-start.4
  89.6 36.7 %collective-permute-start.11 = (bf16[1024,384]{1,0:T(8,128)(2,1)}, bf16[1024,384]{1,0:T(8,128)(2,1)}, u32[]{:S(2)}, u32[]{:S(2)}) collective-permute-start(bf16[1024,384]{1,0:T(8,128)(2,1)} %collective-permute-done.4), channel_id=1, source_target_pairs={{4,0},{8,12},{5,1},{9,13},{6,2},{10,14},{7,3},{11,15},{20,16},{24,... | collective-permute-start | bytes 2359304 | tf_op jit(solution)/shard_map/ppermute | solution.py:286
  90.9 35.4 %collective-permute-start.12 = (bf16[1024,384]{1,0:T(8,128)(2,1)}, bf16[1024,384]{1,0:T(8,128)(2,1)}, u32[]{:S(2)}, u32[]{:S(2)}) collective-permute-start(bf16[1024,384]{1,0:T(8,128)(2,1)} %get-tuple-element.43.near_ref.refs_2_), channel_id=1, source_target_pairs={{4,8},{8,4},{5,9},{9,5},{6,10},{10,6},{7,11},{11,7},{20,24},{24,20... | collective-permute-start | bytes 2359304 | tf_op jit(solution)/shard_map/ppermute | solution.py:256
  102.8 32.9 %collective-permute-start.9 = (bf16[1024,256]{1,0:T(8,128)(2,1)}, bf16[1024,256]{1,0:T(8,128)(2,1)S(1)}, u32[]{:S(2)}, u32[]{:S(2)}) collective-permute-start(bf16[1024,256]{1,0:T(8,128)(2,1)} %copy-done.4), channel_id=1, source_target_pairs={{4,8},{8,4},{5,9},{9,5},{6,10},{10,6},{7,11},{11,7},{20,24},{24,20... | collective-permute-start | bytes 1572872 | tf_op jit(solution)/shard_map/ppermute | solution.py:256
  109.0 28.2 %collective-permute-start.13 = (bf16[512,640]{1,0:T(8,128)(2,1)S(1)}, bf16[512,640]{1,0:T(8,128)(2,1)S(1)}, u32[]{:S(2)}, u32[]{:S(2)}) collective-permute-start(bf16[512,640]{1,0:T(8,128)(2,1)S(1)} %shard_map.50.refs_0_), channel_id=1, source_target_pairs={{0,2},{2,0},{1,3},{3,1},{4,6},{6,4},{5,7},{7,5},{8,10},{10,8},{9,1... | collective-permute-start | bytes 1966088 | tf_op jit(solution)/shard_map/ppermute | solution.py:214
  126.3 25.7 %collective-permute-start.14 = (bf16[1024,384]{1,0:T(8,128)(2,1)}, bf16[1024,384]{1,0:T(8,128)(2,1)S(1)}, u32[]{:S(2)}, u32[]{:S(2)}) collective-permute-start(bf16[1024,384]{1,0:T(8,128)(2,1)} %collective-permute-done.12), channel_id=1, source_target_pairs={{4,0},{8,12},{5,1},{9,13},{6,2},{10,14},{7,3},{11,15},{20,16},{24,... | collective-permute-start | bytes 2359304 | tf_op jit(solution)/shard_map/ppermute | solution.py:286
  128.8 6.9 %copy-start.5 = (bf16[1024,256]{1,0:T(8,128)(2,1)S(1)}, bf16[1024,256]{1,0:T(8,128)(2,1)}, u32[]{:S(2)}) copy-start(bf16[1024,256]{1,0:T(8,128)(2,1)} %copy-done.4) | copy-start | bytes 1572868
  133.8 25.0 %collective-permute-start.15 = (bf16[768,640]{1,0:T(8,128)(2,1)S(1)}, bf16[768,640]{1,0:T(8,128)(2,1)S(1)}, u32[]{:S(2)}, u32[]{:S(2)}) collective-permute-start(bf16[768,640]{1,0:T(8,128)(2,1)S(1)} %shard_map.51.refs_0_), channel_id=1, source_target_pairs={{0,2},{2,0},{1,3},{3,1},{4,6},{6,4},{5,7},{7,5},{8,10},{10,8},{9,1... | collective-permute-start | bytes 2949128 | tf_op jit(solution)/shard_map/ppermute | solution.py:214
  135.7 33.7 %collective-permute-start.17 = (bf16[1024,256]{1,0:T(8,128)(2,1)S(1)}, bf16[1024,256]{1,0:T(8,128)(2,1)S(1)}, u32[]{:S(2)}, u32[]{:S(2)}) collective-permute-start(bf16[1024,256]{1,0:T(8,128)(2,1)S(1)} %copy-done.5), channel_id=1, source_target_pairs={{0,1},{1,0},{2,3},{3,2},{4,5},{5,4},{6,7},{7,6},{8,9},{9,8},{10,11... | collective-permute-start | bytes 1572872 | tf_op jit(solution)/shard_map/ppermute | solution.py:301
  135.8 31.2 %collective-permute-start.16 = (bf16[1024,256]{1,0:T(8,128)(2,1)S(1)}, bf16[1024,256]{1,0:T(8,128)(2,1)S(1)}, u32[]{:S(2)}, u32[]{:S(2)}) collective-permute-start(bf16[1024,256]{1,0:T(8,128)(2,1)S(1)} %collective-permute-done.9), channel_id=1, source_target_pairs={{4,0},{8,12},{5,1},{9,13},{6,2},{10,14},{7,3},{11,15},{20,16},{24,... | collective-permute-start | bytes 1572872 | tf_op jit(solution)/shard_map/ppermute | solution.py:286
  142.7 2.4 %copy-start.2 = (f32[2048,640]{1,0:T(8,128)}, f32[2048,640]{1,0:T(8,128)S(1)}, u32[]{:S(2)}) copy-start(f32[2048,640]{1,0:T(8,128)S(1)} %get-tuple-element.47.refs_5_) | copy-start | bytes 15728644
  157.2 20.6 %collective-permute-start.20 = (bf16[768,640]{1,0:T(8,128)(2,1)S(1)}, bf16[768,640]{1,0:T(8,128)(2,1)S(1)}, u32[]{:S(2)}, u32[]{:S(2)}) collective-permute-start(bf16[768,640]{1,0:T(8,128)(2,1)S(1)} %shard_map.53.refs_0_), channel_id=1, source_target_pairs={{0,2},{2,0},{1,3},{3,1},{4,6},{6,4},{5,7},{7,5},{8,10},{10,8},{9,1... | collective-permute-start | bytes 2949128 | tf_op jit(solution)/shard_map/ppermute | solution.py:214
  167.0 2.4 %copy-start = (f32[2048,640]{1,0:T(8,128)}, f32[2048,640]{1,0:T(8,128)S(1)}, u32[]{:S(2)}) copy-start(f32[2048,640]{1,0:T(8,128)S(1)} %get-tuple-element.53.refs_5_) | copy-start | bytes 15728644
  167.1 2.3 %collective-permute-start.18 = (bf16[1024,256]{1,0:T(8,128)(2,1)S(1)}, bf16[1024,256]{1,0:T(8,128)(2,1)S(1)}, u32[]{:S(2)}, u32[]{:S(2)}) collective-permute-start(bf16[1024,256]{1,0:T(8,128)(2,1)S(1)} %broadcast_select_fusion.3.far_ref.refs_3_), channel_id=1, source_target_pairs={{0,1},{1,0},{2,3},{3,2},{4,5},{5,4},{6,7},{7,6},{8,9},{9,8},{10,11... | collective-permute-start | bytes 1572872 | tf_op jit(solution)/shard_map/ppermute | solution.py:301
  169.4 8.4 %copy-start.1 = (f32[2048,640]{1,0:T(8,128)S(1)}, f32[2048,640]{1,0:T(8,128)}, u32[]{:S(2)}) copy-start(f32[2048,640]{1,0:T(8,128)} %copy-done) | copy-start | bytes 15728644
  184.6 17.2 %collective-permute-start.21 = (bf16[2048,640]{1,0:T(8,128)(2,1)S(1)}, bf16[2048,640]{1,0:T(8,128)(2,1)S(1)}, u32[]{:S(2)}, u32[]{:S(2)}) collective-permute-start(bf16[2048,640]{1,0:T(8,128)(2,1)S(1)} %get-tuple-element.58), channel_id=1, source_target_pairs={{0,1},{1,0},{2,3},{3,2},{4,5},{5,4},{6,7},{7,6},{8,9},{9,8},{10,11... | collective-permute-start | bytes 7864328 | tf_op jit(solution)/shard_map/ppermute | solution.py:278
  184.6 17.1 %collective-permute-start.19 = (bf16[512,640]{1,0:T(8,128)(2,1)S(1)}, bf16[512,640]{1,0:T(8,128)(2,1)S(1)}, u32[]{:S(2)}, u32[]{:S(2)}) collective-permute-start(bf16[512,640]{1,0:T(8,128)(2,1)S(1)} %pad_maximum_fusion.1.refs_0_), channel_id=1, source_target_pairs={{0,2},{2,0},{1,3},{3,1},{4,6},{6,4},{5,7},{7,5},{8,10},{10,8},{9,1... | collective-permute-start | bytes 1966088 | tf_op jit(solution)/shard_map/ppermute | solution.py:214

commit v5 on v4

--- a/solution.py
+++ b/solution.py
@@ -256,7 +256,7 @@
         mid[c] = lax.ppermute(after(half[c], *done), "occ", MIDDLE)
 
     hop(0, b3_mid)
-    hop(1, b2, b3_end)
+    hop(1, b2)
     none = jnp.zeros((1,), jnp.int32)
     (mine_near,) = pack(none, orbital(me), (beside, 1), [(0, width)])
     (mine_far,) = pack(none, b2, (jnp.where(is_mid, b3_mid, b3_end), 0), [(0, width)])

time: 211 us -> 211 us (level)
  no operation moved by 1% of the time
where the time goes in v5:
time: 211 us; the launch traced here: 208 us
  waiting for transfers between devices  111 us (53%)
  Pallas kernels  49 us (23%)
  starting transfers between devices  28.1 us (13%)
  local copies, waits for them, and re-layouts  11.3 us (5%)
  other arithmetic  4.6 us (2%)
  between operations  4.2 us (2%)
    ppermute x1, waiting for transfers between devices, local_four(): lax.ppermute(jnp.concatenate([own[0], orbital(me ^ 1)], axis=0), 'occ', P...  47.7 us
    ppermute x4, waiting for transfers between devices, local_four(): end = lax.ppermute(mid[c], 'occ', OUTWARD)  31.6 us
    pallas_call x4, Pallas kernels, gamma_step(): pl.pallas_call(functools.partial(gamma_kernel, len(parts), turn, start, w...  26.8 us
    ppermute x4, waiting for transfers between devices, shifted(): lax.ppermute(part, axis, [(k, (k + d) % n) for k in range(n)])  22.2 us
    pallas_call x5, Pallas kernels, pair_sum(): pl.pallas_call(pair_kernel, grid_spec=pltpu.PrefetchScalarGridSpec(num_sc...  17.8 us
    ppermute x1, waiting for transfers between devices, local_four(): near = [(beside, 0), (lax.ppermute(own[1], 'occ', PAIRS), 0)]  7.2 us
    unnamed x19, local copies, waits for them, and re-layouts  6.83 us
    ppermute x4, starting transfers between devices, shifted(): lax.ppermute(part, axis, [(k, (k + d) % n) for k in range(n)])  6.25 us
  transfers between devices with their start and end apart: 22, of which 8 were waited for; matrix products, arithmetic and copies ran while one was open for 3% of the time, Pallas kernels for 17%

profile of v5, /device:TPU:0, one launch (start us, length us, event | category | flops | bytes accessed | tf_op | source)
XLA Modules:
  0.0 208.0 jit_solution(10377190077063124170)
XLA Ops:
  3.9 2.1 copy.13
  7.2 1.6 dynamic-slice_bitcast_fusion
  9.0 3.1 %collective-permute-start.1 = (bf16[1024,640]{1,0:T(8,128)(2,1)S(1)}, bf16[1024,640]{1,0:T(8,128)(2,1)S(1)}, u32[]{:S(2)}, u32[]{:S(2)}) collective-permute-start(bf16[1024,640]{1,0:T(8,128)(2,1)S(1)} %pad_maximum_fusion), channel_id=1, source_target_pairs={{0,4},{4,0},{8,12},{12,8},{1,5},{5,1},{9,13},{13,9},{2,6},{6,2},{1... | collective-permute-start | bytes 3932168 | tf_op jit(solution)/shard_map/ppermute | solution.py:229
  12.1 1.5 collective-permute-start.5
  13.6 4.4 %collective-permute-start.6 = (bf16[512,640]{1,0:T(8,128)(2,1)}, bf16[512,640]{1,0:T(8,128)(2,1)}, u32[]{:S(2)}, u32[]{:S(2)}) collective-permute-start(bf16[512,640]{1,0:T(8,128)(2,1)} %get-tuple-element.59), channel_id=1, source_target_pairs={{0,12},{12,0},{1,13},{13,1},{2,14},{14,2},{3,15},{15,3},{16,28},{2... | collective-permute-start | bytes 1966088 | tf_op jit(solution)/shard_map/ppermute | solution.py:232
  18.1 1.8 collective-permute-start
  19.9 47.7 %collective-permute-done.1.second_ref = bf16[1024,640]{1,0:T(8,128)(2,1)S(1)} collective-permute-done((bf16[1024,640]{1,0:T(8,128)(2,1)S(1)}, bf16[1024,640]{1,0:T(8,128)(2,1)S(1)}, u32[]{:S(2)}, u32[]{:S(2)}) %collective-permute-start.1) | collective-permute-done | bytes 1310752 | tf_op jit(solution)/shard_map/ppermute | solution.py:229
  72.5 2.2 %collective-permute-done.2.first_ref = bf16[512,640]{1,0:T(8,128)(2,1)} collective-permute-done((bf16[512,640]{1,0:T(8,128)(2,1)}, bf16[512,640]{1,0:T(8,128)(2,1)}, u32[]{:S(2)}, u32[]{:S(2)}) %collective-permute-start.2) | collective-permute-done | bytes 655392 | tf_op jit(solution)/shard_map/ppermute | solution.py:231
  75.9 7.2 %collective-permute-done.second_ref = bf16[512,640]{1,0:T(8,128)(2,1)} collective-permute-done((bf16[512,640]{1,0:T(8,128)(2,1)}, bf16[512,640]{1,0:T(8,128)(2,1)}, u32[]{:S(2)}, u32[]{:S(2)}) %collective-permute-start) | collective-permute-done | bytes 655392 | tf_op jit(solution)/shard_map/ppermute | solution.py:233
  83.1 1.6 collective-permute-start.3
  86.6 2.2 %shard_map.46 = (bf16[1024,384]{1,0:T(8,128)(2,1)}, bf16[1024,256]{1,0:T(8,128)(2,1)S(1)}) custom-call(s32[1]{0:T(128)} %bitcast.2.index_ref.par_ref, bf16[512,640]{1,0:T(8,128)(2,1)} %get-tuple-element.64.first_ref, bf16[512,640]{1,0:T(8,128)(2,1)} %collective-permute-done.second_ref), custom_call_target="tpu_custom_call" | custom-call | bytes 2621440 | tf_op jit(solution)/shard_map/pallas_call | solution.py:49
  90.9 1.6 collective-permute-start.12
  93.8 9.0 %collective-permute-done.10 = bf16[1024,256]{1,0:T(8,128)(2,1)} collective-permute-done((bf16[1024,256]{1,0:T(8,128)(2,1)}, bf16[1024,256]{1,0:T(8,128)(2,1)}, u32[]{:S(2)}, u32[]{:S(2)}) %collective-permute-start.10) | collective-permute-done | bytes 524320 | tf_op jit(solution)/shard_map/ppermute | solution.py:286
  104.7 4.4 %shard_map.50.refs_0_ = bf16[512,640]{1,0:T(8,128)(2,1)S(1)} custom-call(s32[1]{0:T(128)} %bitcast.2.index_ref.par_ref, bf16[1024,256]{1,0:T(8,128)(2,1)} %get-tuple-element.36.near_ref.refs_2_, bf16[1024,256]{1,0:T(8,128)(2,1)S(1)} %broadcast_select_fusion.4.far_ref.refs_3_, bf16[1024,640]{1,0:T(8,128)(2,1)S(1)} %shard_map.48.refs_0_, ...), custom_call_target="tpu_custom_call" | custom-call | flops 1342177280 | bytes 6946816 | tf_op jit(solution)/shard_map/pallas_call | solution.py:98
  109.0 1.6 collective-permute-start.13
  110.6 15.6 %collective-permute-done.11 = bf16[1024,384]{1,0:T(8,128)(2,1)} collective-permute-done((bf16[1024,384]{1,0:T(8,128)(2,1)}, bf16[1024,384]{1,0:T(8,128)(2,1)}, u32[]{:S(2)}, u32[]{:S(2)}) %collective-permute-start.11) | collective-permute-done | bytes 786464 | tf_op jit(solution)/shard_map/ppermute | solution.py:286
  128.8 5.0 %shard_map.51.refs_0_ = bf16[768,640]{1,0:T(8,128)(2,1)S(1)} custom-call(s32[1]{0:T(128)} %bitcast.2.index_ref.par_ref, bf16[1024,384]{1,0:T(8,128)(2,1)S(1)} %get-tuple-element.34.near_ref.refs_2_, bf16[1024,384]{1,0:T(8,128)(2,1)S(1)} %broadcast_select_fusion.1.far_ref.refs_3_, bf16[1024,640]{1,0:T(8,128)(2,1)S(1)} %shard_map.48.refs_0_, ...), custom_call_target="tpu_custom_call" | custom-call | flops 2013265920 | bytes 7798784 | tf_op jit(solution)/shard_map/pallas_call | solution.py:98
  133.8 1.6 collective-permute-start.15
  135.8 1.5 collective-permute-start.16
  137.2 5.4 %shard_map.52 = (f32[2048,640]{1,0:T(8,128)S(1)}, f32[2048,640]{1,0:T(8,128)S(1)}) custom-call(s32[4]{0:T(128)S(1)} %iota_xor_fusion.order_ref, s32[1]{0:T(128)} %bitcast.core_ref, f32[4,640]{1,0:T(4,128)S(1)} %pad_maximum_fusion.2.base_ref, f32[1280,1]{1,0:T(8,128)S(1)} %broadcast_in_dim.14.column_ref, bf16[512,640]{1,0:T(8,128)(2,1)S(1)} %shard_map.50.refs_0_, ...), custom_call_target="tpu_custom_call" | custom-call | flops 1342177280 | bytes 13893632 | tf_op jit(solution)/shard_map/pallas_call | solution.py:194
  142.7 2.3 %copy-done.2 = f32[2048,640]{1,0:T(8,128)} copy-done((f32[2048,640]{1,0:T(8,128)}, f32[2048,640]{1,0:T(8,128)S(1)}, u32[]{:S(2)}) %copy-start.2) | copy-done | bytes 5242904
  145.1 6.9 %collective-permute-done.14 = bf16[1024,384]{1,0:T(8,128)(2,1)S(1)} collective-permute-done((bf16[1024,384]{1,0:T(8,128)(2,1)}, bf16[1024,384]{1,0:T(8,128)(2,1)S(1)}, u32[]{:S(2)}, u32[]{:S(2)}) %collective-permute-start.14) | collective-permute-done | bytes 786464 | tf_op jit(solution)/shard_map/ppermute | solution.py:286
  152.1 5.1 %shard_map.53.refs_0_ = bf16[768,640]{1,0:T(8,128)(2,1)S(1)} custom-call(s32[1]{0:T(128)} %bitcast.2.index_ref.par_ref, bf16[1024,384]{1,0:T(8,128)(2,1)} %get-tuple-element.43.near_ref.refs_2_, bf16[1024,384]{1,0:T(8,128)(2,1)S(1)} %broadcast_select_fusion.far_ref.refs_3_, bf16[1024,640]{1,0:T(8,128)(2,1)S(1)} %shard_map.48.refs_0_, ...), custom_call_target="tpu_custom_call" | custom-call | flops 2013265920 | bytes 7798784 | tf_op jit(solution)/shard_map/pallas_call | solution.py:98
  157.2 1.6 collective-permute-start.20
  158.7 8.3 %shard_map.54 = (f32[2048,640]{1,0:T(8,128)S(1)}, f32[2048,640]{1,0:T(8,128)S(1)}) custom-call(s32[4]{0:T(128)S(1)} %iota_xor_fusion.order_ref, s32[1]{0:T(128)} %bitcast.core_ref, f32[4,640]{1,0:T(4,128)S(1)} %pad_maximum_fusion.2.base_ref, f32[1280,1]{1,0:T(8,128)S(1)} %broadcast_in_dim.14.column_ref, bf16[768,640]{1,0:T(8,128)(2,1)S(1)} %shard_map.51.refs_0_, ...), custom_call_target="tpu_custom_call" | custom-call | flops 2013265920 | bytes 15597568 | tf_op jit(solution)/shard_map/pallas_call | solution.py:194
  167.2 1.7 shard_map.55
  169.4 1.7 shard_map.56
  171.1 6.6 %collective-permute-done.20.refs_1_ = bf16[768,640]{1,0:T(8,128)(2,1)S(1)} collective-permute-done((bf16[768,640]{1,0:T(8,128)(2,1)S(1)}, bf16[768,640]{1,0:T(8,128)(2,1)S(1)}, u32[]{:S(2)}, u32[]{:S(2)}) %collective-permute-start.20) | collective-permute-done | bytes 983072 | tf_op jit(solution)/shard_map/ppermute | solution.py:214
  177.7 6.8 %shard_map.57 = (f32[2048,640]{1,0:T(8,128)S(1)}, bf16[2048,640]{1,0:T(8,128)(2,1)S(1)}) custom-call(s32[4]{0:T(128)S(1)} %iota_xor_fusion.order_ref, s32[1]{0:T(128)} %bitcast.core_ref, f32[4,640]{1,0:T(4,128)S(1)} %pad_maximum_fusion.2.base_ref, f32[1280,1]{1,0:T(8,128)S(1)} %broadcast_in_dim.14.column_ref, bf16[768,640]{1,0:T(8,128)(2,1)S(1)} %shard_map.53.refs_0_, ...), custom_call_target="tpu_custom_call" | custom-call | flops 2013265920 | bytes 15597568 | tf_op jit(solution)/shard_map/pallas_call | solution.py:194
  184.6 1.6 collective-permute-start.19
  186.2 15.6 %collective-permute-done.19.refs_1_ = bf16[512,640]{1,0:T(8,128)(2,1)S(1)} collective-permute-done((bf16[512,640]{1,0:T(8,128)(2,1)S(1)}, bf16[512,640]{1,0:T(8,128)(2,1)S(1)}, u32[]{:S(2)}, u32[]{:S(2)}) %collective-permute-start.19) | collective-permute-done | bytes 655392 | tf_op jit(solution)/shard_map/ppermute | solution.py:214
  201.8 6.2 %shard_map.58 = f32[10240,128]{1,0:T(8,128)} custom-call(s32[4]{0:T(128)S(1)} %iota_xor_fusion.order_ref, s32[1]{0:T(128)} %bitcast.core_ref, f32[4,640]{1,0:T(4,128)S(1)} %pad_maximum_fusion.2.base_ref, f32[1280,1]{1,0:T(8,128)S(1)} %broadcast_in_dim.14.column_ref, bf16[512,640]{1,0:T(8,128)(2,1)S(1)} %pad_maximum_fusion.1.refs_0_, ...), custom_call_target="tpu_custom_call" | custom-call | flops 1342177280 | bytes 13893632 | tf_op jit(solution)/shard_map/pallas_call | solution.py:194
  (63 shorter events, 18.6 us)
Async XLA Ops:
  9.0 58.6 %collective-permute-start.1 = (bf16[1024,640]{1,0:T(8,128)(2,1)S(1)}, bf16[1024,640]{1,0:T(8,128)(2,1)S(1)}, u32[]{:S(2)}, u32[]{:S(2)}) collective-permute-start(bf16[1024,640]{1,0:T(8,128)(2,1)S(1)} %pad_maximum_fusion), channel_id=1, source_target_pairs={{0,4},{4,0},{8,12},{12,8},{1,5},{5,1},{9,13},{13,9},{2,6},{6,2},{1... | collective-permute-start | bytes 3932168 | tf_op jit(solution)/shard_map/ppermute | solution.py:229
  12.1 56.4 %collective-permute-start.5 = (bf16[512,640]{1,0:T(8,128)(2,1)}, bf16[512,640]{1,0:T(8,128)(2,1)}, u32[]{:S(2)}, u32[]{:S(2)}) collective-permute-start(bf16[512,640]{1,0:T(8,128)(2,1)} %get-tuple-element.59), channel_id=1, source_target_pairs={{4,8},{8,4},{5,9},{9,5},{6,10},{10,6},{7,11},{11,7},{20,24},{24,20... | collective-permute-start | bytes 1966088 | tf_op jit(solution)/shard_map/ppermute | solution.py:230
  13.6 57.7 %collective-permute-start.6 = (bf16[512,640]{1,0:T(8,128)(2,1)}, bf16[512,640]{1,0:T(8,128)(2,1)}, u32[]{:S(2)}, u32[]{:S(2)}) collective-permute-start(bf16[512,640]{1,0:T(8,128)(2,1)} %get-tuple-element.59), channel_id=1, source_target_pairs={{0,12},{12,0},{1,13},{13,1},{2,14},{14,2},{3,15},{15,3},{16,28},{2... | collective-permute-start | bytes 1966088 | tf_op jit(solution)/shard_map/ppermute | solution.py:232
  17.9 56.7 %collective-permute-start.2 = (bf16[512,640]{1,0:T(8,128)(2,1)}, bf16[512,640]{1,0:T(8,128)(2,1)}, u32[]{:S(2)}, u32[]{:S(2)}) collective-permute-start(bf16[512,640]{1,0:T(8,128)(2,1)} %get-tuple-element.61), channel_id=1, source_target_pairs={{0,8},{8,0},{4,12},{12,4},{1,9},{9,1},{5,13},{13,5},{2,10},{10,2},... | collective-permute-start | bytes 1966088 | tf_op jit(solution)/shard_map/ppermute | solution.py:231
  18.1 65.0 %collective-permute-start = (bf16[512,640]{1,0:T(8,128)(2,1)}, bf16[512,640]{1,0:T(8,128)(2,1)}, u32[]{:S(2)}, u32[]{:S(2)}) collective-permute-start(bf16[512,640]{1,0:T(8,128)(2,1)} %get-tuple-element.64.first_ref), channel_id=1, source_target_pairs={{0,4},{4,0},{8,12},{12,8},{1,5},{5,1},{9,13},{13,9},{2,6},{6,2},{1... | collective-permute-start | bytes 1966088 | tf_op jit(solution)/shard_map/ppermute | solution.py:233
  68.5 14.6 %collective-permute-start.7 = (bf16[1024,256]{1,0:T(8,128)(2,1)}, bf16[1024,256]{1,0:T(8,128)(2,1)}, u32[]{:S(2)}, u32[]{:S(2)}) collective-permute-start(bf16[1024,256]{1,0:T(8,128)(2,1)} %get-tuple-element.36.near_ref.refs_2_), channel_id=1, source_target_pairs={{4,8},{8,4},{5,9},{9,5},{6,10},{10,6},{7,11},{11,7},{20,24},{24,20... | collective-permute-start | bytes 1572872 | tf_op jit(solution)/shard_map/ppermute | solution.py:256
  69.9 1.1 copy-start.3
  71.2 14.8 %copy-start.8 = (s32[2]{0:T(128)S(1)}, s32[2]{0:T(128)}, u32[]{:S(2)}) copy-start(s32[2]{0:T(128)} %param.7) | copy-start | bytes 28
  71.2 14.8 %copy-start.6 = (f32[4]{0:T(128)S(1)}, f32[4]{0:T(128)}, u32[]{:S(2)}) copy-start(f32[4]{0:T(128)} %param.5) | copy-start | bytes 52
  71.2 19.7 %collective-permute-start.4 = (bf16[1024,640]{1,0:T(8,128)(2,1)S(1)}, bf16[1024,640]{1,0:T(8,128)(2,1)}, u32[]{:S(2)}, u32[]{:S(2)}) collective-permute-start(bf16[1024,640]{1,0:T(8,128)(2,1)S(1)} %shard_map.48.refs_0_), channel_id=1, source_target_pairs={{0,1},{1,0},{2,3},{3,2},{4,5},{5,4},{6,7},{7,6},{8,9},{9,8},{10,11... | collective-permute-start | bytes 3932168 | tf_op jit(solution)/shard_map/ppermute | solution.py:264
  72.5 20.7 %copy-start.7 = (f32[1280]{0:T(1024)S(1)}, f32[1280]{0:T(1024)}, u32[]{:S(2)}) copy-start(f32[1280]{0:T(1024)} %param.6) | copy-start | bytes 15364
  83.1 19.8 %collective-permute-start.8 = (bf16[1024,640]{1,0:T(8,128)(2,1)S(1)}, bf16[1024,640]{1,0:T(8,128)(2,1)}, u32[]{:S(2)}, u32[]{:S(2)}) collective-permute-start(bf16[1024,640]{1,0:T(8,128)(2,1)S(1)} %shard_map.49.refs_1_), channel_id=1, source_target_pairs={{0,1},{1,0},{2,3},{3,2},{4,5},{5,4},{6,7},{7,6},{8,9},{9,8},{10,11... | collective-permute-start | bytes 3932168 | tf_op jit(solution)/shard_map/ppermute | solution.py:265
  83.1 6.5 %collective-permute-start.3 = (bf16[1024,384]{1,0:T(8,128)(2,1)S(1)}, bf16[1024,384]{1,0:T(8,128)(2,1)}, u32[]{:S(2)}, u32[]{:S(2)}) collective-permute-start(bf16[1024,384]{1,0:T(8,128)(2,1)S(1)} %get-tuple-element.34.near_ref.refs_2_), channel_id=1, source_target_pairs={{4,8},{8,4},{5,9},{9,5},{6,10},{10,6},{7,11},{11,7},{20,24},{24,20... | collective-permute-start | bytes 2359304 | tf_op jit(solution)/shard_map/ppermute | solution.py:256
  84.6 18.2 %collective-permute-start.10 = (bf16[1024,256]{1,0:T(8,128)(2,1)}, bf16[1024,256]{1,0:T(8,128)(2,1)}, u32[]{:S(2)}, u32[]{:S(2)}) collective-permute-start(bf16[1024,256]{1,0:T(8,128)(2,1)} %collective-permute-done.7), channel_id=1, source_target_pairs={{4,0},{8,12},{5,1},{9,13},{6,2},{10,14},{7,3},{11,15},{20,16},{24,... | collective-permute-start | bytes 1572872 | tf_op jit(solution)/shard_map/ppermute | solution.py:286
  88.8 0.8 copy-start.4
  89.6 36.7 %collective-permute-start.11 = (bf16[1024,384]{1,0:T(8,128)(2,1)}, bf16[1024,384]{1,0:T(8,128)(2,1)}, u32[]{:S(2)}, u32[]{:S(2)}) collective-permute-start(bf16[1024,384]{1,0:T(8,128)(2,1)} %collective-permute-done.3), channel_id=1, source_target_pairs={{4,0},{8,12},{5,1},{9,13},{6,2},{10,14},{7,3},{11,15},{20,16},{24,... | collective-permute-start | bytes 2359304 | tf_op jit(solution)/shard_map/ppermute | solution.py:286
  90.9 35.4 %collective-permute-start.12 = (bf16[1024,384]{1,0:T(8,128)(2,1)}, bf16[1024,384]{1,0:T(8,128)(2,1)}, u32[]{:S(2)}, u32[]{:S(2)}) collective-permute-start(bf16[1024,384]{1,0:T(8,128)(2,1)} %get-tuple-element.43.near_ref.refs_2_), channel_id=1, source_target_pairs={{4,8},{8,4},{5,9},{9,5},{6,10},{10,6},{7,11},{11,7},{20,24},{24,20... | collective-permute-start | bytes 2359304 | tf_op jit(solution)/shard_map/ppermute | solution.py:256
  102.8 32.9 %collective-permute-start.9 = (bf16[1024,256]{1,0:T(8,128)(2,1)}, bf16[1024,256]{1,0:T(8,128)(2,1)S(1)}, u32[]{:S(2)}, u32[]{:S(2)}) collective-permute-start(bf16[1024,256]{1,0:T(8,128)(2,1)} %copy-done.4), channel_id=1, source_target_pairs={{4,8},{8,4},{5,9},{9,5},{6,10},{10,6},{7,11},{11,7},{20,24},{24,20... | collective-permute-start | bytes 1572872 | tf_op jit(solution)/shard_map/ppermute | solution.py:256
  109.0 28.2 %collective-permute-start.13 = (bf16[512,640]{1,0:T(8,128)(2,1)S(1)}, bf16[512,640]{1,0:T(8,128)(2,1)S(1)}, u32[]{:S(2)}, u32[]{:S(2)}) collective-permute-start(bf16[512,640]{1,0:T(8,128)(2,1)S(1)} %shard_map.50.refs_0_), channel_id=1, source_target_pairs={{0,2},{2,0},{1,3},{3,1},{4,6},{6,4},{5,7},{7,5},{8,10},{10,8},{9,1... | collective-permute-start | bytes 1966088 | tf_op jit(solution)/shard_map/ppermute | solution.py:214
  126.3 25.7 %collective-permute-start.14 = (bf16[1024,384]{1,0:T(8,128)(2,1)}, bf16[1024,384]{1,0:T(8,128)(2,1)S(1)}, u32[]{:S(2)}, u32[]{:S(2)}) collective-permute-start(bf16[1024,384]{1,0:T(8,128)(2,1)} %collective-permute-done.12), channel_id=1, source_target_pairs={{4,0},{8,12},{5,1},{9,13},{6,2},{10,14},{7,3},{11,15},{20,16},{24,... | collective-permute-start | bytes 2359304 | tf_op jit(solution)/shard_map/ppermute | solution.py:286
  128.8 6.9 %copy-start.5 = (bf16[1024,256]{1,0:T(8,128)(2,1)S(1)}, bf16[1024,256]{1,0:T(8,128)(2,1)}, u32[]{:S(2)}) copy-start(bf16[1024,256]{1,0:T(8,128)(2,1)} %copy-done.4) | copy-start | bytes 1572868
  133.8 24.9 %collective-permute-start.15 = (bf16[768,640]{1,0:T(8,128)(2,1)S(1)}, bf16[768,640]{1,0:T(8,128)(2,1)S(1)}, u32[]{:S(2)}, u32[]{:S(2)}) collective-permute-start(bf16[768,640]{1,0:T(8,128)(2,1)S(1)} %shard_map.51.refs_0_), channel_id=1, source_target_pairs={{0,2},{2,0},{1,3},{3,1},{4,6},{6,4},{5,7},{7,5},{8,10},{10,8},{9,1... | collective-permute-start | bytes 2949128 | tf_op jit(solution)/shard_map/ppermute | solution.py:214
  135.7 33.7 %collective-permute-start.17 = (bf16[1024,256]{1,0:T(8,128)(2,1)S(1)}, bf16[1024,256]{1,0:T(8,128)(2,1)S(1)}, u32[]{:S(2)}, u32[]{:S(2)}) collective-permute-start(bf16[1024,256]{1,0:T(8,128)(2,1)S(1)} %copy-done.5), channel_id=1, source_target_pairs={{0,1},{1,0},{2,3},{3,2},{4,5},{5,4},{6,7},{7,6},{8,9},{9,8},{10,11... | collective-permute-start | bytes 1572872 | tf_op jit(solution)/shard_map/ppermute | solution.py:301
  135.8 31.2 %collective-permute-start.16 = (bf16[1024,256]{1,0:T(8,128)(2,1)S(1)}, bf16[1024,256]{1,0:T(8,128)(2,1)S(1)}, u32[]{:S(2)}, u32[]{:S(2)}) collective-permute-start(bf16[1024,256]{1,0:T(8,128)(2,1)S(1)} %collective-permute-done.9), channel_id=1, source_target_pairs={{4,0},{8,12},{5,1},{9,13},{6,2},{10,14},{7,3},{11,15},{20,16},{24,... | collective-permute-start | bytes 1572872 | tf_op jit(solution)/shard_map/ppermute | solution.py:286
  142.7 2.4 %copy-start.2 = (f32[2048,640]{1,0:T(8,128)}, f32[2048,640]{1,0:T(8,128)S(1)}, u32[]{:S(2)}) copy-start(f32[2048,640]{1,0:T(8,128)S(1)} %get-tuple-element.47.refs_5_) | copy-start | bytes 15728644
  157.2 20.6 %collective-permute-start.20 = (bf16[768,640]{1,0:T(8,128)(2,1)S(1)}, bf16[768,640]{1,0:T(8,128)(2,1)S(1)}, u32[]{:S(2)}, u32[]{:S(2)}) collective-permute-start(bf16[768,640]{1,0:T(8,128)(2,1)S(1)} %shard_map.53.refs_0_), channel_id=1, source_target_pairs={{0,2},{2,0},{1,3},{3,1},{4,6},{6,4},{5,7},{7,5},{8,10},{10,8},{9,1... | collective-permute-start | bytes 2949128 | tf_op jit(solution)/shard_map/ppermute | solution.py:214
  167.0 2.4 %copy-start = (f32[2048,640]{1,0:T(8,128)}, f32[2048,640]{1,0:T(8,128)S(1)}, u32[]{:S(2)}) copy-start(f32[2048,640]{1,0:T(8,128)S(1)} %get-tuple-element.53.refs_5_) | copy-start | bytes 15728644
  167.1 2.3 %collective-permute-start.18 = (bf16[1024,256]{1,0:T(8,128)(2,1)S(1)}, bf16[1024,256]{1,0:T(8,128)(2,1)S(1)}, u32[]{:S(2)}, u32[]{:S(2)}) collective-permute-start(bf16[1024,256]{1,0:T(8,128)(2,1)S(1)} %broadcast_select_fusion.3.far_ref.refs_3_), channel_id=1, source_target_pairs={{0,1},{1,0},{2,3},{3,2},{4,5},{5,4},{6,7},{7,6},{8,9},{9,8},{10,11... | collective-permute-start | bytes 1572872 | tf_op jit(solution)/shard_map/ppermute | solution.py:301
  169.4 8.4 %copy-start.1 = (f32[2048,640]{1,0:T(8,128)S(1)}, f32[2048,640]{1,0:T(8,128)}, u32[]{:S(2)}) copy-start(f32[2048,640]{1,0:T(8,128)} %copy-done) | copy-start | bytes 15728644
  184.6 17.2 %collective-permute-start.21 = (bf16[2048,640]{1,0:T(8,128)(2,1)S(1)}, bf16[2048,640]{1,0:T(8,128)(2,1)S(1)}, u32[]{:S(2)}, u32[]{:S(2)}) collective-permute-start(bf16[2048,640]{1,0:T(8,128)(2,1)S(1)} %get-tuple-element.58), channel_id=1, source_target_pairs={{0,1},{1,0},{2,3},{3,2},{4,5},{5,4},{6,7},{7,6},{8,9},{9,8},{10,11... | collective-permute-start | bytes 7864328 | tf_op jit(solution)/shard_map/ppermute | solution.py:278
  184.6 17.1 %collective-permute-start.19 = (bf16[512,640]{1,0:T(8,128)(2,1)S(1)}, bf16[512,640]{1,0:T(8,128)(2,1)S(1)}, u32[]{:S(2)}, u32[]{:S(2)}) collective-permute-start(bf16[512,640]{1,0:T(8,128)(2,1)S(1)} %pad_maximum_fusion.1.refs_0_), channel_id=1, source_target_pairs={{0,2},{2,0},{1,3},{3,1},{4,6},{6,4},{5,7},{7,5},{8,10},{10,8},{9,1... | collective-permute-start | bytes 1966088 | tf_op jit(solution)/shard_map/ppermute | solution.py:214
